TPU v7x, 128 devices: a whole 4x4x4 slice. The times are simulated.
128 devices in a mesh: row: 16 (over z_hi, y, core), col: 8 (over z_lo, x).
Axes of the slice: x: 4, y: 4, z: 4 (z_hi: 2, z_lo: 2; z = z_hi * 2 + z_lo), core: 2. Of those that a mesh axis runs over, the one named last changes fastest.
Arguments:
- at: bfloat16 [32768, 16384], P('row', 'col'), may hold values from -0.09375 to 0.09375
- bmat: bfloat16 [32768, 16384], P('col', 'row'), may hold values from -6 to 6
- mask_a: int32 [512, 256], P('row', 'col'), may hold values 0 or 1
- mask_b: int32 [512, 256], P('col', 'row'), may hold values 0 or 1
- filt: int32 [256, 256], P('col', 'row'), may hold values 0 or 1
- kdist: int32 [512], replicated, may hold values from 0 to 511, as said below
Outputs:
- product_blocks: float32 [16384, 16384], P('col', 'row')
Inputs may be any that keep to these rules, and one draw needn't show every extreme that they name: kdist is a permutation; entry k lies in run s = k // 32 and equals p * 32 + s * 2 + j for some panel p and j below 2, each run giving every panel exactly 2 blocks.
All inputs are finite; a program needn't handle non-finite values. No bound on the sum of `mask_a` or of `mask_b` or of `filt` on one device may be relied on, other than what follows from the above.
Results may differ from a plain program's by a relative error of at most 0.0003.
Values may be sent and summed in bfloat16 or wider, within the bound.
No kernel may reach another device: no remote copies, remote signals or barrier semaphores. Data moves between devices by JAX's collectives and lax.ppermute only.
A program may use at most 192 MiB of HBM per device.

v0:
```python
import jax
import jax.numpy as jnp
from jax import lax
from jax.sharding import PartitionSpec as P

BS = 64
KB = 32


def from_behind(value, axis, steps):
    count = lax.axis_size(axis)
    pairs = [(source, (source + steps) % count) for source in range(count)]
    return lax.ppermute(value, axis, pairs)


def expand(mask):
    widened = jnp.repeat(mask.astype(jnp.bfloat16), BS, axis=0)
    return jnp.repeat(widened, BS, axis=1)


def product(left, right):
    return lax.dot_general(
        left, right, (((0,), (0,)), ((), ())), preferred_element_type=jnp.float32
    )


def inverse_of(send_order, count):
    return jnp.zeros((count,), jnp.int32).at[send_order].set(jnp.arange(count, dtype=jnp.int32))


def on_device(at, bmat, mask_a, mask_b, filt, kdist):
    panels = lax.axis_size("row")
    halves = lax.axis_size("col")
    per_peer = KB // panels
    row_id = lax.axis_index("row")
    col_id = lax.axis_index("col")
    a_masked = at * expand(mask_a)
    b_masked = bmat * expand(mask_b)
    a_width = a_masked.shape[1] // 2
    a_blocks = a_masked.reshape(KB, BS, 2, a_width)
    a_pos = lax.dynamic_slice_in_dim(kdist, row_id * KB, KB)
    a_panel = a_pos // KB
    a_slot = a_pos % KB - row_id * per_peer
    pieces = []
    for a_tile_id in range(2):
        dest_row = (a_panel - 2 * col_id - a_tile_id) % panels
        order_idx = inverse_of(dest_row * per_peer + a_slot, KB)
        pieces.append(a_blocks[:, :, a_tile_id, :][order_idx])
    received = lax.all_to_all(
        jnp.stack(pieces).reshape(2, panels, per_peer * BS, a_width),
        "row",
        split_axis=1,
        concat_axis=1,
        tiled=True,
    )
    a_now = received.reshape(2, KB * BS, a_width)
    a_later = from_behind(a_now, "row", -1)
    b_width = b_masked.shape[1]
    b_blocks = b_masked.reshape(2 * KB, BS, b_width)
    b_pos = lax.dynamic_slice_in_dim(kdist, col_id * 2 * KB, 2 * KB)
    b_group = (b_pos // KB - row_id) % panels
    b_slot = b_pos % KB - 2 * col_id * per_peer
    b_order = b_group % 2 * KB + b_group // 2 * (2 * per_peer) + b_slot
    b_send = b_blocks[inverse_of(b_order, 2 * KB)].reshape(2, halves, 2 * per_peer * BS, b_width)
    b_now = lax.all_to_all(b_send, "col", split_axis=1, concat_axis=1, tiled=True).reshape(
        2, KB * BS, b_width
    )
    b_upper = from_behind(b_now[0], "col", -1)
    b_later = (b_now[1], b_upper)
    summed = []
    for tile_id in range(2):
        first_stop = product(a_now[tile_id], b_now[tile_id])
        summed.append(first_stop + product(a_later[tile_id], b_later[tile_id]))
    gathered = jnp.concatenate(summed, axis=0)
    return gathered * expand(filt).astype(jnp.float32)


def solution(mesh):
    in_specs = (
        P("row", "col"),
        P("col", "row"),
        P("row", "col"),
        P("col", "row"),
        P("col", "row"),
        P(),
    )
    out_specs = P("col", "row")
    return jax.shard_map(
        on_device, mesh=mesh, in_specs=in_specs, out_specs=out_specs, check_vma=False
    )
```

profile of v0, /device:TPU:30, one launch (start us, length us, event | category | flops | bytes accessed | tf_op | source)
XLA Modules:
  0.0 515.2 jit_solution(8202804458347490161)
XLA Ops:
  0.0 0.8 compare_select_fusion.5
  0.8 0.7 scatter_custom_fusion.1
  1.5 0.0 copy-start.1
  1.5 12.2 %copy.31 = bf16[2048,2048]{0,1:T(8,128)(2,1)} copy(bf16[2048,2048]{1,0:T(8,128)(2,1)} %param.6) | data formatting | bytes 16777216 | tf_op args[0]
  13.8 0.0 copy-done.1
  13.8 0.1 copy.30
  13.9 0.2 broadcast_in_dim.36
  14.1 0.3 reshape.42
  14.3 7.4 %bitcast_multiply_fusion.1 = bf16[2048,2048]{0,1:T(8,128)(2,1)} fusion(bf16[2048,2048]{0,1:T(8,128)(2,1)} %copy.31, bf16[2048,32]{0,1:T(8,128)(2,1)S(1)} %reshape.42), kind=kLoop, calls=%fused_computation.9 | loop fusion | flops 4194304 | bytes 16908288 | tf_op jit(solution)/shard_map/mul | solution.py:37
  21.7 12.3 %copy.32 = bf16[2048,2048]{1,0:T(8,128)(2,1)} copy(bf16[2048,2048]{0,1:T(8,128)(2,1)} %bitcast_multiply_fusion.1) | data formatting | bytes 16777216 | tf_op jit(solution)/shard_map/mul | solution.py:37
  34.0 14.4 %reshape.44 = bf16[32,64,2,1024]{3,2,1,0:T(2,128)(2,1)} reshape(bf16[2048,2048]{1,0:T(8,128)(2,1)} %copy.32) | data formatting | bytes 16777216 | tf_op jit(solution)/shard_map/reshape | solution.py:40
  48.4 17.5 %fusion.27 = (bf16[32,64,1,1024]{3,2,1,0:T(2,128)(2,1)}, bf16[32,64,1,1024]{3,2,1,0:T(2,128)(2,1)}) fusion(bf16[32,64,2,1024]{3,2,1,0:T(2,128)(2,1)} %reshape.44), kind=kLoop, calls=%fused_computation.73 | loop fusion | bytes 16777216 | tf_op jit(solution)/shard_map/slice | solution.py:48
  66.0 0.7 scatter_custom_fusion
  66.7 12.6 %copy_bitcast_fusion = (bf16[32,64,1024]{2,1,0:T(8,128)(2,1)}, bf16[32,64,1024]{2,1,0:T(8,128)(2,1)}) fusion(bf16[32,64,1,1024]{3,2,1,0:T(2,128)(2,1)} %get-tuple-element.13, bf16[32,64,1,1024]{3,2,1,0:T(2,128)(2,1)} %get-tuple-element.12), kind=kLoop, calls=%fused_computation.14 | loop fusion | bytes 16777216
  79.3 4.9 gather_fusion.1
  84.3 5.0 gather_fusion
  89.3 7.6 %pad_maximum_fusion = bf16[2,16,128,1024]{3,2,0,1:T(8,128)(2,1)} fusion(bf16[1,16,128,1024]{3,2,0,1:T(8,128)(2,1)} %bitcast.49, bf16[1,16,128,1024]{3,2,0,1:T(8,128)(2,1)} %bitcast.50), kind=kLoop, calls=%fused_computation.6 | loop fusion | flops 4194304 | bytes 16777216 | tf_op jit(solution)/shard_map/stack | solution.py:50
  96.9 8.0 %all-to-all-start = ((bf16[2,16,128,1024]{3,2,0,1:T(8,128)(2,1)}), bf16[2,16,128,1024]{3,2,0,1:T(8,128)(2,1)}, u32[]{:S(2)}, u32[]{:S(2)}) async-start(bf16[2,16,128,1024]{3,2,0,1:T(8,128)(2,1)} %pad_maximum_fusion), calls=%async_computation | async-start | bytes 16777216 | tf_op jit(solution)/shard_map/all_to_all | solution.py:49
  104.9 11.8 %copy.35 = bf16[4096,1024]{0,1:T(8,128)(2,1)} copy(bf16[4096,1024]{1,0:T(8,128)(2,1)} %param.7) | data formatting | bytes 16777216 | tf_op args[1]
  116.7 0.2 broadcast_in_dim.42
  116.9 0.3 reshape.45
  117.2 7.2 %bitcast_multiply_fusion = bf16[4096,1024]{0,1:T(8,128)(2,1)} fusion(bf16[4096,1024]{0,1:T(8,128)(2,1)} %copy.35, bf16[4096,16]{0,1:T(8,128)(2,1)S(1)} %reshape.45), kind=kLoop, calls=%fused_computation.8 | loop fusion | flops 4194304 | bytes 16908288 | tf_op jit(solution)/shard_map/mul | solution.py:38
  124.4 11.9 %copy.36 = bf16[4096,1024]{1,0:T(8,128)(2,1)} copy(bf16[4096,1024]{0,1:T(8,128)(2,1)} %bitcast_multiply_fusion) | data formatting | bytes 16777216 | tf_op jit(solution)/shard_map/mul | solution.py:38
  136.3 0.8 compare_select_fusion.1
  137.1 1.0 scatter_custom_fusion.2
  138.1 8.9 %gather_fusion.2 = bf16[64,64,1024]{2,1,0:T(8,128)(2,1)} fusion(bf16[64,64,1024]{2,1,0:T(8,128)(2,1)} %bitcast.46, s32[1024]{0:T(1024)S(1)} %pad_clamp_fusion), kind=kCustom, calls=%fused_computation.2 | custom fusion | bytes 16777472 | tf_op jit(solution)/shard_map/gather | solution.py:64
  147.0 7.9 %copy.37 = bf16[2,8,256,1024]{3,2,0,1:T(8,128)(2,1)} copy(bf16[2,8,256,1024]{3,2,1,0:T(8,128)(2,1)} %bitcast.47) | data formatting | bytes 16777216 | tf_op jit(solution)/shard_map/reshape | solution.py:64
  155.0 59.9 %all-to-all-done = bf16[2,16,128,1024]{3,2,0,1:T(8,128)(2,1)} async-done(((bf16[2,16,128,1024]{3,2,0,1:T(8,128)(2,1)}), bf16[2,16,128,1024]{3,2,0,1:T(8,128)(2,1)}, u32[]{:S(2)}, u32[]{:S(2)}) %all-to-all-start) | async-done | bytes 8388640 | tf_op jit(solution)/shard_map/all_to_all | solution.py:49
  214.9 5.4 %all-to-all-start.1 = ((bf16[2,8,256,1024]{3,2,0,1:T(8,128)(2,1)}), bf16[2,8,256,1024]{3,2,0,1:T(8,128)(2,1)}, u32[]{:S(2)}, u32[]{:S(2)}) async-start(bf16[2,8,256,1024]{3,2,0,1:T(8,128)(2,1)} %copy.37), calls=%async_computation.1 | async-start | bytes 16777216 | tf_op jit(solution)/shard_map/all_to_all | solution.py:65
  220.3 8.2 %copy.38 = bf16[2,16,128,1024]{3,2,1,0:T(8,128)(2,1)} copy(bf16[2,16,128,1024]{3,2,0,1:T(8,128)(2,1)} %all-to-all-done) | data formatting | bytes 16777216 | tf_op jit(solution)/shard_map/all_to_all | solution.py:49
  228.5 1.6 collective-permute-start
  230.1 171.9 %all-to-all-done.1 = bf16[2,8,256,1024]{3,2,0,1:T(8,128)(2,1)} async-done(((bf16[2,8,256,1024]{3,2,0,1:T(8,128)(2,1)}), bf16[2,8,256,1024]{3,2,0,1:T(8,128)(2,1)}, u32[]{:S(2)}, u32[]{:S(2)}) %all-to-all-start.1) | async-done | bytes 8388640 | tf_op jit(solution)/shard_map/all_to_all | solution.py:65
  402.0 6.0 %fusion.26 = (bf16[1,8,256,1024]{3,2,0,1:T(8,128)(2,1)}, bf16[1,8,256,1024]{3,2,0,1:T(8,128)(2,1)}) fusion(bf16[2,8,256,1024]{3,2,0,1:T(8,128)(2,1)} %all-to-all-done.1), kind=kLoop, calls=%fused_computation.72 | loop fusion | bytes 16777216 | tf_op jit(solution)/shard_map/slice | solution.py:72
  408.0 0.9 collective-permute-start.1
  408.9 0.1 broadcast_in_dim.46
  409.0 0.1 convert_element_type.24
  409.1 4.5 broadcast_in_dim.47
  413.6 9.2 %copy.39 = f32[2048,1024]{1,0:T(8,128)} copy(f32[2048,1024]{0,1:T(8,128)} %bitcast.48) | data formatting | bytes 16777216 | tf_op jit(solution)/shard_map/convert_element_type | solution.py:75
  422.8 4.0 fusion.25
  426.8 6.5 %fusion.28 = f32[1024,1024]{1,0:T(8,128)S(1)} fusion(bf16[2048,1024]{1,0:T(8,128)(2,1)S(1)} %bitcast.55, bf16[2048,1024]{1,0:T(8,128)(2,1)} %bitcast.9), kind=kOutput, calls=%fused_computation.74 | convolution fusion | flops 4294967296 | bytes 12582912 | tf_op jit(solution)/shard_map/dot_general | solution.py:22
  433.3 4.8 fusion.29
  438.1 0.0 collective-permute-done
  438.1 0.0 slice-start
  438.1 6.5 %fusion.2 = f32[1024,1024]{1,0:T(8,128)S(1)} fusion(f32[1024,1024]{1,0:T(8,128)S(1)} %fusion.28, bf16[2048,1024]{1,0:T(8,128)(2,1)S(1)} %bitcast.52, bf16[2,2048,1024]{2,1,0:T(8,128)(2,1)} %collective-permute-done), kind=kOutput, calls=%fused_computation.16 | convolution fusion | flops 4296015872 | bytes 16777216 | tf_op jit(solution)/shard_map/dot_general | solution.py:22
  444.6 0.0 slice-start.1
  444.7 58.3 %collective-permute-done.1 = bf16[2048,1024]{1,0:T(8,128)(2,1)} collective-permute-done((bf16[2048,1024]{1,0:T(8,128)(2,1)}, bf16[2048,1024]{1,0:T(8,128)(2,1)}, u32[]{:S(2)}, u32[]{:S(2)}) %collective-permute-start.1) | collective-permute-done | bytes 4194336 | tf_op jit(solution)/shard_map/ppermute | solution.py:13
  502.9 7.5 %fusion.3 = f32[1024,1024]{1,0:T(8,128)S(1)} fusion(f32[1024,1024]{1,0:T(8,128)S(1)} %fusion.29, bf16[2048,1024]{1,0:T(8,128)(2,1)} %collective-permute-done.1, bf16[2,2048,1024]{2,1,0:T(8,128)(2,1)} %collective-permute-done), kind=kOutput, calls=%fused_computation.17 | convolution fusion | flops 4296015872 | bytes 16777216 | tf_op jit(solution)/shard_map/dot_general | solution.py:22
  510.5 4.7 maximum_multiply_fusion
  (22 shorter events, 0.1 us)
Async XLA Ops:
  1.5 12.3 %copy-start.1 = (s32[32,32]{1,0:T(8,128)S(1)}, s32[32,32]{1,0:T(8,128)}, u32[]{:S(2)}) copy-start(s32[32,32]{1,0:T(8,128)} %param.8) | copy-start | bytes 12292
  96.9 118.0 %all-to-all-start = ((bf16[2,16,128,1024]{3,2,0,1:T(8,128)(2,1)}), bf16[2,16,128,1024]{3,2,0,1:T(8,128)(2,1)}, u32[]{:S(2)}, u32[]{:S(2)}) async-start(bf16[2,16,128,1024]{3,2,0,1:T(8,128)(2,1)} %pad_maximum_fusion), calls=%async_computation | async-start | bytes 16777216 | tf_op jit(solution)/shard_map/all_to_all | solution.py:49
  104.9 11.8 %copy-start.2 = (s32[64,16]{0,1:T(8,128)S(1)}, s32[64,16]{0,1:T(8,128)}, u32[]{:S(2)}) copy-start(s32[64,16]{0,1:T(8,128)} %param.9) | copy-start | bytes 12292
  214.9 187.2 %all-to-all-start.1 = ((bf16[2,8,256,1024]{3,2,0,1:T(8,128)(2,1)}), bf16[2,8,256,1024]{3,2,0,1:T(8,128)(2,1)}, u32[]{:S(2)}, u32[]{:S(2)}) async-start(bf16[2,8,256,1024]{3,2,0,1:T(8,128)(2,1)} %copy.37), calls=%async_computation.1 | async-start | bytes 16777216 | tf_op jit(solution)/shard_map/all_to_all | solution.py:65
  228.5 180.4 %copy-start.3 = (s32[32,16]{0,1:T(8,128)S(1)}, s32[32,16]{0,1:T(8,128)}, u32[]{:S(2)}) copy-start(s32[32,16]{0,1:T(8,128)} %param.10) | copy-start | bytes 6148
  228.5 209.6 %collective-permute-start = (bf16[2,2048,1024]{2,1,0:T(8,128)(2,1)}, bf16[2,2048,1024]{2,1,0:T(8,128)(2,1)}, u32[]{:S(2)}, u32[]{:S(2)}) collective-permute-start(bf16[2,2048,1024]{2,1,0:T(8,128)(2,1)} %bitcast.53), channel_id=1, source_target_pairs={{0,120},{8,0},{16,8},{24,16},{32,24},{40,32},{48,40},{56,48},{64,5... | collective-permute-start | bytes 25165832 | tf_op jit(solution)/shard_map/ppermute | solution.py:13
  408.0 94.9 %collective-permute-start.1 = (bf16[2048,1024]{1,0:T(8,128)(2,1)}, bf16[2048,1024]{1,0:T(8,128)(2,1)}, u32[]{:S(2)}, u32[]{:S(2)}) collective-permute-start(bf16[2048,1024]{1,0:T(8,128)(2,1)} %bitcast.9), channel_id=1, source_target_pairs={{0,7},{1,0},{2,1},{3,2},{4,3},{5,4},{6,5},{7,6},{8,15},{9,8},{10,9... | collective-permute-start | bytes 12582920 | tf_op jit(solution)/shard_map/ppermute | solution.py:13
  426.8 6.5 %copy-start = (bf16[1,8,256,1024]{3,2,0,1:T(8,128)(2,1)S(1)}, bf16[1,8,256,1024]{3,2,0,1:T(8,128)(2,1)}, u32[]{:S(2)}) copy-start(bf16[1,8,256,1024]{3,2,0,1:T(8,128)(2,1)} %get-tuple-element.11) | copy-start | bytes 12582916
  438.1 72.4 %slice-start = ((s8[8388608]{0:T(1024)(128)(4,1)}), s8[4194304]{0:T(1024)(128)(4,1)S(1)}, s32[]{:S(2)}) async-start(s8[8388608]{0:T(1024)(128)(4,1)} %bitcast.44), calls=%async_computation.2 | async-start | bytes 8388608
  444.6 65.8 %slice-start.1 = ((s8[8388608]{0:T(1024)(128)(4,1)}), s8[4194304]{0:T(1024)(128)(4,1)S(1)}, s32[]{:S(2)}) async-start(s8[8388608]{0:T(1024)(128)(4,1)} %bitcast.44), calls=%async_computation.3 | async-start | bytes 8388608
where the time goes:
time: 517 us; the launch traced here: 515 us
  waiting for transfers between devices  290 us (56%)
  local copies, waits for them, and re-layouts  155 us (30%)
  other arithmetic  28.5 us (6%)
  matrix products  25.4 us (5%)
  starting transfers between devices  15.9 us (3%)
    all_to_all x1, waiting for transfers between devices, on_device(): lax.all_to_all(b_send, 'col', split_axis=1, concat_axis=1, tiled=True)  172 us
    all_to_all x1, waiting for transfers between devices, on_device(): lax.all_to_all(jnp.stack(pieces).reshape(2, panels, per_peer * BS, a_widt...  59.9 us
    ppermute x2, waiting for transfers between devices, from_behind(): return lax.ppermute(value, axis, pairs)  58.3 us
    unnamed x15, local copies, waits for them, and re-layouts  36.7 us
    dot_general x4, matrix products, product(): lax.dot_general(left, right, (((0,), (0,)), ((), ())), preferred_element_...  25.4 us
    slice x1, local copies, waits for them, and re-layouts, on_device(): pieces.append(a_blocks[:, :, a_tile_id, :][order_idx])  17.5 us
    reshape x1, local copies, waits for them, and re-layouts, on_device(): a_blocks = a_masked.reshape(KB, BS, 2, a_width)  14.4 us
    mul x1, local copies, waits for them, and re-layouts, on_device(): a_masked = at * expand(mask_a)  12.3 us
  transfers between devices with their start and end apart: 4, of which 3 were waited for; matrix products, arithmetic and copies ran while one was open for 19% of the time, Pallas kernels for 0%

commit v1 on v0

v1 whole, which is shorter than its diff:
```python
import jax
import jax.numpy as jnp
from jax import lax
from jax.experimental import pallas as pl
from jax.experimental.pallas import tpu as pltpu
from jax.sharding import PartitionSpec as P

BS = 64
KB = 32
NP = 16
W = 1024
MIB = 1 << 20
Y_GROUPS = [list(range(8)), list(range(8, 16))]


def spread(mask, width):
    count = mask.shape[1]
    lane = lax.broadcasted_iota(jnp.int32, (count, width), 1) // BS
    entry = lax.broadcasted_iota(jnp.int32, (count, width), 0)
    chosen = jnp.where(lane == entry, 1.0, 0.0).astype(jnp.bfloat16)
    return jnp.dot(
        mask.astype(jnp.float32).astype(jnp.bfloat16), chosen, preferred_element_type=jnp.float32
    )


def prep_a(ids, kdist, mask, at, to_y, to_z, to_odd, wide, held, sems):
    step = pl.program_id(0)
    row_id, col_id = ids[0], ids[1]
    half = row_id // 8

    @pl.when(step == 0)
    def _():
        wide[...] = spread(mask[...], 2 * W)

    for b in range(4):
        block = step * 4 + b
        gain = wide[pl.ds(block, 1), :].astype(jnp.bfloat16)
        rows = pl.ds(pl.multiple_of(block * BS, BS), BS)
        held[rows, :] = at[b * BS:(b + 1) * BS, :] * gain
        pos = kdist[row_id * KB + block]
        inner = pl.ds(pl.multiple_of((pos % KB - 2 * row_id) * BS, BS), BS)
        for t in range(2):
            tile = (pos // KB - 2 * col_id - t + 2 * NP) % NP
            cols = pl.ds(t * W, W)
            src = held.at[rows, cols]
            near = (tile - 8 * half + NP) % NP
            far = (near + 8) % NP
            even = tile % 2 == 0

            @pl.when(even & (near < 8))
            def _():
                pltpu.make_async_copy(src, to_y.at[near, inner, cols], sems.at[0]).start()

            @pl.when(even & (near > 0) & (near <= 8))
            def _():
                pltpu.make_async_copy(src, to_y.at[near - 1, inner, cols], sems.at[0]).start()

            @pl.when(even & (far <= 8))
            def _():
                pltpu.make_async_copy(src, to_z.at[far // 2, inner, cols], sems.at[1]).start()

            @pl.when(tile % 2 == 1)
            def _():
                pltpu.make_async_copy(src, to_odd.at[tile - 1 + t, inner, :], sems.at[2]).start()

    @pl.when(step == pl.num_programs(0) - 1)
    def _():
        for n, ref in enumerate((to_y, to_z, to_odd)):
            pltpu.make_async_copy(ref, ref, sems.at[n]).wait()


def prep_b(ids, kdist, mask, bmat, x0, x1, x2, x3, to_z, wide, held, sems):
    step = pl.program_id(0)
    row_id, col_id = ids[0], ids[1]
    half, here = col_id // 4, col_id % 4
    to_x = (x0, x1, x2, x3)

    @pl.when(step == 0)
    def _():
        wide[...] = spread(mask[...], W)

    for b in range(8):
        block = step * 8 + b
        gain = wide[pl.ds(block, 1), :].astype(jnp.bfloat16)
        rows = pl.ds(pl.multiple_of(block * BS, BS), BS)
        held[rows, :] = bmat[b * BS:(b + 1) * BS, :] * gain
        pos = kdist[col_id * 2 * KB + block]
        inner = pl.ds(pl.multiple_of((pos % KB - 4 * col_id) * BS, BS), BS)
        tile = (pos // KB - row_id + NP) % NP
        src = held.at[rows, :]
        near = (tile - 8 * half + NP) % NP
        far = (near + 8) % NP
        even = tile % 2 == 0
        first = (near // 2 - here + 4) % 4
        second = (near // 2 - 1 - here + 8) % 4
        odd_at = (tile // 2 - here + 8) % 4
        odd_kind = jnp.where(tile // 8 == half, 1, 3)
        for hop in range(4):

            @pl.when(even & (near < 8) & (first == hop))
            def _():
                pltpu.make_async_copy(src, to_x[hop].at[0, inner, :], sems.at[hop]).start()

            @pl.when(even & (near > 0) & (near <= 8) & (second == hop))
            def _():
                pltpu.make_async_copy(src, to_x[hop].at[2, inner, :], sems.at[hop]).start()

            @pl.when((tile % 2 == 1) & (odd_at == hop))
            def _():
                pltpu.make_async_copy(src, to_x[hop].at[odd_kind, inner, :], sems.at[hop]).start()

        @pl.when(even & (far <= 8))
        def _():
            pltpu.make_async_copy(src, to_z.at[far // 2, inner, :], sems.at[4]).start()

    @pl.when(step == pl.num_programs(0) - 1)
    def _():
        for n, ref in enumerate((x0, x1, x2, x3, to_z)):
            pltpu.make_async_copy(ref, ref, sems.at[n]).wait()


def multiply(ids, filt, e_near, e_far, o_mine, o_swap, r0, r1, r2, r3, p0, p1, p2, p3, q,
             out, e_v, o_v, b_v, wide, sems):
    row_id, col_id = ids[0], ids[1]
    core = row_id % 2
    a_half = row_id // 8
    b_half, here = col_id // 4, col_id % 4
    copies = []

    def fetch(src, dst):
        copy = pltpu.make_async_copy(src, dst, sems.at[len(copies)])
        copy.start()
        copies.append(copy)

    def half_rows(which):
        return pl.ds(pl.multiple_of(which * W, W), W)

    fetch(e_near, e_v.at[half_rows(a_half)])
    fetch(e_far, e_v.at[half_rows(1 - a_half)])
    fetch(o_mine, o_v.at[core])
    fetch(o_swap, o_v.at[1 - core])
    for hop, (near, far) in enumerate(zip((r0, r1, r2, r3), (p0, p1, p2, p3))):
        place = (here - hop + 4) % 4
        mine = pl.ds(pl.multiple_of((b_half * 4 + place) * 256, 256), 256)
        other = pl.ds(pl.multiple_of(((1 - b_half) * 4 + place) * 256, 256), 256)
        fetch(near.at[pl.ds(0, 3)], b_v.at[:, mine])
        fetch(far.at[0], b_v.at[0, other])
        fetch(far.at[1], b_v.at[2, other])
        fetch(q.at[hop], b_v.at[1, other])
    wide[...] = spread(filt[...], W)
    for copy in copies:
        copy.wait()
    contract = (((0,), (0,)), ((), ()))
    for t in range(2):
        for m in range(4):
            col = t * W + m * 256
            left = e_v[:, col:col + 256]
            total = lax.dot_general(left, b_v[t + core], contract, preferred_element_type=jnp.float32)
            left = o_v[t, :, m * 256:(m + 1) * 256]
            total += lax.dot_general(left, b_v[t + 1 - core], contract, preferred_element_type=jnp.float32)
            for i in range(4):
                block = col // BS + i
                gain = wide[block:block + 1, :]
                out[block * BS:(block + 1) * BS, :] = total[i * BS:(i + 1) * BS, :] * gain


SMEM = pl.BlockSpec(memory_space=pltpu.SMEM)
ANY = pl.BlockSpec(memory_space=pl.ANY)
VMEM = pl.BlockSpec(memory_space=pltpu.VMEM)


def bf16(*shape):
    return jax.ShapeDtypeStruct(shape, jnp.bfloat16)


def on_device(at, bmat, mask_a, mask_b, filt, kdist):
    row_id = lax.axis_index("row")
    col_id = lax.axis_index("col")
    ids = jnp.stack([row_id, col_id]).astype(jnp.int32)
    here = col_id % 4

    def swap_z_hi(value):
        return lax.ppermute(value, "row", [(i, i ^ 8) for i in range(16)])

    def swap_z_lo(value):
        return lax.ppermute(value, "col", [(i, i ^ 4) for i in range(8)])

    def along_x(value, hop):
        return lax.ppermute(value, "col", [(i, i // 4 * 4 + (i % 4 + hop) % 4) for i in range(8)])

    x0, x1, x2, x3, b_z = pl.pallas_call(
        prep_b,
        grid=(8,),
        out_shape=[bf16(4, 256, W)] * 4 + [bf16(5, 256, W)],
        in_specs=[SMEM, SMEM, pl.BlockSpec((64, 16), lambda s: (0, 0)),
                  pl.BlockSpec((512, W), lambda s: (s, 0))],
        out_specs=[ANY] * 5,
        scratch_shapes=[pltpu.VMEM((64, W), jnp.float32), pltpu.VMEM((4096, W), jnp.bfloat16),
                        pltpu.SemaphoreType.DMA((5,))],
        compiler_params=pltpu.CompilerParams(vmem_limit_bytes=32 * MIB),
        name="prep_b",
    )(ids, kdist, mask_b, bmat)
    a_y, a_z, a_odd = pl.pallas_call(
        prep_a,
        grid=(8,),
        out_shape=[bf16(8, 128, 2 * W), bf16(5, 128, 2 * W), bf16(16, 128, W)],
        in_specs=[SMEM, SMEM, pl.BlockSpec((32, 32), lambda s: (0, 0)),
                  pl.BlockSpec((256, 2 * W), lambda s: (s, 0))],
        out_specs=[ANY] * 3,
        scratch_shapes=[pltpu.VMEM((32, 2 * W), jnp.float32), pltpu.VMEM((2048, 2 * W), jnp.bfloat16),
                        pltpu.SemaphoreType.DMA((3,))],
        compiler_params=pltpu.CompilerParams(vmem_limit_bytes=32 * MIB),
        name="prep_a",
    )(ids, kdist, mask_a, at)

    a_cross = swap_z_hi(a_z)
    b_cross = swap_z_lo(b_z)
    e_near = lax.all_to_all(a_y, "row", 0, 0, axis_index_groups=Y_GROUPS, tiled=True)
    r1, r2, r3 = along_x(x1, 1), along_x(x2, 2), along_x(x3, 3)
    o_mine = lax.all_to_all(a_odd, "row", 0, 0, tiled=True)
    o_swap = lax.ppermute(o_mine, "row", [(i, i ^ 1) for i in range(16)])

    q_send = jnp.concatenate([v[3:4] for v in (x0, r1, r2, r3)], axis=0)
    q_send, a_cross, b_cross = lax.optimization_barrier((q_send, a_cross, b_cross))
    q = swap_z_lo(q_send)
    far = [lax.dynamic_slice_in_dim(b_cross, (here + hop) % 4, 2, 0) for hop in range(4)]
    p1, p2, p3 = along_x(far[1], 1), along_x(far[2], 2), along_x(far[3], 3)
    a_again = jnp.stack([a_cross[:4], a_cross[1:]], axis=1).reshape(8, 128, 2 * W)
    e_far = lax.all_to_all(a_again, "row", 0, 0, axis_index_groups=Y_GROUPS, tiled=True)

    return pl.pallas_call(
        multiply,
        out_shape=jax.ShapeDtypeStruct((2 * W, W), jnp.float32),
        in_specs=[SMEM, VMEM] + [ANY] * 13,
        out_specs=VMEM,
        scratch_shapes=[pltpu.VMEM((2048, 2 * W), jnp.bfloat16), pltpu.VMEM((2, 2048, W), jnp.bfloat16),
                        pltpu.VMEM((3, 2048, W), jnp.bfloat16), pltpu.VMEM((32, W), jnp.float32),
                        pltpu.SemaphoreType.DMA((20,))],
        compiler_params=pltpu.CompilerParams(vmem_limit_bytes=56 * MIB),
        name="multiply",
    )(ids, filt, e_near.reshape(W, 2 * W), e_far.reshape(W, 2 * W), o_mine.reshape(2 * W, W),
      o_swap.reshape(2 * W, W), x0, r1, r2, r3, far[0], p1, p2, p3, q)


def solution(mesh):
    in_specs = (
        P("row", "col"),
        P("col", "row"),
        P("row", "col"),
        P("col", "row"),
        P("col", "row"),
        P(),
    )
    out_specs = P("col", "row")
    return jax.shard_map(
        on_device, mesh=mesh, in_specs=in_specs, out_specs=out_specs, check_vma=False
    )
```

time: 517 us -> 312 us (0.60)
  the two profiles are of different devices: /device:TPU:30 before, /device:TPU:1 now
where the time goes in v1:
time: 312 us
  waiting for transfers between devices  153 us (49%)
  Pallas kernels  60 us (19%)
  blocking collectives  59.9 us (19%)
  starting transfers between devices  21.3 us (7%)
  local copies, waits for them, and re-layouts  14.8 us (5%)
    ppermute x6, waiting for transfers between devices, along_x(): lax.ppermute(value, 'col', [(i, i // 4 * 4 + (i % 4 + hop) % 4) for i in...  136 us
    all_to_all x1, blocking collectives, on_device(): o_mine = lax.all_to_all(a_odd, 'row', 0, 0, tiled=True)  59.9 us
    pallas_call x1, Pallas kernels, on_device(): pl.pallas_call(multiply, out_shape=jax.ShapeDtypeStruct((2 * W, W), jnp.f...  31.1 us
    pallas_call x1, Pallas kernels, on_device(): pl.pallas_call(prep_b, grid=(8,), out_shape=[bf16(4, 256, W)] * 4 + [bf16...  23.1 us
    ppermute x1, waiting for transfers between devices, swap_z_hi(): return lax.ppermute(value, 'row', [(i, i ^ 8) for i in range(16)])  16.8 us
    unnamed x36, local copies, waits for them, and re-layouts  9.67 us
    ppermute x6, starting transfers between devices, along_x(): lax.ppermute(value, 'col', [(i, i // 4 * 4 + (i % 4 + hop) % 4) for i in...  8.43 us
  transfers between devices with their start and end apart: 12, of which 5 were waited for; matrix products, arithmetic and copies ran while one was open for 3% of the time, Pallas kernels for 7%

profile of v1, /device:TPU:1, one launch (start us, length us, event | category | flops | bytes accessed | tf_op | source)
XLA Modules:
  0.0 311.8 jit_solution(10505029822418964291)
XLA Ops:
  0.0 0.1 pad_add_fusion.ids
  0.1 3.4 %copy-done = bf16[2048,2048]{1,0:T(8,128)(2,1)S(1)} copy-done((bf16[2048,2048]{1,0:T(8,128)(2,1)S(1)}, bf16[2048,2048]{1,0:T(8,128)(2,1)}, u32[]{:S(2)}) %copy-start) | copy-done | bytes 8388632
  3.5 0.7 copy-done.4
  4.2 0.7 copy-done.5
  4.9 5.7 %prep_a.1 = (bf16[8,128,2048]{2,1,0:T(8,128)(2,1)S(1)}, bf16[5,128,2048]{2,1,0:T(8,128)(2,1)S(1)}, bf16[16,128,1024]{2,1,0:T(8,128)(2,1)S(1)}) custom-call(s32[2]{0:T(128)S(1)} %pad_add_fusion.ids, s32[512]{0:T(512)S(1)} %copy-done.5, s32[32,32]{1,0:T(8,128)S(1)} %copy-done.4, bf16[2048,2048]{1,0:T(8,128)(2,1)S(1)} %copy-done), custom_call_target="tpu_custom_call" | custom-call | tf_op jit(solution)/shard_map/prep_a/pallas_call | solution.py:203
  10.6 0.0 copy-start.2
  10.6 59.9 %all_to_all.15 = bf16[16,128,1024]{2,1,0:T(8,128)(2,1)} all-to-all(bf16[16,128,1024]{2,1,0:T(8,128)(2,1)S(1)} %get-tuple-element.24), channel_id=1, replica_groups=mesh['row'=16,'col'=8] {'row'}, dimensions={0} | all-to-all | bytes 8388608 | tf_op jit(solution)/shard_map/all_to_all | solution.py:220
  70.5 5.6 %all-to-all-start = ((bf16[8,128,2048]{2,1,0:T(8,128)(2,1)}), bf16[8,128,2048]{2,1,0:T(8,128)(2,1)}, u32[]{:S(2)}, u32[]{:S(2)}) async-start(bf16[8,128,2048]{2,1,0:T(8,128)(2,1)} %copy-done.2), calls=%async_computation | async-start | bytes 8388608 | tf_op jit(solution)/shard_map/all_to_all | solution.py:218
  76.2 0.0 copy-done.15
  76.2 0.1 copy.9.mask
  76.3 0.0 copy-start.1
  76.3 3.4 %copy-done.1 = bf16[4096,1024]{1,0:T(8,128)(2,1)S(1)} copy-done((bf16[4096,1024]{1,0:T(8,128)(2,1)S(1)}, bf16[4096,1024]{1,0:T(8,128)(2,1)}, u32[]{:S(2)}) %copy-start.1) | copy-done | bytes 8388632
  79.7 23.1 %prep_b.1 = (bf16[4,256,1024]{2,1,0:T(8,128)(2,1)S(1)}, bf16[4,256,1024]{2,1,0:T(8,128)(2,1)S(1)}, bf16[4,256,1024]{2,1,0:T(8,128)(2,1)S(1)}, bf16[4,256,1024]{2,1,0:T(8,128)(2,1)S(1)}, bf16[5,256,1024]{2,1,0:T(8,128)(2,1)S(1)}) custom-call(s32[2]{0:T(128)S(1)} %pad_add_fusion.ids, s32[512]{0:T(512)S(1)} %copy-done.6, s32[64,16]{1,0:T(8,128)S(1)} %copy.9.mask, ...), custom_call_target="tpu_custom_call" | custom-call | tf_op jit(solution)/shard_map/prep_b/pallas_call | solution.py:191
  102.8 0.8 collective-permute-start.4
  103.6 0.0 copy-done.9
  103.6 0.9 collective-permute-start.3
  104.5 1.2 collective-permute-start
  105.7 2.4 collective-permute-start.1
  108.2 1.1 collective-permute-start.2
  109.4 42.8 %collective-permute-done.r1 = bf16[4,256,1024]{2,1,0:T(8,128)(2,1)S(1)} collective-permute-done((bf16[4,256,1024]{2,1,0:T(8,128)(2,1)S(1)}, bf16[4,256,1024]{2,1,0:T(8,128)(2,1)S(1)}, u32[]{:S(2)}, u32[]{:S(2)}) %collective-permute-start) | collective-permute-done | bytes 2097184 | tf_op jit(solution)/shard_map/ppermute | solution.py:189
  152.2 45.9 %collective-permute-done.1.r2 = bf16[4,256,1024]{2,1,0:T(8,128)(2,1)S(1)} collective-permute-done((bf16[4,256,1024]{2,1,0:T(8,128)(2,1)S(1)}, bf16[4,256,1024]{2,1,0:T(8,128)(2,1)S(1)}, u32[]{:S(2)}, u32[]{:S(2)}) %collective-permute-start.1) | collective-permute-done | bytes 2097184 | tf_op jit(solution)/shard_map/ppermute | solution.py:189
  198.1 0.0 collective-permute-done.2.r3
  198.2 1.8 pad_maximum_fusion.1
  200.1 0.0 copy-done.11
  200.1 0.7 copy-done.12
  200.8 0.0 collective-permute-done.4
  200.8 16.8 %collective-permute-done.3 = bf16[5,128,2048]{2,1,0:T(8,128)(2,1)S(1)} collective-permute-done((bf16[5,128,2048]{2,1,0:T(8,128)(2,1)S(1)}, bf16[5,128,2048]{2,1,0:T(8,128)(2,1)S(1)}, u32[]{:S(2)}, u32[]{:S(2)}) %collective-permute-start.3) | collective-permute-done | bytes 2621472 | tf_op jit(solution)/shard_map/ppermute | solution.py:183
  217.5 1.0 collective-permute-start.5
  218.5 0.4 slice_bitcast_fusion.1
  218.9 0.4 pad_maximum_fusion
  219.3 2.3 copy.10
  221.5 0.0 all-to-all-done
  221.5 4.6 %all-to-all-start.1 = ((bf16[8,128,2048]{2,1,0:T(8,128)(2,1)}), bf16[8,128,2048]{2,1,0:T(8,128)(2,1)}, u32[]{:S(2)}, u32[]{:S(2)}) async-start(bf16[8,128,2048]{2,1,0:T(8,128)(2,1)} %bitcast.11), calls=%async_computation.1 | async-start | bytes 8388608 | tf_op jit(solution)/shard_map/all_to_all | solution.py:229
  226.1 0.0 collective-permute-start.9
  226.2 0.0 copy-start.16
  226.2 2.3 constant_dynamic-slice_fusion
  228.6 2.5 collective-permute-start.8
  231.1 0.5 collective-permute-start.7
  231.6 0.6 collective-permute-start.6
  232.2 0.0 copy-done.16
  232.2 0.7 copy.11.filt
  232.9 43.4 %collective-permute-done.8.p3 = bf16[2,256,1024]{2,1,0:T(8,128)(2,1)S(1)} collective-permute-done((bf16[2,256,1024]{2,1,0:T(8,128)(2,1)}, bf16[2,256,1024]{2,1,0:T(8,128)(2,1)S(1)}, u32[]{:S(2)}, u32[]{:S(2)}) %collective-permute-start.8) | collective-permute-done | bytes 1048608 | tf_op jit(solution)/shard_map/ppermute | solution.py:189
  276.2 0.0 collective-permute-done.7.p2
  276.2 4.2 %collective-permute-done.6.p1 = bf16[2,256,1024]{2,1,0:T(8,128)(2,1)} collective-permute-done((bf16[2,256,1024]{2,1,0:T(8,128)(2,1)}, bf16[2,256,1024]{2,1,0:T(8,128)(2,1)}, u32[]{:S(2)}, u32[]{:S(2)}) %collective-permute-start.6) | collective-permute-done | bytes 1048608 | tf_op jit(solution)/shard_map/ppermute | solution.py:189
  280.4 0.0 collective-permute-done.9.q
  280.4 0.0 all-to-all-done.1
  280.4 0.0 collective-permute-done.5
  280.5 31.1 %multiply.1 = f32[2048,1024]{1,0:T(8,128)} custom-call(s32[2]{0:T(128)} %copy-done.7, s32[32,16]{1,0:T(8,128)} %copy.11.filt, bf16[1024,2048]{1,0:T(8,128)(2,1)} %bitcast.2.e_near, bf16[1024,2048]{1,0:T(8,128)(2,1)} %bitcast.6.e_far, bf16[2048,1024]{1,0:T(8,128)(2,1)} %bitcast.7.o_mine, bf16[2048,1024]{1,0:T(8,128)(2,1)} %bitcast.8.o_swap, ...), custom_call_target="tpu_custom_call" | custom-call | tf_op jit(solution)/shard_map/multiply/pallas_call | solution.py:231
  (26 shorter events, 0.2 us)
Async XLA Ops:
  0.1 3.4 %copy-start = (bf16[2048,2048]{1,0:T(8,128)(2,1)S(1)}, bf16[2048,2048]{1,0:T(8,128)(2,1)}, u32[]{:S(2)}) copy-start(bf16[2048,2048]{1,0:T(8,128)(2,1)} %at.1) | copy-start | bytes 25165828
  3.5 0.7 copy-start.4
  4.2 0.7 copy-start.5
  4.9 71.4 %copy-start.7 = (s32[2]{0:T(128)}, s32[2]{0:T(128)S(1)}, u32[]{:S(2)}) copy-start(s32[2]{0:T(128)S(1)} %pad_add_fusion.ids) | copy-start | bytes 28
  10.6 59.9 %copy-start.2 = (bf16[8,128,2048]{2,1,0:T(8,128)(2,1)}, bf16[8,128,2048]{2,1,0:T(8,128)(2,1)S(1)}, u32[]{:S(2)}) copy-start(bf16[8,128,2048]{2,1,0:T(8,128)(2,1)S(1)} %get-tuple-element.16) | copy-start | bytes 12582916
  10.6 59.9 %copy-start.8 = (bf16[5,128,2048]{2,1,0:T(8,128)(2,1)}, bf16[5,128,2048]{2,1,0:T(8,128)(2,1)S(1)}, u32[]{:S(2)}) copy-start(bf16[5,128,2048]{2,1,0:T(8,128)(2,1)S(1)} %get-tuple-element.21) | copy-start | bytes 7864324
  70.5 5.7 %copy-start.15 = (s32[64,16]{0,1:T(8,128)S(1)}, s32[64,16]{0,1:T(8,128)}, u32[]{:S(2)}) copy-start(s32[64,16]{0,1:T(8,128)} %param.9) | copy-start | bytes 12292
  70.5 5.7 %copy-start.6 = (s32[512]{0:T(512)S(1)}, s32[512]{0:T(512)}, u32[]{:S(2)}) copy-start(s32[512]{0:T(512)} %kdist.3) | copy-start | bytes 6148
  70.5 151.0 %all-to-all-start = ((bf16[8,128,2048]{2,1,0:T(8,128)(2,1)}), bf16[8,128,2048]{2,1,0:T(8,128)(2,1)}, u32[]{:S(2)}, u32[]{:S(2)}) async-start(bf16[8,128,2048]{2,1,0:T(8,128)(2,1)} %copy-done.2), calls=%async_computation | async-start | bytes 8388608 | tf_op jit(solution)/shard_map/all_to_all | solution.py:218
  76.3 3.4 %copy-start.1 = (bf16[4096,1024]{1,0:T(8,128)(2,1)S(1)}, bf16[4096,1024]{1,0:T(8,128)(2,1)}, u32[]{:S(2)}) copy-start(bf16[4096,1024]{1,0:T(8,128)(2,1)} %bmat.1) | copy-start | bytes 25165828
  79.7 24.0 %copy-start.9 = (bf16[5,128,2048]{2,1,0:T(8,128)(2,1)S(1)}, bf16[5,128,2048]{2,1,0:T(8,128)(2,1)}, u32[]{:S(2)}) copy-start(bf16[5,128,2048]{2,1,0:T(8,128)(2,1)} %copy-done.8) | copy-start | bytes 7864324
  102.8 95.4 %copy-start.3 = (bf16[4,256,1024]{2,1,0:T(8,128)(2,1)}, bf16[4,256,1024]{2,1,0:T(8,128)(2,1)S(1)}, u32[]{:S(2)}) copy-start(bf16[4,256,1024]{2,1,0:T(8,128)(2,1)S(1)} %get-tuple-element.17.r0) | copy-start | bytes 6291460
  102.8 98.0 %collective-permute-start.4 = (bf16[5,256,1024]{2,1,0:T(8,128)(2,1)S(1)}, bf16[5,256,1024]{2,1,0:T(8,128)(2,1)S(1)}, u32[]{:S(2)}, u32[]{:S(2)}) collective-permute-start(bf16[5,256,1024]{2,1,0:T(8,128)(2,1)S(1)} %get-tuple-element.22), channel_id=1, source_target_pairs={{0,4},{1,5},{2,6},{3,7},{4,0},{5,1},{6,2},{7,3},{8,12},{9,13},{10,... | collective-permute-start | bytes 7864328 | tf_op jit(solution)/shard_map/ppermute | solution.py:186
  103.6 113.9 %collective-permute-start.3 = (bf16[5,128,2048]{2,1,0:T(8,128)(2,1)S(1)}, bf16[5,128,2048]{2,1,0:T(8,128)(2,1)S(1)}, u32[]{:S(2)}, u32[]{:S(2)}) collective-permute-start(bf16[5,128,2048]{2,1,0:T(8,128)(2,1)S(1)} %copy-done.9), channel_id=1, source_target_pairs={{0,64},{8,72},{16,80},{24,88},{32,96},{40,104},{48,112},{56,120},{... | collective-permute-start | bytes 7864328 | tf_op jit(solution)/shard_map/ppermute | solution.py:183
  104.5 47.7 %collective-permute-start = (bf16[4,256,1024]{2,1,0:T(8,128)(2,1)S(1)}, bf16[4,256,1024]{2,1,0:T(8,128)(2,1)S(1)}, u32[]{:S(2)}, u32[]{:S(2)}) collective-permute-start(bf16[4,256,1024]{2,1,0:T(8,128)(2,1)S(1)} %get-tuple-element.18), channel_id=1, source_target_pairs={{0,1},{1,2},{2,3},{3,0},{4,5},{5,6},{6,7},{7,4},{8,9},{9,10},{10,1... | collective-permute-start | bytes 6291464 | tf_op jit(solution)/shard_map/ppermute | solution.py:189
  105.7 92.4 %collective-permute-start.1 = (bf16[4,256,1024]{2,1,0:T(8,128)(2,1)S(1)}, bf16[4,256,1024]{2,1,0:T(8,128)(2,1)S(1)}, u32[]{:S(2)}, u32[]{:S(2)}) collective-permute-start(bf16[4,256,1024]{2,1,0:T(8,128)(2,1)S(1)} %get-tuple-element.19), channel_id=1, source_target_pairs={{0,2},{1,3},{2,0},{3,1},{4,6},{5,7},{6,4},{7,5},{8,10},{9,11},{10,... | collective-permute-start | bytes 6291464 | tf_op jit(solution)/shard_map/ppermute | solution.py:189
  108.2 90.0 %collective-permute-start.2 = (bf16[4,256,1024]{2,1,0:T(8,128)(2,1)S(1)}, bf16[4,256,1024]{2,1,0:T(8,128)(2,1)S(1)}, u32[]{:S(2)}, u32[]{:S(2)}) collective-permute-start(bf16[4,256,1024]{2,1,0:T(8,128)(2,1)S(1)} %get-tuple-element.20), channel_id=1, source_target_pairs={{0,3},{1,0},{2,1},{3,2},{4,7},{5,4},{6,5},{7,6},{8,11},{9,8},{10,9... | collective-permute-start | bytes 6291464 | tf_op jit(solution)/shard_map/ppermute | solution.py:189
  152.2 47.9 %copy-start.10 = (bf16[4,256,1024]{2,1,0:T(8,128)(2,1)}, bf16[4,256,1024]{2,1,0:T(8,128)(2,1)S(1)}, u32[]{:S(2)}) copy-start(bf16[4,256,1024]{2,1,0:T(8,128)(2,1)S(1)} %collective-permute-done.r1) | copy-start | bytes 6291460
  198.1 2.0 copy-start.11
  198.2 2.6 copy-start.12
  217.5 62.9 %collective-permute-start.5 = (bf16[16,128,1024]{2,1,0:T(8,128)(2,1)}, bf16[16,128,1024]{2,1,0:T(8,128)(2,1)}, u32[]{:S(2)}, u32[]{:S(2)}) collective-permute-start(bf16[16,128,1024]{2,1,0:T(8,128)(2,1)} %all_to_all.15), channel_id=1, source_target_pairs={{0,8},{8,0},{16,24},{24,16},{32,40},{40,32},{48,56},{56,48},{64,72... | collective-permute-start | bytes 12582920 | tf_op jit(solution)/shard_map/ppermute | solution.py:221
  221.5 58.9 %all-to-all-start.1 = ((bf16[8,128,2048]{2,1,0:T(8,128)(2,1)}), bf16[8,128,2048]{2,1,0:T(8,128)(2,1)}, u32[]{:S(2)}, u32[]{:S(2)}) async-start(bf16[8,128,2048]{2,1,0:T(8,128)(2,1)} %bitcast.11), calls=%async_computation.1 | async-start | bytes 8388608 | tf_op jit(solution)/shard_map/all_to_all | solution.py:229
  226.1 54.3 %collective-permute-start.9 = (bf16[4,256,1024]{2,1,0:T(8,128)(2,1)}, bf16[4,256,1024]{2,1,0:T(8,128)(2,1)}, u32[]{:S(2)}, u32[]{:S(2)}) collective-permute-start(bf16[4,256,1024]{2,1,0:T(8,128)(2,1)} %pad_maximum_fusion.1), channel_id=1, source_target_pairs={{0,4},{1,5},{2,6},{3,7},{4,0},{5,1},{6,2},{7,3},{8,12},{9,13},{10,... | collective-permute-start | bytes 6291464 | tf_op jit(solution)/shard_map/ppermute | solution.py:186
  226.2 6.0 %copy-start.16 = (s32[32,16]{0,1:T(8,128)S(1)}, s32[32,16]{0,1:T(8,128)}, u32[]{:S(2)}) copy-start(s32[32,16]{0,1:T(8,128)} %param.10) | copy-start | bytes 6148
  228.6 47.7 %collective-permute-start.8 = (bf16[2,256,1024]{2,1,0:T(8,128)(2,1)}, bf16[2,256,1024]{2,1,0:T(8,128)(2,1)S(1)}, u32[]{:S(2)}, u32[]{:S(2)}) collective-permute-start(bf16[2,256,1024]{2,1,0:T(8,128)(2,1)} %get-tuple-element.27), channel_id=1, source_target_pairs={{0,3},{1,0},{2,1},{3,2},{4,7},{5,4},{6,5},{7,6},{8,11},{9,8},{10,9... | collective-permute-start | bytes 3145736 | tf_op jit(solution)/shard_map/ppermute | solution.py:189
  231.1 45.2 %collective-permute-start.7 = (bf16[2,256,1024]{2,1,0:T(8,128)(2,1)}, bf16[2,256,1024]{2,1,0:T(8,128)(2,1)S(1)}, u32[]{:S(2)}, u32[]{:S(2)}) collective-permute-start(bf16[2,256,1024]{2,1,0:T(8,128)(2,1)} %get-tuple-element.28), channel_id=1, source_target_pairs={{0,2},{1,3},{2,0},{3,1},{4,6},{5,7},{6,4},{7,5},{8,10},{9,11},{10,... | collective-permute-start | bytes 3145736 | tf_op jit(solution)/shard_map/ppermute | solution.py:189
  231.6 48.8 %collective-permute-start.6 = (bf16[2,256,1024]{2,1,0:T(8,128)(2,1)}, bf16[2,256,1024]{2,1,0:T(8,128)(2,1)}, u32[]{:S(2)}, u32[]{:S(2)}) collective-permute-start(bf16[2,256,1024]{2,1,0:T(8,128)(2,1)} %get-tuple-element.29), channel_id=1, source_target_pairs={{0,1},{1,2},{2,3},{3,0},{4,5},{5,6},{6,7},{7,4},{8,9},{9,10},{10,1... | collective-permute-start | bytes 3145736 | tf_op jit(solution)/shard_map/ppermute | solution.py:189
  276.2 4.2 %copy-start.13 = (bf16[2,256,1024]{2,1,0:T(8,128)(2,1)}, bf16[2,256,1024]{2,1,0:T(8,128)(2,1)S(1)}, u32[]{:S(2)}) copy-start(bf16[2,256,1024]{2,1,0:T(8,128)(2,1)S(1)} %collective-permute-done.8.p3) | copy-start | bytes 3145732
  276.2 4.2 %copy-start.14 = (bf16[2,256,1024]{2,1,0:T(8,128)(2,1)}, bf16[2,256,1024]{2,1,0:T(8,128)(2,1)S(1)}, u32[]{:S(2)}) copy-start(bf16[2,256,1024]{2,1,0:T(8,128)(2,1)S(1)} %collective-permute-done.7.p2) | copy-start | bytes 3145732

commit v2 on v1

v2 whole, which is shorter than its diff:
```python
import jax
import jax.numpy as jnp
from jax import lax
from jax.experimental import pallas as pl
from jax.experimental.pallas import tpu as pltpu
from jax.sharding import PartitionSpec as P

BS = 64
KB = 32
NP = 16
W = 1024
MIB = 1 << 20
Y_GROUPS = [list(range(8)), list(range(8, 16))]


def spread(mask, width):
    count = mask.shape[1]
    lane = lax.broadcasted_iota(jnp.int32, (count, width), 1) // BS
    entry = lax.broadcasted_iota(jnp.int32, (count, width), 0)
    chosen = jnp.where(lane == entry, 1.0, 0.0).astype(jnp.bfloat16)
    return jnp.dot(
        mask.astype(jnp.float32).astype(jnp.bfloat16), chosen, preferred_element_type=jnp.float32
    )


def prep_a(ids, kdist, mask, at, to_y, to_z, wide, held, in_sems, sems):
    row_id, col_id = ids[0], ids[1]
    half = row_id // 8

    def chunk(n):
        rows = pl.ds(n * 256, 256)
        return pltpu.make_async_copy(at.at[rows], held.at[rows], in_sems.at[n])

    for n in range(8):
        chunk(n).start()
    wide[...] = spread(mask[...], 2 * W)
    for block in range(KB):
        if block % 4 == 0:
            chunk(block // 4).wait()
        gain = wide[block:block + 1, :].astype(jnp.bfloat16)
        rows = pl.ds(block * BS, BS)
        held[rows, :] = held[rows, :] * gain
        pos = kdist[row_id * KB + block]
        slot = (pos % KB - 2 * row_id) * BS
        inner = pl.ds(pl.multiple_of(slot, BS), BS)
        for t in range(2):
            tile = (pos // KB - 2 * col_id - t + 2 * NP) % NP
            cols = pl.ds(t * W, W)
            src = held.at[rows, cols]
            near = (tile - 8 * half + NP) % NP
            far = (near + 8) % NP
            odd = tile % 2 == 1
            even = tile % 2 == 0
            first = jnp.where(odd, tile // 2 % 4 * 2 + t, near)
            first_row = jnp.where(odd, 128, 0) + slot
            first_col = jnp.where(odd, jnp.where(tile // 8 == half, 0, W), t * W)

            @pl.when(odd | (near < 8))
            def _():
                dst = to_y.at[first, pl.ds(pl.multiple_of(first_row, BS), BS), pl.ds(pl.multiple_of(first_col, W), W)]
                pltpu.make_async_copy(src, dst, sems.at[0]).start()

            @pl.when(even & (near > 0) & (near <= 8))
            def _():
                pltpu.make_async_copy(src, to_y.at[near - 1, inner, cols], sems.at[0]).start()

            @pl.when(even & (far <= 8))
            def _():
                pltpu.make_async_copy(src, to_z.at[far // 2, inner, cols], sems.at[1]).start()

    for n, ref in enumerate((to_y, to_z)):
        pltpu.make_async_copy(ref, ref, sems.at[n]).wait()


def prep_b(ids, kdist, mask, bmat, x0, x1, x2, x3, to_z, wide, held, in_sems, sems):
    row_id, col_id = ids[0], ids[1]
    half, here = col_id // 4, col_id % 4
    to_x = (x0, x1, x2, x3)

    def chunk(n):
        rows = pl.ds(n * 512, 512)
        return pltpu.make_async_copy(bmat.at[rows], held.at[rows], in_sems.at[n])

    for n in range(8):
        chunk(n).start()
    wide[...] = spread(mask[...], W)
    for block in range(2 * KB):
        if block % 8 == 0:
            chunk(block // 8).wait()
        gain = wide[block:block + 1, :].astype(jnp.bfloat16)
        rows = pl.ds(block * BS, BS)
        held[rows, :] = held[rows, :] * gain
        pos = kdist[col_id * 2 * KB + block]
        inner = pl.ds(pl.multiple_of((pos % KB - 4 * col_id) * BS, BS), BS)
        tile = (pos // KB - row_id + NP) % NP
        src = held.at[rows, :]
        near = (tile - 8 * half + NP) % NP
        far = (near + 8) % NP
        odd = tile % 2 == 1
        even = tile % 2 == 0
        first = (jnp.where(odd, tile, near) // 2 - here + 8) % 4
        kind = jnp.where(odd, jnp.where(tile // 8 == half, 1, 3), 0)
        second = (near // 2 - 1 - here + 8) % 4

        def send(hop, kind):
            def to(n):
                def run():
                    pltpu.make_async_copy(src, to_x[n].at[kind, inner, :], sems.at[n]).start()

                return run

            lax.cond(hop < 2, lambda: lax.cond(hop == 0, to(0), to(1)), lambda: lax.cond(hop == 2, to(2), to(3)))

        @pl.when(odd | (near < 8))
        def _():
            send(first, kind)

        @pl.when(even & (near > 0) & (near <= 8))
        def _():
            send(second, 2)

        @pl.when(even & (far <= 8))
        def _():
            pltpu.make_async_copy(src, to_z.at[far // 2, inner, :], sems.at[4]).start()

    for n, ref in enumerate((x0, x1, x2, x3, to_z)):
        pltpu.make_async_copy(ref, ref, sems.at[n]).wait()


CONTRACT = (((0,), (0,)), ((), ()))


def product(left, right):
    return lax.dot_general(left, right, CONTRACT, preferred_element_type=jnp.float32)


def multiply(ids, near_a, e_far, o_near, o_cross, o_swap, r0, r1, r2, r3, p0, p1, p2, p3,
             out, left_out, left_v, b_v, sems, out_sem):
    row_id, col_id = ids[0], ids[1]
    core = row_id % 2
    a_half = row_id // 8
    b_half, here = col_id // 4, col_id % 4
    copies = []

    def fetch(src, dst):
        copy = pltpu.make_async_copy(src, dst, sems.at[len(copies)])
        copy.start()
        copies.append(copy)

    def group(which):
        return pl.ds(pl.multiple_of(which * W, W), W)

    sources = pl.ds(0, 8)
    a_near = pl.ds(pl.multiple_of(a_half * 8, 8), 8)
    a_far = pl.ds(pl.multiple_of(8 - a_half * 8, 8), 8)
    fetch(near_a.at[sources, pl.ds(0, 128), group(core)], left_v.at[0, core, a_near])
    fetch(near_a.at[sources, pl.ds(0, 128), group(1 - core)], left_v.at[1, 1 - core, a_near])
    fetch(near_a.at[sources, pl.ds(128, 128), group(0)], left_v.at[1, core, a_near])
    fetch(o_near, left_v.at[0, 1 - core, a_near])
    for hop, near in enumerate((r0, r1, r2, r3)):
        place = (here - hop + 4) % 4
        fetch(near.at[pl.ds(0, 3)], b_v.at[:, pl.ds(pl.multiple_of((b_half * 4 + place) * 256, 256), 256)])
    for hop, far in enumerate((p0, p1, p2, p3)):
        place = (here - hop + 4) % 4
        rows = pl.ds(pl.multiple_of(((1 - b_half) * 4 + place) * 256, 256), 256)
        fetch(far.at[0], b_v.at[0, rows])
        fetch(far.at[1], b_v.at[2, rows])
    fetch(e_far.at[sources, :, group(core)], left_v.at[0, core, a_far])
    fetch(e_far.at[sources, :, group(1 - core)], left_v.at[1, 1 - core, a_far])
    fetch(o_cross, left_v.at[1, core, a_far])
    fetch(o_swap, left_v.at[0, 1 - core, a_far])
    for copy in copies:
        copy.wait()
    later = []
    for t in range(2):
        for hop in range(4):
            place = (here - hop + 4) % 4
            part = pltpu.make_async_copy(
                left_v.at[1, t, pl.ds((1 - b_half) * 8 + place * 2, 2)],
                left_out.at[t, pl.ds(hop * 2, 2)], out_sem.at[t * 4 + hop])
            part.start()
            later.append(part)
    near_rows = pl.ds(pl.multiple_of(b_half * W, W), W)
    near_pieces = pl.ds(pl.multiple_of(b_half * 8, 8), 8)
    for t in range(2):
        for m in range(4):
            cols = slice(m * 256, (m + 1) * 256)
            total = product(left_v[0, t, :, :, cols].reshape(2 * W, 256), b_v[2 * t])
            total += product(left_v[1, t, near_pieces, :, cols].reshape(W, 256), b_v[1, near_rows])
            out[t * W + m * 256:t * W + (m + 1) * 256, :] = total
    for part in later:
        part.wait()


def finish(filt, part, left, right, out, wide):
    step = pl.program_id(0)

    @pl.when(step == 0)
    def _():
        wide[...] = spread(filt[...], W)

    total = part[...] + product(left[...].reshape(W, 256), right[...].reshape(W, W))
    for i in range(4):
        rows = slice(i * BS, (i + 1) * BS)
        out[rows, :] = total[rows, :] * wide[pl.ds(step * 4 + i, 1), :]


SMEM = pl.BlockSpec(memory_space=pltpu.SMEM)
ANY = pl.BlockSpec(memory_space=pl.ANY)
HBM = pl.BlockSpec(memory_space=pltpu.HBM)
VMEM = pl.BlockSpec(memory_space=pltpu.VMEM)


def bf16(*shape):
    return jax.ShapeDtypeStruct(shape, jnp.bfloat16)


def on_device(at, bmat, mask_a, mask_b, filt, kdist):
    row_id = lax.axis_index("row")
    col_id = lax.axis_index("col")
    ids = jnp.stack([row_id, col_id]).astype(jnp.int32)
    here = col_id % 4

    def swap_z_hi(value):
        return lax.ppermute(value, "row", [(i, i ^ 8) for i in range(16)])

    def swap_z_lo(value):
        return lax.ppermute(value, "col", [(i, i ^ 4) for i in range(8)])

    def swap_core(value):
        return lax.ppermute(value, "row", [(i, i ^ 1) for i in range(16)])

    def along_x(value, hop):
        return lax.ppermute(value, "col", [(i, i // 4 * 4 + (i % 4 + hop) % 4) for i in range(8)])

    def along_y(value):
        return lax.all_to_all(value, "row", 0, 0, axis_index_groups=Y_GROUPS, tiled=True)

    a_y, a_z = pl.pallas_call(
        prep_a,
        out_shape=[bf16(8, 256, 2 * W), bf16(5, 128, 2 * W)],
        in_specs=[SMEM, SMEM, VMEM, HBM],
        out_specs=[ANY] * 2,
        scratch_shapes=[pltpu.VMEM((32, 2 * W), jnp.float32), pltpu.VMEM((2048, 2 * W), jnp.bfloat16),
                        pltpu.SemaphoreType.DMA((8,)), pltpu.SemaphoreType.DMA((2,))],
        compiler_params=pltpu.CompilerParams(vmem_limit_bytes=24 * MIB),
        name="prep_a",
    )(ids, kdist, mask_a, pltpu.with_memory_space_constraint(at, pltpu.HBM))
    x0, x1, x2, x3, b_z = pl.pallas_call(
        prep_b,
        out_shape=[bf16(4, 256, W)] * 4 + [bf16(5, 256, W)],
        in_specs=[SMEM, SMEM, VMEM, HBM],
        out_specs=[ANY] * 5,
        scratch_shapes=[pltpu.VMEM((64, W), jnp.float32), pltpu.VMEM((4096, W), jnp.bfloat16),
                        pltpu.SemaphoreType.DMA((8,)), pltpu.SemaphoreType.DMA((5,))],
        compiler_params=pltpu.CompilerParams(vmem_limit_bytes=24 * MIB),
        name="prep_b",
    )(ids, kdist, mask_b, pltpu.with_memory_space_constraint(bmat, pltpu.HBM))

    a_cross = swap_z_hi(a_z)
    b_cross = swap_z_lo(b_z)
    near_a = along_y(a_y)
    r1, r2, r3 = along_x(x1, 1), along_x(x2, 2), along_x(x3, 3)

    o_cross = swap_z_hi(near_a[:, 128:, W:])
    o_near = swap_core(near_a[:, 128:, :W])

    q_send = jnp.concatenate([v[3:4] for v in (x0, r1, r2, r3)], axis=0)
    q_send, a_cross, b_cross = lax.optimization_barrier((q_send, a_cross, b_cross))
    q = swap_z_lo(q_send)
    far = [lax.dynamic_slice_in_dim(b_cross, (here + hop) % 4, 2, 0) for hop in range(4)]
    p1, p2, p3 = along_x(far[1], 1), along_x(far[2], 2), along_x(far[3], 3)
    e_far = along_y(jnp.stack([a_cross[:4], a_cross[1:]], axis=1).reshape(8, 128, 2 * W))

    o_cross, p1, p2, p3 = lax.optimization_barrier((o_cross, p1, p2, p3))
    o_swap = swap_core(o_cross)

    part, left = pl.pallas_call(
        multiply,
        out_shape=[jax.ShapeDtypeStruct((2 * W, W), jnp.float32), bf16(2, 8, 128, W)],
        in_specs=[SMEM] + [ANY] * 13,
        out_specs=[VMEM, ANY],
        scratch_shapes=[pltpu.VMEM((2, 2, 16, 128, W), jnp.bfloat16), pltpu.VMEM((3, 2048, W), jnp.bfloat16),
                        pltpu.SemaphoreType.DMA((20,)), pltpu.SemaphoreType.DMA((8,))],
        compiler_params=pltpu.CompilerParams(vmem_limit_bytes=52 * MIB),
        name="multiply",
    )(ids, near_a, e_far, o_near, o_cross, o_swap, x0, r1, r2, r3, far[0], p1, p2, p3)
    return pl.pallas_call(
        finish,
        grid=(8,),
        out_shape=jax.ShapeDtypeStruct((2 * W, W), jnp.float32),
        in_specs=[pl.BlockSpec((32, 16), lambda s: (0, 0)), pl.BlockSpec((256, W), lambda s: (s, 0)),
                  pl.BlockSpec((None, 8, 128, 256), lambda s: (s // 4, 0, 0, s % 4)),
                  pl.BlockSpec((4, 256, W), lambda s: (0, 0, 0))],
        out_specs=pl.BlockSpec((256, W), lambda s: (s, 0)),
        scratch_shapes=[pltpu.VMEM((32, W), jnp.float32)],
        compiler_params=pltpu.CompilerParams(vmem_limit_bytes=32 * MIB),
        name="finish",
    )(filt, part, left, q)


def solution(mesh):
    in_specs = (
        P("row", "col"),
        P("col", "row"),
        P("row", "col"),
        P("col", "row"),
        P("col", "row"),
        P(),
    )
    out_specs = P("col", "row")
    return jax.shard_map(
        on_device, mesh=mesh, in_specs=in_specs, out_specs=out_specs, check_vma=False
    )
```

time: 312 us -> 287 us (0.920)
  blocking collectives: 59.9 us -> 0 us
  waiting for transfers between devices: 153 us -> 166 us
  local copies, waits for them, and re-layouts: 14.8 us -> 27.1 us
  starting transfers between devices: 21.3 us -> 28.8 us
    all_to_all x1 -> x0, blocking collectives: 59.9 us -> none  [on_device(): o_mine = lax.all_to_all(a_odd, 'row', 0, 0, tiled=True)]
    ppermute x2, waiting for transfers between devices: 0.01 us -> 16.2 us  [swap_z_lo(): return lax.ppermute(value, 'col', [(i, i ^ 4) for i in range(8)])]
    unnamed x36 -> x38, local copies, waits for them, and re-layouts: 9.67 us -> 16.4 us
    slice x0 -> x1, local copies, waits for them, and re-layouts: none -> 4.83 us  [on_device(): o_cross = swap_z_hi(near_a[:, 128:, W:])]
    ppermute x6, waiting for transfers between devices: 136 us -> 132 us  [along_x(): lax.ppermute(value, 'col', [(i, i // 4 * 4 + (i % 4 + hop) % 4) for i in...]
    ppermute x1 -> x2, waiting for transfers between devices: 0.01 us -> 3.72 us  [swap_core(): return lax.ppermute(value, 'row', [(i, i ^ 1) for i in range(16)])]
    ppermute x1 -> x2, waiting for transfers between devices: 16.8 us -> 13.6 us  [swap_z_hi(): return lax.ppermute(value, 'row', [(i, i ^ 8) for i in range(16)])]
    pallas_call x3 -> x4, Pallas kernels: 60 us -> 62.5 us  [the longest x1 26.3 us: on_device(): pl.pallas_call(multiply, out_shape=[jax.ShapeDtypeStruct((2 * W, W), jnp....]
  transfers between devices with their start and end apart: 12 -> 14, of which waited for: 5 -> 7; matrix products, arithmetic and copies ran while one was open for 3% -> 3% of each run, Pallas kernels for 7% -> 17%
where the time goes in v2:
time: 287 us; the launch traced here: 286 us
  waiting for transfers between devices  166 us (58%)
  Pallas kernels  62.5 us (22%)
  starting transfers between devices  28.8 us (10%)
  local copies, waits for them, and re-layouts  27.1 us (9%)
    ppermute x6, waiting for transfers between devices, along_x(): lax.ppermute(value, 'col', [(i, i // 4 * 4 + (i % 4 + hop) % 4) for i in...  132 us
    pallas_call x1, Pallas kernels, on_device(): pl.pallas_call(multiply, out_shape=[jax.ShapeDtypeStruct((2 * W, W), jnp....  26.3 us
    pallas_call x1, Pallas kernels, on_device(): pl.pallas_call(prep_b, out_shape=[bf16(4, 256, W)] * 4 + [bf16(5, 256, W)...  21.2 us
    unnamed x38, local copies, waits for them, and re-layouts  16.4 us
    ppermute x2, waiting for transfers between devices, swap_z_lo(): return lax.ppermute(value, 'col', [(i, i ^ 4) for i in range(8)])  16.2 us
    ppermute x2, waiting for transfers between devices, swap_z_hi(): return lax.ppermute(value, 'row', [(i, i ^ 8) for i in range(16)])  13.6 us
    all_to_all x2, starting transfers between devices, along_y(): lax.all_to_all(value, 'row', 0, 0, axis_index_groups=Y_GROUPS, tiled=True)  11.8 us
    ppermute x6, starting transfers between devices, along_x(): lax.ppermute(value, 'col', [(i, i // 4 * 4 + (i % 4 + hop) % 4) for i in...  9.66 us
  transfers between devices with their start and end apart: 14, of which 7 were waited for; matrix products, arithmetic and copies ran while one was open for 3% of the time, Pallas kernels for 17%

profile of v2, /device:TPU:1, one launch (start us, length us, event | category | flops | bytes accessed | tf_op | source)
XLA Modules:
  0.0 286.1 jit_solution(6018475766403547753)
XLA Ops:
  0.0 0.1 pad_add_fusion.ids
  0.1 0.7 copy-done.4
  0.8 0.7 copy-done.5
  1.5 6.8 %prep_a.1 = (bf16[8,256,2048]{2,1,0:T(8,128)(2,1)S(1)}, bf16[5,128,2048]{2,1,0:T(8,128)(2,1)S(1)}) custom-call(s32[2]{0:T(128)S(1)} %pad_add_fusion.ids, s32[512]{0:T(512)S(1)} %copy-done.5, s32[32,32]{1,0:T(8,128)S(1)} %copy-done.4, bf16[2048,2048]{1,0:T(8,128)(2,1)} %at.1), custom_call_target="tpu_custom_call" | custom-call | tf_op jit(solution)/shard_map/prep_a/pallas_call | solution.py:239
  8.3 0.0 copy-start
  8.3 3.4 %copy-done = bf16[8,256,2048]{2,1,0:T(8,128)(2,1)} copy-done((bf16[8,256,2048]{2,1,0:T(8,128)(2,1)}, bf16[8,256,2048]{2,1,0:T(8,128)(2,1)S(1)}, u32[]{:S(2)}) %copy-start) | copy-done | bytes 8388632
  11.7 1.5 copy-done.7
  13.1 6.4 %all-to-all-start = ((bf16[8,256,2048]{2,1,0:T(8,128)(2,1)}), bf16[8,256,2048]{2,1,0:T(8,128)(2,1)}, u32[]{:S(2)}, u32[]{:S(2)}) async-start(bf16[8,256,2048]{2,1,0:T(8,128)(2,1)} %copy-done), calls=%async_computation | async-start | bytes 16777216 | tf_op jit(solution)/shard_map/all_to_all | solution.py:237
  19.5 0.1 copy.7.mask
  19.6 21.2 %prep_b.1 = (bf16[4,256,1024]{2,1,0:T(8,128)(2,1)S(1)}, bf16[4,256,1024]{2,1,0:T(8,128)(2,1)S(1)}, bf16[4,256,1024]{2,1,0:T(8,128)(2,1)S(1)}, bf16[4,256,1024]{2,1,0:T(8,128)(2,1)S(1)}, bf16[5,256,1024]{2,1,0:T(8,128)(2,1)S(1)}) custom-call(s32[2]{0:T(128)S(1)} %pad_add_fusion.ids, s32[512]{0:T(512)S(1)} %copy-done.6, s32[64,16]{1,0:T(8,128)S(1)} %copy.7.mask, ...), custom_call_target="tpu_custom_call" | custom-call | tf_op jit(solution)/shard_map/prep_b/pallas_call | solution.py:249
  40.8 1.8 collective-permute-start.4
  42.6 3.3 %collective-permute-start.3 = (bf16[5,128,2048]{2,1,0:T(8,128)(2,1)S(1)}, bf16[5,128,2048]{2,1,0:T(8,128)(2,1)S(1)}, u32[]{:S(2)}, u32[]{:S(2)}) collective-permute-start(bf16[5,128,2048]{2,1,0:T(8,128)(2,1)S(1)} %copy-done.8), channel_id=1, source_target_pairs={{0,64},{8,72},{16,80},{24,88},{32,96},{40,104},{48,112},{56,120},{... | collective-permute-start | bytes 7864328 | tf_op jit(solution)/shard_map/ppermute | solution.py:225
  45.9 1.2 collective-permute-start
  47.1 2.5 collective-permute-start.1
  49.6 1.2 collective-permute-start.2
  50.8 42.9 %collective-permute-done.r1 = bf16[4,256,1024]{2,1,0:T(8,128)(2,1)S(1)} collective-permute-done((bf16[4,256,1024]{2,1,0:T(8,128)(2,1)S(1)}, bf16[4,256,1024]{2,1,0:T(8,128)(2,1)S(1)}, u32[]{:S(2)}, u32[]{:S(2)}) %collective-permute-start) | collective-permute-done | bytes 2097184 | tf_op jit(solution)/shard_map/ppermute | solution.py:234
  93.7 45.8 %collective-permute-done.1.r2 = bf16[4,256,1024]{2,1,0:T(8,128)(2,1)S(1)} collective-permute-done((bf16[4,256,1024]{2,1,0:T(8,128)(2,1)S(1)}, bf16[4,256,1024]{2,1,0:T(8,128)(2,1)S(1)}, u32[]{:S(2)}, u32[]{:S(2)}) %collective-permute-start.1) | collective-permute-done | bytes 2097184 | tf_op jit(solution)/shard_map/ppermute | solution.py:234
  139.5 0.0 collective-permute-done.2.r3
  139.6 1.2 copy-done.11
  140.8 1.4 copy-done.12
  142.2 1.6 pad_maximum_fusion.1
  143.8 1.5 copy-done.9
  145.4 13.6 %collective-permute-done.3 = bf16[5,128,2048]{2,1,0:T(8,128)(2,1)S(1)} collective-permute-done((bf16[5,128,2048]{2,1,0:T(8,128)(2,1)S(1)}, bf16[5,128,2048]{2,1,0:T(8,128)(2,1)S(1)}, u32[]{:S(2)}, u32[]{:S(2)}) %collective-permute-start.3) | collective-permute-done | bytes 2621472 | tf_op jit(solution)/shard_map/ppermute | solution.py:225
  159.0 0.0 all-to-all-done.near_a
  159.0 4.8 %fusion = (bf16[8,128,1024]{2,1,0:T(8,128)(2,1)}, bf16[8,128,1024]{2,1,0:T(8,128)(2,1)}) fusion(bf16[8,256,2048]{2,1,0:T(8,128)(2,1)} %all-to-all-done.near_a), kind=kLoop, calls=%fused_computation.9 | loop fusion | bytes 8388608 | tf_op jit(solution)/shard_map/slice | solution.py:265
  163.8 0.0 collective-permute-start.6
  163.8 0.5 slice_bitcast_fusion.1
  164.3 0.4 pad_maximum_fusion
  164.7 2.3 copy.8
  167.0 5.4 %all-to-all-start.1 = ((bf16[8,128,2048]{2,1,0:T(8,128)(2,1)}), bf16[8,128,2048]{2,1,0:T(8,128)(2,1)}, u32[]{:S(2)}, u32[]{:S(2)}) async-start(bf16[8,128,2048]{2,1,0:T(8,128)(2,1)} %bitcast.7), calls=%async_computation.1 | async-start | bytes 8388608 | tf_op jit(solution)/shard_map/all_to_all | solution.py:237
  172.4 2.9 %constant_dynamic-slice_fusion = (bf16[2,256,1024]{2,1,0:T(8,128)(2,1)S(1)}, bf16[2,256,1024]{2,1,0:T(8,128)(2,1)S(1)}, bf16[2,256,1024]{2,1,0:T(8,128)(2,1)S(1)}, bf16[2,256,1024]{2,1,0:T(8,128)(2,1)S(1)}) fusion(bf16[5,256,1024]{2,1,0:T(8,128)(2,1)} %copy-done.9, s32[]{:T(128)S(6)} %select_n.43, s32[]{:T(128)S(6)} %select_n.41, s32[]{:T(128)S(6)} %select_n.39, ...), kind=kLoop, calls=%fused_computation.4 | loop fusion | bytes 8388624 | tf_op jit(solution)/shard_map/dynamic_slice | solution.py:271
  175.3 1.3 collective-permute-start.7
  176.6 2.4 collective-permute-start.8
  179.0 1.1 collective-permute-start.9
  180.2 1.0 collective-permute-start.5
  181.2 20.1 %collective-permute-done.7.p1 = bf16[2,256,1024]{2,1,0:T(8,128)(2,1)S(1)} collective-permute-done((bf16[2,256,1024]{2,1,0:T(8,128)(2,1)S(1)}, bf16[2,256,1024]{2,1,0:T(8,128)(2,1)S(1)}, u32[]{:S(2)}, u32[]{:S(2)}) %collective-permute-start.7) | collective-permute-done | bytes 1048608 | tf_op jit(solution)/shard_map/ppermute | solution.py:234
  201.3 23.3 %collective-permute-done.8.p2 = bf16[2,256,1024]{2,1,0:T(8,128)(2,1)S(1)} collective-permute-done((bf16[2,256,1024]{2,1,0:T(8,128)(2,1)S(1)}, bf16[2,256,1024]{2,1,0:T(8,128)(2,1)S(1)}, u32[]{:S(2)}, u32[]{:S(2)}) %collective-permute-start.8) | collective-permute-done | bytes 1048608 | tf_op jit(solution)/shard_map/ppermute | solution.py:234
  224.6 0.0 collective-permute-done.9.p3
  224.6 1.1 collective-permute-start.10
  225.7 0.3 copy-done.15
  225.9 0.1 collective-permute-start.11
  226.0 0.1 copy.9.filt
  226.1 3.7 %collective-permute-done.10.o_swap = bf16[8,128,1024]{2,1,0:T(8,128)(2,1)} collective-permute-done((bf16[8,128,1024]{2,1,0:T(8,128)(2,1)}, bf16[8,128,1024]{2,1,0:T(8,128)(2,1)}, u32[]{:S(2)}, u32[]{:S(2)}) %collective-permute-start.10) | collective-permute-done | bytes 2097184 | tf_op jit(solution)/shard_map/ppermute | solution.py:231
  229.8 26.3 %multiply.1 = (f32[2048,1024]{1,0:T(8,128)}, bf16[2,8,128,1024]{3,2,1,0:T(8,128)(2,1)}) custom-call(s32[2]{0:T(128)S(1)} %pad_add_fusion.ids, bf16[8,256,2048]{2,1,0:T(8,128)(2,1)} %all-to-all-done.near_a, bf16[8,128,2048]{2,1,0:T(8,128)(2,1)} %all-to-all-done.1.e_far, bf16[8,128,1024]{2,1,0:T(8,128)(2,1)} %collective-permute-done.5.o_near, ...), custom_call_target="tpu_custom_call" | custom-call | tf_op jit(solution)/shard_map/multiply/pallas_call | solution.py:278
  256.2 16.2 %collective-permute-done.11.right = bf16[4,256,1024]{2,1,0:T(8,128)(2,1)S(1)} collective-permute-done((bf16[4,256,1024]{2,1,0:T(8,128)(2,1)}, bf16[4,256,1024]{2,1,0:T(8,128)(2,1)S(1)}, u32[]{:S(2)}, u32[]{:S(2)}) %collective-permute-start.11) | collective-permute-done | bytes 2097184 | tf_op jit(solution)/shard_map/ppermute | solution.py:228
  272.4 3.4 %copy-done.1 = f32[2048,1024]{1,0:T(8,128)S(1)} copy-done((f32[2048,1024]{1,0:T(8,128)S(1)}, f32[2048,1024]{1,0:T(8,128)}, u32[]{:S(2)}) %copy-start.1) | copy-done | bytes 8388632
  275.7 2.2 copy-done.2
  277.9 8.2 %finish.1 = f32[2048,1024]{1,0:T(8,128)} custom-call(s32[32,16]{1,0:T(8,128)S(1)} %copy.9.filt, f32[2048,1024]{1,0:T(8,128)S(1)} %copy-done.1, bf16[2,8,128,1024]{3,2,1,0:T(8,128)(2,1)S(1)} %copy-done.2, bf16[4,256,1024]{2,1,0:T(8,128)(2,1)S(1)} %collective-permute-done.11.right), custom_call_target="tpu_custom_call" | custom-call | tf_op jit(solution)/shard_map/finish/pallas_call | solution.py:288
  (33 shorter events, 0.2 us)
Async XLA Ops:
  0.1 0.7 copy-start.4
  0.8 0.7 copy-start.5
  8.3 3.4 %copy-start = (bf16[8,256,2048]{2,1,0:T(8,128)(2,1)}, bf16[8,256,2048]{2,1,0:T(8,128)(2,1)S(1)}, u32[]{:S(2)}) copy-start(bf16[8,256,2048]{2,1,0:T(8,128)(2,1)S(1)} %get-tuple-element.21) | copy-start | bytes 25165828
  11.7 1.5 copy-start.7
  13.1 6.4 %copy-start.16 = (s32[64,16]{0,1:T(8,128)S(1)}, s32[64,16]{0,1:T(8,128)}, u32[]{:S(2)}) copy-start(s32[64,16]{0,1:T(8,128)} %param.9) | copy-start | bytes 12292
  13.1 6.5 %copy-start.6 = (s32[512]{0:T(512)S(1)}, s32[512]{0:T(512)}, u32[]{:S(2)}) copy-start(s32[512]{0:T(512)} %kdist.3) | copy-start | bytes 6148
  13.1 145.8 %all-to-all-start = ((bf16[8,256,2048]{2,1,0:T(8,128)(2,1)}), bf16[8,256,2048]{2,1,0:T(8,128)(2,1)}, u32[]{:S(2)}, u32[]{:S(2)}) async-start(bf16[8,256,2048]{2,1,0:T(8,128)(2,1)} %copy-done), calls=%async_computation | async-start | bytes 16777216 | tf_op jit(solution)/shard_map/all_to_all | solution.py:237
  19.6 23.0 %copy-start.8 = (bf16[5,128,2048]{2,1,0:T(8,128)(2,1)S(1)}, bf16[5,128,2048]{2,1,0:T(8,128)(2,1)}, u32[]{:S(2)}) copy-start(bf16[5,128,2048]{2,1,0:T(8,128)(2,1)} %copy-done.7) | copy-start | bytes 7864324
  40.8 101.4 %copy-start.3 = (bf16[4,256,1024]{2,1,0:T(8,128)(2,1)}, bf16[4,256,1024]{2,1,0:T(8,128)(2,1)S(1)}, u32[]{:S(2)}) copy-start(bf16[4,256,1024]{2,1,0:T(8,128)(2,1)S(1)} %get-tuple-element.22.r0) | copy-start | bytes 6291460
  40.8 103.0 %collective-permute-start.4 = (bf16[5,256,1024]{2,1,0:T(8,128)(2,1)S(1)}, bf16[5,256,1024]{2,1,0:T(8,128)(2,1)S(1)}, u32[]{:S(2)}, u32[]{:S(2)}) collective-permute-start(bf16[5,256,1024]{2,1,0:T(8,128)(2,1)S(1)} %get-tuple-element.27), channel_id=1, source_target_pairs={{0,4},{1,5},{2,6},{3,7},{4,0},{5,1},{6,2},{7,3},{8,12},{9,13},{10,... | collective-permute-start | bytes 7864328 | tf_op jit(solution)/shard_map/ppermute | solution.py:228
  42.6 116.3 %collective-permute-start.3 = (bf16[5,128,2048]{2,1,0:T(8,128)(2,1)S(1)}, bf16[5,128,2048]{2,1,0:T(8,128)(2,1)S(1)}, u32[]{:S(2)}, u32[]{:S(2)}) collective-permute-start(bf16[5,128,2048]{2,1,0:T(8,128)(2,1)S(1)} %copy-done.8), channel_id=1, source_target_pairs={{0,64},{8,72},{16,80},{24,88},{32,96},{40,104},{48,112},{56,120},{... | collective-permute-start | bytes 7864328 | tf_op jit(solution)/shard_map/ppermute | solution.py:225
  45.9 47.8 %collective-permute-start = (bf16[4,256,1024]{2,1,0:T(8,128)(2,1)S(1)}, bf16[4,256,1024]{2,1,0:T(8,128)(2,1)S(1)}, u32[]{:S(2)}, u32[]{:S(2)}) collective-permute-start(bf16[4,256,1024]{2,1,0:T(8,128)(2,1)S(1)} %get-tuple-element.23), channel_id=1, source_target_pairs={{0,1},{1,2},{2,3},{3,0},{4,5},{5,6},{6,7},{7,4},{8,9},{9,10},{10,1... | collective-permute-start | bytes 6291464 | tf_op jit(solution)/shard_map/ppermute | solution.py:234
  47.1 92.4 %collective-permute-start.1 = (bf16[4,256,1024]{2,1,0:T(8,128)(2,1)S(1)}, bf16[4,256,1024]{2,1,0:T(8,128)(2,1)S(1)}, u32[]{:S(2)}, u32[]{:S(2)}) collective-permute-start(bf16[4,256,1024]{2,1,0:T(8,128)(2,1)S(1)} %get-tuple-element.24), channel_id=1, source_target_pairs={{0,2},{1,3},{2,0},{3,1},{4,6},{5,7},{6,4},{7,5},{8,10},{9,11},{10,... | collective-permute-start | bytes 6291464 | tf_op jit(solution)/shard_map/ppermute | solution.py:234
  49.6 90.0 %collective-permute-start.2 = (bf16[4,256,1024]{2,1,0:T(8,128)(2,1)S(1)}, bf16[4,256,1024]{2,1,0:T(8,128)(2,1)S(1)}, u32[]{:S(2)}, u32[]{:S(2)}) collective-permute-start(bf16[4,256,1024]{2,1,0:T(8,128)(2,1)S(1)} %get-tuple-element.25), channel_id=1, source_target_pairs={{0,3},{1,0},{2,1},{3,2},{4,7},{5,4},{6,5},{7,6},{8,11},{9,8},{10,9... | collective-permute-start | bytes 6291464 | tf_op jit(solution)/shard_map/ppermute | solution.py:234
  93.7 45.9 %copy-start.10 = (bf16[4,256,1024]{2,1,0:T(8,128)(2,1)}, bf16[4,256,1024]{2,1,0:T(8,128)(2,1)S(1)}, u32[]{:S(2)}) copy-start(bf16[4,256,1024]{2,1,0:T(8,128)(2,1)S(1)} %collective-permute-done.r1) | copy-start | bytes 6291460
  139.5 1.3 copy-start.11
  140.8 1.4 copy-start.12
  143.8 1.5 copy-start.9
  163.8 60.8 %collective-permute-start.6 = (bf16[8,128,1024]{2,1,0:T(8,128)(2,1)}, bf16[8,128,1024]{2,1,0:T(8,128)(2,1)}, u32[]{:S(2)}, u32[]{:S(2)}) collective-permute-start(bf16[8,128,1024]{2,1,0:T(8,128)(2,1)} %get-tuple-element.37), channel_id=1, source_target_pairs={{0,64},{8,72},{16,80},{24,88},{32,96},{40,104},{48,112},{56,120},{... | collective-permute-start | bytes 6291464 | tf_op jit(solution)/shard_map/ppermute | solution.py:225
  167.0 59.1 %all-to-all-start.1 = ((bf16[8,128,2048]{2,1,0:T(8,128)(2,1)}), bf16[8,128,2048]{2,1,0:T(8,128)(2,1)}, u32[]{:S(2)}, u32[]{:S(2)}) async-start(bf16[8,128,2048]{2,1,0:T(8,128)(2,1)} %bitcast.7), calls=%async_computation.1 | async-start | bytes 8388608 | tf_op jit(solution)/shard_map/all_to_all | solution.py:237
  172.4 53.6 %copy-start.17 = (s32[32,16]{0,1:T(8,128)S(1)}, s32[32,16]{0,1:T(8,128)}, u32[]{:S(2)}) copy-start(s32[32,16]{0,1:T(8,128)} %param.10) | copy-start | bytes 6148
  175.3 25.9 %collective-permute-start.7 = (bf16[2,256,1024]{2,1,0:T(8,128)(2,1)S(1)}, bf16[2,256,1024]{2,1,0:T(8,128)(2,1)S(1)}, u32[]{:S(2)}, u32[]{:S(2)}) collective-permute-start(bf16[2,256,1024]{2,1,0:T(8,128)(2,1)S(1)} %get-tuple-element.42), channel_id=1, source_target_pairs={{0,1},{1,2},{2,3},{3,0},{4,5},{5,6},{6,7},{7,4},{8,9},{9,10},{10,1... | collective-permute-start | bytes 3145736 | tf_op jit(solution)/shard_map/ppermute | solution.py:234
  176.6 48.0 %collective-permute-start.8 = (bf16[2,256,1024]{2,1,0:T(8,128)(2,1)S(1)}, bf16[2,256,1024]{2,1,0:T(8,128)(2,1)S(1)}, u32[]{:S(2)}, u32[]{:S(2)}) collective-permute-start(bf16[2,256,1024]{2,1,0:T(8,128)(2,1)S(1)} %get-tuple-element.41), channel_id=1, source_target_pairs={{0,2},{1,3},{2,0},{3,1},{4,6},{5,7},{6,4},{7,5},{8,10},{9,11},{10,... | collective-permute-start | bytes 3145736 | tf_op jit(solution)/shard_map/ppermute | solution.py:234
  179.0 45.6 %collective-permute-start.9 = (bf16[2,256,1024]{2,1,0:T(8,128)(2,1)S(1)}, bf16[2,256,1024]{2,1,0:T(8,128)(2,1)S(1)}, u32[]{:S(2)}, u32[]{:S(2)}) collective-permute-start(bf16[2,256,1024]{2,1,0:T(8,128)(2,1)S(1)} %get-tuple-element.40), channel_id=1, source_target_pairs={{0,3},{1,0},{2,1},{3,2},{4,7},{5,4},{6,5},{7,6},{8,11},{9,8},{10,9... | collective-permute-start | bytes 3145736 | tf_op jit(solution)/shard_map/ppermute | solution.py:234
  180.2 45.9 %collective-permute-start.5 = (bf16[8,128,1024]{2,1,0:T(8,128)(2,1)}, bf16[8,128,1024]{2,1,0:T(8,128)(2,1)}, u32[]{:S(2)}, u32[]{:S(2)}) collective-permute-start(bf16[8,128,1024]{2,1,0:T(8,128)(2,1)} %get-tuple-element.38), channel_id=1, source_target_pairs={{0,8},{8,0},{16,24},{24,16},{32,40},{40,32},{48,56},{56,48},{64,72... | collective-permute-start | bytes 6291464 | tf_op jit(solution)/shard_map/ppermute | solution.py:231
  201.3 24.4 %copy-start.13 = (bf16[2,256,1024]{2,1,0:T(8,128)(2,1)}, bf16[2,256,1024]{2,1,0:T(8,128)(2,1)S(1)}, u32[]{:S(2)}) copy-start(bf16[2,256,1024]{2,1,0:T(8,128)(2,1)S(1)} %collective-permute-done.7.p1) | copy-start | bytes 3145732
  224.6 1.1 copy-start.14
  224.6 1.4 copy-start.15
  224.6 5.2 %collective-permute-start.10 = (bf16[8,128,1024]{2,1,0:T(8,128)(2,1)}, bf16[8,128,1024]{2,1,0:T(8,128)(2,1)}, u32[]{:S(2)}, u32[]{:S(2)}) collective-permute-start(bf16[8,128,1024]{2,1,0:T(8,128)(2,1)} %collective-permute-done.6.o_cross), channel_id=1, source_target_pairs={{0,8},{8,0},{16,24},{24,16},{32,40},{40,32},{48,56},{56,48},{64,72... | collective-permute-start | bytes 6291464 | tf_op jit(solution)/shard_map/ppermute | solution.py:231
  225.9 46.4 %collective-permute-start.11 = (bf16[4,256,1024]{2,1,0:T(8,128)(2,1)}, bf16[4,256,1024]{2,1,0:T(8,128)(2,1)S(1)}, u32[]{:S(2)}, u32[]{:S(2)}) collective-permute-start(bf16[4,256,1024]{2,1,0:T(8,128)(2,1)} %pad_maximum_fusion.1), channel_id=1, source_target_pairs={{0,4},{1,5},{2,6},{3,7},{4,0},{5,1},{6,2},{7,3},{8,12},{9,13},{10,... | collective-permute-start | bytes 6291464 | tf_op jit(solution)/shard_map/ppermute | solution.py:228
  272.4 3.4 %copy-start.1 = (f32[2048,1024]{1,0:T(8,128)S(1)}, f32[2048,1024]{1,0:T(8,128)}, u32[]{:S(2)}) copy-start(f32[2048,1024]{1,0:T(8,128)} %get-tuple-element.34.part) | copy-start | bytes 25165828
  275.7 2.2 copy-start.2

commit v3 on v2

--- a/solution.py
+++ b/solution.py
@@ -52,17 +52,16 @@
             odd = tile % 2 == 1
             even = tile % 2 == 0
             first = jnp.where(odd, tile // 2 % 4 * 2 + t, near)
-            first_row = jnp.where(odd, 128, 0) + slot
-            first_col = jnp.where(odd, jnp.where(tile // 8 == half, 0, W), t * W)
+            first_row = jnp.where(odd, jnp.where(tile // 8 == half, 256, 384), t * 128) + slot
 
             @pl.when(odd | (near < 8))
             def _():
-                dst = to_y.at[first, pl.ds(pl.multiple_of(first_row, BS), BS), pl.ds(pl.multiple_of(first_col, W), W)]
+                dst = to_y.at[first, pl.ds(pl.multiple_of(first_row, BS), BS), :]
                 pltpu.make_async_copy(src, dst, sems.at[0]).start()
 
             @pl.when(even & (near > 0) & (near <= 8))
             def _():
-                pltpu.make_async_copy(src, to_y.at[near - 1, inner, cols], sems.at[0]).start()
+                pltpu.make_async_copy(src, to_y.at[near - 1, pl.ds(pl.multiple_of(t * 128 + slot, BS), BS), :], sems.at[0]).start()
 
             @pl.when(even & (far <= 8))
             def _():
@@ -153,9 +152,9 @@
     sources = pl.ds(0, 8)
     a_near = pl.ds(pl.multiple_of(a_half * 8, 8), 8)
     a_far = pl.ds(pl.multiple_of(8 - a_half * 8, 8), 8)
-    fetch(near_a.at[sources, pl.ds(0, 128), group(core)], left_v.at[0, core, a_near])
-    fetch(near_a.at[sources, pl.ds(0, 128), group(1 - core)], left_v.at[1, 1 - core, a_near])
-    fetch(near_a.at[sources, pl.ds(128, 128), group(0)], left_v.at[1, core, a_near])
+    fetch(near_a.at[sources, pl.ds(pl.multiple_of(core * 128, 128), 128)], left_v.at[0, core, a_near])
+    fetch(near_a.at[sources, pl.ds(pl.multiple_of(128 - core * 128, 128), 128)], left_v.at[1, 1 - core, a_near])
+    fetch(near_a.at[sources, pl.ds(256, 128)], left_v.at[1, core, a_near])
     fetch(o_near, left_v.at[0, 1 - core, a_near])
     for hop, near in enumerate((r0, r1, r2, r3)):
         place = (here - hop + 4) % 4
@@ -212,7 +211,11 @@
 
 
 def bf16(*shape):
-    return jax.ShapeDtypeStruct(shape, jnp.bfloat16)
+    return pltpu.HBM(shape, jnp.bfloat16)
+
+
+def in_hbm(*values):
+    return [pltpu.with_memory_space_constraint(value, pltpu.HBM) for value in values]
 
 
 def on_device(at, bmat, mask_a, mask_b, filt, kdist):
@@ -238,9 +241,9 @@
 
     a_y, a_z = pl.pallas_call(
         prep_a,
-        out_shape=[bf16(8, 256, 2 * W), bf16(5, 128, 2 * W)],
+        out_shape=[bf16(8, 512, W), bf16(5, 128, 2 * W)],
         in_specs=[SMEM, SMEM, VMEM, HBM],
-        out_specs=[ANY] * 2,
+        out_specs=[HBM] * 2,
         scratch_shapes=[pltpu.VMEM((32, 2 * W), jnp.float32), pltpu.VMEM((2048, 2 * W), jnp.bfloat16),
                         pltpu.SemaphoreType.DMA((8,)), pltpu.SemaphoreType.DMA((2,))],
         compiler_params=pltpu.CompilerParams(vmem_limit_bytes=24 * MIB),
@@ -250,36 +253,42 @@
         prep_b,
         out_shape=[bf16(4, 256, W)] * 4 + [bf16(5, 256, W)],
         in_specs=[SMEM, SMEM, VMEM, HBM],
-        out_specs=[ANY] * 5,
+        out_specs=[HBM] * 5,
         scratch_shapes=[pltpu.VMEM((64, W), jnp.float32), pltpu.VMEM((4096, W), jnp.bfloat16),
                         pltpu.SemaphoreType.DMA((8,)), pltpu.SemaphoreType.DMA((5,))],
         compiler_params=pltpu.CompilerParams(vmem_limit_bytes=24 * MIB),
         name="prep_b",
     )(ids, kdist, mask_b, pltpu.with_memory_space_constraint(bmat, pltpu.HBM))
 
+    a_y, a_z, x0, x1, x2, x3, b_z = lax.optimization_barrier((a_y, a_z, x0, x1, x2, x3, b_z))
     a_cross = swap_z_hi(a_z)
     b_cross = swap_z_lo(b_z)
     near_a = along_y(a_y)
-    r1, r2, r3 = along_x(x1, 1), along_x(x2, 2), along_x(x3, 3)
-
-    o_cross = swap_z_hi(near_a[:, 128:, W:])
-    o_near = swap_core(near_a[:, 128:, :W])
-
+    r1, r3 = along_x(x1, 1), along_x(x3, 3)
+    x2, r1, r3 = lax.optimization_barrier((x2, r1, r3))
+    r2 = along_x(x2, 2)
+
+    o_send = near_a[:, 384:]
     q_send = jnp.concatenate([v[3:4] for v in (x0, r1, r2, r3)], axis=0)
-    q_send, a_cross, b_cross = lax.optimization_barrier((q_send, a_cross, b_cross))
+    a_cross, b_cross, near_a, o_send, q_send = lax.optimization_barrier((a_cross, b_cross, near_a, o_send, q_send))
+    o_cross = swap_z_hi(o_send)
+    o_near = swap_core(near_a[:, 256:384])
+
+    e_far = along_y(jnp.stack([a_cross[:4], a_cross[1:]], axis=1).reshape(8, 128, 2 * W))
+    far = [lax.dynamic_slice_in_dim(b_cross, (here + hop) % 4, 2, 0) for hop in range(4)]
+    p1, p3 = along_x(far[1], 1), along_x(far[3], 3)
+    p2_send, p1, p3 = lax.optimization_barrier((far[2], p1, p3))
+    p2 = along_x(p2_send, 2)
+
+    q_send, o_cross, p1, p3 = lax.optimization_barrier((q_send, o_cross, p1, p3))
     q = swap_z_lo(q_send)
-    far = [lax.dynamic_slice_in_dim(b_cross, (here + hop) % 4, 2, 0) for hop in range(4)]
-    p1, p2, p3 = along_x(far[1], 1), along_x(far[2], 2), along_x(far[3], 3)
-    e_far = along_y(jnp.stack([a_cross[:4], a_cross[1:]], axis=1).reshape(8, 128, 2 * W))
-
-    o_cross, p1, p2, p3 = lax.optimization_barrier((o_cross, p1, p2, p3))
     o_swap = swap_core(o_cross)
 
     part, left = pl.pallas_call(
         multiply,
         out_shape=[jax.ShapeDtypeStruct((2 * W, W), jnp.float32), bf16(2, 8, 128, W)],
         in_specs=[SMEM] + [ANY] * 13,
-        out_specs=[VMEM, ANY],
+        out_specs=[VMEM, HBM],
         scratch_shapes=[pltpu.VMEM((2, 2, 16, 128, W), jnp.bfloat16), pltpu.VMEM((3, 2048, W), jnp.bfloat16),
                         pltpu.SemaphoreType.DMA((20,)), pltpu.SemaphoreType.DMA((8,))],
         compiler_params=pltpu.CompilerParams(vmem_limit_bytes=52 * MIB),
@@ -296,7 +305,7 @@
         scratch_shapes=[pltpu.VMEM((32, W), jnp.float32)],
         compiler_params=pltpu.CompilerParams(vmem_limit_bytes=32 * MIB),
         name="finish",
-    )(filt, part, left, q)
+    )(filt, *in_hbm(part, left), q)
 
 
 def solution(mesh):

time: 287 us -> 258 us (0.90)
  waiting for transfers between devices: 166 us -> 152 us
  Pallas kernels: 62.5 us -> 53 us
  local copies, waits for them, and re-layouts: 27.1 us -> 19.1 us
    pallas_call x1, Pallas kernels: 21.2 us -> 7.24 us  [on_device(): pl.pallas_call(prep_b, out_shape=[bf16(4, 256, W)] * 4 + [bf16(5, 256, W)...]
    unnamed x38 -> x20, local copies, waits for them, and re-layouts: 16.4 us -> 2.84 us
    ppermute x2, waiting for transfers between devices: 13.6 us -> 4.84 us  [swap_z_hi(): return lax.ppermute(value, 'row', [(i, i ^ 8) for i in range(16)])]
    pallas_call x1, Pallas kernels: 8.15 us -> 12.1 us  [on_device(): pl.pallas_call(finish, grid=(8,), out_shape=jax.ShapeDtypeStruct((2 * W,...]
    ppermute x2, waiting for transfers between devices: 3.72 us -> 0.01 us  [swap_core(): return lax.ppermute(value, 'row', [(i, i ^ 1) for i in range(16)])]
    slice x1 -> x2, local copies, waits for them, and re-layouts: 4.83 us -> 6.3 us  [the longest x1 3.17 us: on_device(): o_near = swap_core(near_a[:, 256:384])]
  transfers between devices with their start and end apart: 14 -> 14, of which waited for: 7 -> 6; matrix products, arithmetic and copies ran while one was open for 3% -> 7% of each run, Pallas kernels for 17% -> 10%
where the time goes in v3:
time: 258 us; the launch traced here: 257 us
  waiting for transfers between devices  152 us (59%)
  Pallas kernels  53 us (21%)
  starting transfers between devices  31.4 us (12%)
  local copies, waits for them, and re-layouts  19.1 us (7%)
    ppermute x6, waiting for transfers between devices, along_x(): lax.ppermute(value, 'col', [(i, i // 4 * 4 + (i % 4 + hop) % 4) for i in...  130 us
    pallas_call x1, Pallas kernels, on_device(): pl.pallas_call(multiply, out_shape=[jax.ShapeDtypeStruct((2 * W, W), jnp....  26.2 us
    ppermute x2, waiting for transfers between devices, swap_z_lo(): return lax.ppermute(value, 'col', [(i, i ^ 4) for i in range(8)])  17 us
    all_to_all x2, starting transfers between devices, along_y(): lax.all_to_all(value, 'row', 0, 0, axis_index_groups=Y_GROUPS, tiled=True)  12.9 us
    pallas_call x1, Pallas kernels, on_device(): pl.pallas_call(finish, grid=(8,), out_shape=jax.ShapeDtypeStruct((2 * W,...  12.1 us
    ppermute x6, starting transfers between devices, along_x(): lax.ppermute(value, 'col', [(i, i // 4 * 4 + (i % 4 + hop) % 4) for i in...  9.17 us
    pallas_call x1, Pallas kernels, on_device(): pl.pallas_call(prep_a, out_shape=[bf16(8, 512, W), bf16(5, 128, 2 * W)],...  7.45 us
    pallas_call x1, Pallas kernels, on_device(): pl.pallas_call(prep_b, out_shape=[bf16(4, 256, W)] * 4 + [bf16(5, 256, W)...  7.24 us
  transfers between devices with their start and end apart: 14, of which 6 were waited for; matrix products, arithmetic and copies ran while one was open for 7% of the time, Pallas kernels for 10%

profile of v3, /device:TPU:1, one launch (start us, length us, event | category | flops | bytes accessed | tf_op | source)
XLA Modules:
  0.0 257.5 jit_solution(15854033493920749257)
XLA Ops:
  0.0 0.8 copy.7.mask
  0.8 0.1 pad_add_fusion.ids
  0.9 0.7 copy-done.1
  1.5 7.2 %prep_b.1 = (bf16[4,256,1024]{2,1,0:T(8,128)(2,1)}, bf16[4,256,1024]{2,1,0:T(8,128)(2,1)}, bf16[4,256,1024]{2,1,0:T(8,128)(2,1)}, bf16[4,256,1024]{2,1,0:T(8,128)(2,1)}, bf16[5,256,1024]{2,1,0:T(8,128)(2,1)}) custom-call(s32[2]{0:T(128)S(1)} %pad_add_fusion.ids, s32[512]{0:T(512)S(1)} %copy-done.1, s32[64,16]{1,0:T(8,128)S(1)} %copy.7.mask, ...), custom_call_target="tpu_custom_call" | custom-call | tf_op jit(solution)/shard_map/prep_b/pallas_call | solution.py:252
  8.8 0.0 copy-done
  8.8 7.4 %prep_a.1 = (bf16[8,512,1024]{2,1,0:T(8,128)(2,1)}, bf16[5,128,2048]{2,1,0:T(8,128)(2,1)}) custom-call(s32[2]{0:T(128)S(1)} %pad_add_fusion.ids, s32[512]{0:T(512)S(1)} %copy-done.1, s32[32,32]{1,0:T(8,128)S(1)} %copy-done, bf16[2048,2048]{1,0:T(8,128)(2,1)} %at.1), custom_call_target="tpu_custom_call" | custom-call | tf_op jit(solution)/shard_map/prep_a/pallas_call | solution.py:242
  16.3 6.4 %all-to-all-start = ((bf16[8,512,1024]{2,1,0:T(8,128)(2,1)}), bf16[8,512,1024]{2,1,0:T(8,128)(2,1)}, u32[]{:S(2)}, u32[]{:S(2)}) async-start(bf16[8,512,1024]{2,1,0:T(8,128)(2,1)} %get-tuple-element.45), calls=%async_computation | async-start | bytes 16777216 | tf_op jit(solution)/shard_map/all_to_all | solution.py:240
  22.6 1.3 collective-permute-start.2
  23.9 1.4 collective-permute-start.3
  25.3 3.7 %collective-permute-start = (bf16[5,128,2048]{2,1,0:T(8,128)(2,1)}, bf16[5,128,2048]{2,1,0:T(8,128)(2,1)}, u32[]{:S(2)}, u32[]{:S(2)}) collective-permute-start(bf16[5,128,2048]{2,1,0:T(8,128)(2,1)} %get-tuple-element.43), channel_id=1, source_target_pairs={{0,64},{8,72},{16,80},{24,88},{32,96},{40,104},{48,112},{56,120},{... | collective-permute-start | bytes 7864328 | tf_op jit(solution)/shard_map/ppermute | solution.py:228
  29.0 0.8 collective-permute-start.1
  29.7 41.4 %collective-permute-done.2.r1 = bf16[4,256,1024]{2,1,0:T(8,128)(2,1)S(1)} collective-permute-done((bf16[4,256,1024]{2,1,0:T(8,128)(2,1)}, bf16[4,256,1024]{2,1,0:T(8,128)(2,1)S(1)}, u32[]{:S(2)}, u32[]{:S(2)}) %collective-permute-start.2) | collective-permute-done | bytes 2097184 | tf_op jit(solution)/shard_map/ppermute | solution.py:237
  71.2 0.0 collective-permute-done.3.r3
  71.2 2.3 collective-permute-start.4
  73.5 1.1 slice.25
  74.6 0.0 copy-done.4
  74.6 44.6 %collective-permute-done.4.r2 = bf16[4,256,1024]{2,1,0:T(8,128)(2,1)S(1)} collective-permute-done((bf16[4,256,1024]{2,1,0:T(8,128)(2,1)}, bf16[4,256,1024]{2,1,0:T(8,128)(2,1)S(1)}, u32[]{:S(2)}, u32[]{:S(2)}) %collective-permute-start.4) | collective-permute-done | bytes 2097184 | tf_op jit(solution)/shard_map/ppermute | solution.py:237
  119.2 1.3 copy-done.5
  120.5 1.6 pad_maximum_fusion.1
  122.2 0.0 all-to-all-done.near_a
  122.2 3.1 %slice.32 = bf16[8,128,1024]{2,1,0:T(8,128)(2,1)} slice(bf16[8,512,1024]{2,1,0:T(8,128)(2,1)} %all-to-all-done.near_a), slice={[0:8], [384:512], [0:1024]} | slice | bytes 4194304 | tf_op jit(solution)/shard_map/slice | solution.py:271
  125.3 0.0 collective-permute-done
  125.3 17.0 %collective-permute-done.1 = bf16[5,256,1024]{2,1,0:T(8,128)(2,1)S(1)} collective-permute-done((bf16[5,256,1024]{2,1,0:T(8,128)(2,1)}, bf16[5,256,1024]{2,1,0:T(8,128)(2,1)S(1)}, u32[]{:S(2)}, u32[]{:S(2)}) %collective-permute-start.1) | collective-permute-done | bytes 2621472 | tf_op jit(solution)/shard_map/ppermute | solution.py:231
  142.3 0.9 collective-permute-start.6
  143.2 2.6 %slice_bitcast_fusion.1 = (bf16[4,1,128,2048]{3,2,0,1:T(8,128)(2,1)S(1)}, bf16[4,1,128,2048]{3,2,0,1:T(8,128)(2,1)S(1)}) fusion(bf16[5,128,2048]{2,1,0:T(8,128)(2,1)} %collective-permute-done), kind=kLoop, calls=%fused_computation.3 | loop fusion | bytes 8388608 | tf_op jit(solution)/shard_map/stack | solution.py:277
  145.8 0.0 copy-done.2
  145.8 0.4 pad_maximum_fusion
  146.2 2.3 copy.8
  148.5 6.5 %all-to-all-start.1 = ((bf16[8,128,2048]{2,1,0:T(8,128)(2,1)}), bf16[8,128,2048]{2,1,0:T(8,128)(2,1)}, u32[]{:S(2)}, u32[]{:S(2)}) async-start(bf16[8,128,2048]{2,1,0:T(8,128)(2,1)} %bitcast.7), calls=%async_computation.1 | async-start | bytes 8388608 | tf_op jit(solution)/shard_map/all_to_all | solution.py:240
  155.1 3.8 %constant_dynamic-slice_fusion = (bf16[2,256,1024]{2,1,0:T(8,128)(2,1)S(1)}, bf16[2,256,1024]{2,1,0:T(8,128)(2,1)S(1)}, bf16[2,256,1024]{2,1,0:T(8,128)(2,1)S(1)}, bf16[2,256,1024]{2,1,0:T(8,128)(2,1)}) fusion(bf16[5,256,1024]{2,1,0:T(8,128)(2,1)} %copy-done.2, s32[]{:T(128)S(6)} %select_n.43, s32[]{:T(128)S(6)} %select_n.41, s32[]{:T(128)S(6)} %select_n.39, ...), kind=kLoop, calls=%fused_computation.4 | loop fusion | bytes 8388624 | tf_op jit(solution)/shard_map/dynamic_slice | solution.py:278
  158.9 0.0 collective-permute-start.7
  158.9 2.7 %collective-permute-start.8 = (bf16[2,256,1024]{2,1,0:T(8,128)(2,1)S(1)}, bf16[2,256,1024]{2,1,0:T(8,128)(2,1)S(1)}, u32[]{:S(2)}, u32[]{:S(2)}) collective-permute-start(bf16[2,256,1024]{2,1,0:T(8,128)(2,1)S(1)} %get-tuple-element.68), channel_id=1, source_target_pairs={{0,3},{1,0},{2,1},{3,2},{4,7},{5,4},{6,5},{7,6},{8,11},{9,8},{10,9... | collective-permute-start | bytes 3145736 | tf_op jit(solution)/shard_map/ppermute | solution.py:237
  161.6 3.2 %slice.31 = bf16[8,128,1024]{2,1,0:T(8,128)(2,1)} slice(bf16[8,512,1024]{2,1,0:T(8,128)(2,1)} %all-to-all-done.near_a), slice={[0:8], [256:384], [0:1024]} | slice | bytes 4194304 | tf_op jit(solution)/shard_map/slice | solution.py:275
  164.7 0.8 collective-permute-start.5
  165.5 19.2 %collective-permute-done.7.p1 = bf16[2,256,1024]{2,1,0:T(8,128)(2,1)S(1)} collective-permute-done((bf16[2,256,1024]{2,1,0:T(8,128)(2,1)S(1)}, bf16[2,256,1024]{2,1,0:T(8,128)(2,1)S(1)}, u32[]{:S(2)}, u32[]{:S(2)}) %collective-permute-start.7) | collective-permute-done | bytes 1048608 | tf_op jit(solution)/shard_map/ppermute | solution.py:237
  184.8 0.0 collective-permute-done.8.p3
  184.8 4.8 %collective-permute-done.6.o_cross = bf16[8,128,1024]{2,1,0:T(8,128)(2,1)} collective-permute-done((bf16[8,128,1024]{2,1,0:T(8,128)(2,1)}, bf16[8,128,1024]{2,1,0:T(8,128)(2,1)}, u32[]{:S(2)}, u32[]{:S(2)}) %collective-permute-start.6) | collective-permute-done | bytes 2097184 | tf_op jit(solution)/shard_map/ppermute | solution.py:228
  189.6 2.6 collective-permute-start.9
  192.2 0.7 collective-permute-start.11
  192.9 1.6 collective-permute-start.10
  194.4 0.1 copy.9.filt
  194.5 24.7 %collective-permute-done.10.p2 = bf16[2,256,1024]{2,1,0:T(8,128)(2,1)} collective-permute-done((bf16[2,256,1024]{2,1,0:T(8,128)(2,1)}, bf16[2,256,1024]{2,1,0:T(8,128)(2,1)}, u32[]{:S(2)}, u32[]{:S(2)}) %collective-permute-start.10) | collective-permute-done | bytes 1048608 | tf_op jit(solution)/shard_map/ppermute | solution.py:237
  219.2 0.0 collective-permute-done.5.o_near
  219.2 0.0 all-to-all-done.1.e_far
  219.2 0.0 collective-permute-done.9.o_swap
  219.2 26.2 %multiply.1 = (f32[2048,1024]{1,0:T(8,128)}, bf16[2,8,128,1024]{3,2,1,0:T(8,128)(2,1)}) custom-call(s32[2]{0:T(128)S(1)} %pad_add_fusion.ids, bf16[8,512,1024]{2,1,0:T(8,128)(2,1)} %all-to-all-done.near_a, bf16[8,128,2048]{2,1,0:T(8,128)(2,1)} %all-to-all-done.1.e_far, bf16[8,128,1024]{2,1,0:T(8,128)(2,1)} %collective-permute-done.5.o_near, ...), custom_call_target="tpu_custom_call" | custom-call | tf_op jit(solution)/shard_map/multiply/pallas_call | solution.py:287
  245.4 0.0 collective-permute-done.11.right
  245.4 12.1 %finish.1 = f32[2048,1024]{1,0:T(8,128)} custom-call(s32[32,16]{1,0:T(8,128)S(1)} %copy.9.filt, f32[2048,1024]{1,0:T(8,128)} %get-tuple-element.64.part, bf16[2,8,128,1024]{3,2,1,0:T(8,128)(2,1)} %get-tuple-element.65.left, bf16[4,256,1024]{2,1,0:T(8,128)(2,1)S(1)} %collective-permute-done.11.right), custom_call_target="tpu_custom_call" | custom-call | tf_op jit(solution)/shard_map/finish/pallas_call | solution.py:297
  (16 shorter events, 0.1 us)
Async XLA Ops:
  0.9 0.7 copy-start.1
  1.5 7.3 %copy-start = (s32[32,32]{1,0:T(8,128)S(1)}, s32[32,32]{1,0:T(8,128)}, u32[]{:S(2)}) copy-start(s32[32,32]{1,0:T(8,128)} %mask.2) | copy-start | bytes 12292
  16.3 105.9 %all-to-all-start = ((bf16[8,512,1024]{2,1,0:T(8,128)(2,1)}), bf16[8,512,1024]{2,1,0:T(8,128)(2,1)}, u32[]{:S(2)}, u32[]{:S(2)}) async-start(bf16[8,512,1024]{2,1,0:T(8,128)(2,1)} %get-tuple-element.45), calls=%async_computation | async-start | bytes 16777216 | tf_op jit(solution)/shard_map/all_to_all | solution.py:240
  22.6 48.6 %collective-permute-start.2 = (bf16[4,256,1024]{2,1,0:T(8,128)(2,1)}, bf16[4,256,1024]{2,1,0:T(8,128)(2,1)S(1)}, u32[]{:S(2)}, u32[]{:S(2)}) collective-permute-start(bf16[4,256,1024]{2,1,0:T(8,128)(2,1)} %get-tuple-element.48), channel_id=1, source_target_pairs={{0,1},{1,2},{2,3},{3,0},{4,5},{5,6},{6,7},{7,4},{8,9},{9,10},{10,1... | collective-permute-start | bytes 6291464 | tf_op jit(solution)/shard_map/ppermute | solution.py:237
  23.9 47.3 %collective-permute-start.3 = (bf16[4,256,1024]{2,1,0:T(8,128)(2,1)}, bf16[4,256,1024]{2,1,0:T(8,128)(2,1)S(1)}, u32[]{:S(2)}, u32[]{:S(2)}) collective-permute-start(bf16[4,256,1024]{2,1,0:T(8,128)(2,1)} %get-tuple-element.49), channel_id=1, source_target_pairs={{0,3},{1,0},{2,1},{3,2},{4,7},{5,4},{6,5},{7,6},{8,11},{9,8},{10,9... | collective-permute-start | bytes 6291464 | tf_op jit(solution)/shard_map/ppermute | solution.py:237
  25.3 100.0 %collective-permute-start = (bf16[5,128,2048]{2,1,0:T(8,128)(2,1)}, bf16[5,128,2048]{2,1,0:T(8,128)(2,1)}, u32[]{:S(2)}, u32[]{:S(2)}) collective-permute-start(bf16[5,128,2048]{2,1,0:T(8,128)(2,1)} %get-tuple-element.43), channel_id=1, source_target_pairs={{0,64},{8,72},{16,80},{24,88},{32,96},{40,104},{48,112},{56,120},{... | collective-permute-start | bytes 7864328 | tf_op jit(solution)/shard_map/ppermute | solution.py:228
  29.0 113.3 %collective-permute-start.1 = (bf16[5,256,1024]{2,1,0:T(8,128)(2,1)}, bf16[5,256,1024]{2,1,0:T(8,128)(2,1)S(1)}, u32[]{:S(2)}, u32[]{:S(2)}) collective-permute-start(bf16[5,256,1024]{2,1,0:T(8,128)(2,1)} %get-tuple-element.44), channel_id=1, source_target_pairs={{0,4},{1,5},{2,6},{3,7},{4,0},{5,1},{6,2},{7,3},{8,12},{9,13},{10,... | collective-permute-start | bytes 7864328 | tf_op jit(solution)/shard_map/ppermute | solution.py:231
  71.2 3.4 %copy-start.3 = (bf16[4,256,1024]{2,1,0:T(8,128)(2,1)}, bf16[4,256,1024]{2,1,0:T(8,128)(2,1)S(1)}, u32[]{:S(2)}) copy-start(bf16[4,256,1024]{2,1,0:T(8,128)(2,1)S(1)} %collective-permute-done.2.r1) | copy-start | bytes 6291460
  71.2 3.4 %copy-start.4 = (bf16[4,256,1024]{2,1,0:T(8,128)(2,1)}, bf16[4,256,1024]{2,1,0:T(8,128)(2,1)S(1)}, u32[]{:S(2)}) copy-start(bf16[4,256,1024]{2,1,0:T(8,128)(2,1)S(1)} %collective-permute-done.3.r3) | copy-start | bytes 6291460
  71.2 48.0 %collective-permute-start.4 = (bf16[4,256,1024]{2,1,0:T(8,128)(2,1)}, bf16[4,256,1024]{2,1,0:T(8,128)(2,1)S(1)}, u32[]{:S(2)}, u32[]{:S(2)}) collective-permute-start(bf16[4,256,1024]{2,1,0:T(8,128)(2,1)} %get-tuple-element.51), channel_id=1, source_target_pairs={{0,2},{1,3},{2,0},{3,1},{4,6},{5,7},{6,4},{7,5},{8,10},{9,11},{10,... | collective-permute-start | bytes 6291464 | tf_op jit(solution)/shard_map/ppermute | solution.py:237
  119.2 1.3 copy-start.5
  142.3 3.5 %copy-start.2 = (bf16[5,256,1024]{2,1,0:T(8,128)(2,1)}, bf16[5,256,1024]{2,1,0:T(8,128)(2,1)S(1)}, u32[]{:S(2)}) copy-start(bf16[5,256,1024]{2,1,0:T(8,128)(2,1)S(1)} %collective-permute-done.1) | copy-start | bytes 7864324
  142.3 47.3 %collective-permute-start.6 = (bf16[8,128,1024]{2,1,0:T(8,128)(2,1)}, bf16[8,128,1024]{2,1,0:T(8,128)(2,1)}, u32[]{:S(2)}, u32[]{:S(2)}) collective-permute-start(bf16[8,128,1024]{2,1,0:T(8,128)(2,1)} %slice.32), channel_id=1, source_target_pairs={{0,64},{8,72},{16,80},{24,88},{32,96},{40,104},{48,112},{56,120},{... | collective-permute-start | bytes 6291464 | tf_op jit(solution)/shard_map/ppermute | solution.py:228
  148.5 70.6 %all-to-all-start.1 = ((bf16[8,128,2048]{2,1,0:T(8,128)(2,1)}), bf16[8,128,2048]{2,1,0:T(8,128)(2,1)}, u32[]{:S(2)}, u32[]{:S(2)}) async-start(bf16[8,128,2048]{2,1,0:T(8,128)(2,1)} %bitcast.7), calls=%async_computation.1 | async-start | bytes 8388608 | tf_op jit(solution)/shard_map/all_to_all | solution.py:240
  158.9 25.9 %collective-permute-start.7 = (bf16[2,256,1024]{2,1,0:T(8,128)(2,1)S(1)}, bf16[2,256,1024]{2,1,0:T(8,128)(2,1)S(1)}, u32[]{:S(2)}, u32[]{:S(2)}) collective-permute-start(bf16[2,256,1024]{2,1,0:T(8,128)(2,1)S(1)} %get-tuple-element.69), channel_id=1, source_target_pairs={{0,1},{1,2},{2,3},{3,0},{4,5},{5,6},{6,7},{7,4},{8,9},{9,10},{10,1... | collective-permute-start | bytes 3145736 | tf_op jit(solution)/shard_map/ppermute | solution.py:237
  158.9 35.5 %copy-start.8 = (s32[32,16]{0,1:T(8,128)S(1)}, s32[32,16]{0,1:T(8,128)}, u32[]{:S(2)}) copy-start(s32[32,16]{0,1:T(8,128)} %param.10) | copy-start | bytes 6148
  158.9 25.8 %collective-permute-start.8 = (bf16[2,256,1024]{2,1,0:T(8,128)(2,1)S(1)}, bf16[2,256,1024]{2,1,0:T(8,128)(2,1)S(1)}, u32[]{:S(2)}, u32[]{:S(2)}) collective-permute-start(bf16[2,256,1024]{2,1,0:T(8,128)(2,1)S(1)} %get-tuple-element.68), channel_id=1, source_target_pairs={{0,3},{1,0},{2,1},{3,2},{4,7},{5,4},{6,5},{7,6},{8,11},{9,8},{10,9... | collective-permute-start | bytes 3145736 | tf_op jit(solution)/shard_map/ppermute | solution.py:237
  164.7 54.4 %collective-permute-start.5 = (bf16[8,128,1024]{2,1,0:T(8,128)(2,1)}, bf16[8,128,1024]{2,1,0:T(8,128)(2,1)}, u32[]{:S(2)}, u32[]{:S(2)}) collective-permute-start(bf16[8,128,1024]{2,1,0:T(8,128)(2,1)} %slice.31), channel_id=1, source_target_pairs={{0,8},{8,0},{16,24},{24,16},{32,40},{40,32},{48,56},{56,48},{64,72... | collective-permute-start | bytes 6291464 | tf_op jit(solution)/shard_map/ppermute | solution.py:234
  184.8 8.1 %copy-start.6 = (bf16[2,256,1024]{2,1,0:T(8,128)(2,1)}, bf16[2,256,1024]{2,1,0:T(8,128)(2,1)S(1)}, u32[]{:S(2)}) copy-start(bf16[2,256,1024]{2,1,0:T(8,128)(2,1)S(1)} %collective-permute-done.7.p1) | copy-start | bytes 3145732
  184.8 8.1 %copy-start.7 = (bf16[2,256,1024]{2,1,0:T(8,128)(2,1)}, bf16[2,256,1024]{2,1,0:T(8,128)(2,1)S(1)}, u32[]{:S(2)}) copy-start(bf16[2,256,1024]{2,1,0:T(8,128)(2,1)S(1)} %collective-permute-done.8.p3) | copy-start | bytes 3145732
  189.6 29.6 %collective-permute-start.9 = (bf16[8,128,1024]{2,1,0:T(8,128)(2,1)}, bf16[8,128,1024]{2,1,0:T(8,128)(2,1)}, u32[]{:S(2)}, u32[]{:S(2)}) collective-permute-start(bf16[8,128,1024]{2,1,0:T(8,128)(2,1)} %collective-permute-done.6.o_cross), channel_id=1, source_target_pairs={{0,8},{8,0},{16,24},{24,16},{32,40},{40,32},{48,56},{56,48},{64,72... | collective-permute-start | bytes 6291464 | tf_op jit(solution)/shard_map/ppermute | solution.py:234
  192.2 53.3 %collective-permute-start.11 = (bf16[4,256,1024]{2,1,0:T(8,128)(2,1)}, bf16[4,256,1024]{2,1,0:T(8,128)(2,1)S(1)}, u32[]{:S(2)}, u32[]{:S(2)}) collective-permute-start(bf16[4,256,1024]{2,1,0:T(8,128)(2,1)} %pad_maximum_fusion.1), channel_id=1, source_target_pairs={{0,4},{1,5},{2,6},{3,7},{4,0},{5,1},{6,2},{7,3},{8,12},{9,13},{10,... | collective-permute-start | bytes 6291464 | tf_op jit(solution)/shard_map/ppermute | solution.py:231
  192.9 26.3 %collective-permute-start.10 = (bf16[2,256,1024]{2,1,0:T(8,128)(2,1)}, bf16[2,256,1024]{2,1,0:T(8,128)(2,1)}, u32[]{:S(2)}, u32[]{:S(2)}) collective-permute-start(bf16[2,256,1024]{2,1,0:T(8,128)(2,1)} %get-tuple-element.62), channel_id=1, source_target_pairs={{0,2},{1,3},{2,0},{3,1},{4,6},{5,7},{6,4},{7,5},{8,10},{9,11},{10,... | collective-permute-start | bytes 3145736 | tf_op jit(solution)/shard_map/ppermute | solution.py:237

commit v4 on v3

v4 whole, which is shorter than its diff:
```python
import jax
import jax.numpy as jnp
from jax import lax
from jax.experimental import pallas as pl
from jax.experimental.pallas import tpu as pltpu
from jax.sharding import PartitionSpec as P

BS = 64
KB = 32
NP = 16
W = 1024
MIB = 1 << 20
Y_GROUPS = [list(range(8)), list(range(8, 16))]


def spread(mask, width):
    count = mask.shape[0]
    lane = lax.broadcasted_iota(jnp.int32, (count, width), 1) // BS
    entry = lax.broadcasted_iota(jnp.int32, (count, width), 0)
    chosen = jnp.where(lane == entry, 1.0, 0.0).astype(jnp.bfloat16)
    return product(mask.astype(jnp.float32).astype(jnp.bfloat16), chosen)


def load(src, dst, chunk, sem):
    rows = pl.ds(chunk * (src.shape[0] // 8), src.shape[0] // 8)
    return pltpu.make_async_copy(src.at[rows], dst.at[rows], sem)


def prep(ids, kdist, mask_a, at, mask_b, bmat, to_y, a_z, x0, x1, x2, x3, b_z,
         wide_a, held_a, wide_b, held_b, in_sems, sems):
    row_id, col_id = ids[0], ids[1]
    a_half = row_id // 8
    b_half, here = col_id // 4, col_id % 4
    to_x = (x0, x1, x2, x3)
    for n in range(8):
        load(bmat, held_b, n, in_sems.at[8 + n]).start()
    for n in range(8):
        load(at, held_a, n, in_sems.at[n]).start()
    wide_b[...] = spread(mask_b[...], W)
    wide_a[...] = spread(mask_a[...].T, 2 * W)

    for block in range(2 * KB):
        if block % 8 == 0:
            load(bmat, held_b, block // 8, in_sems.at[8 + block // 8]).wait()
        gain = wide_b[block:block + 1, :].astype(jnp.bfloat16)
        rows = pl.ds(block * BS, BS)
        held_b[rows, :] = held_b[rows, :] * gain
        pos = kdist[col_id * 2 * KB + block]
        inner = pl.ds(pl.multiple_of((pos % KB - 4 * col_id) * BS, BS), BS)
        tile = (pos // KB - row_id + NP) % NP
        src = held_b.at[rows, :]
        near = (tile - 8 * b_half + NP) % NP
        far = (near + 8) % NP
        odd = tile % 2 == 1
        even = tile % 2 == 0
        first = (jnp.where(odd, tile, near) // 2 - here + 8) % 4
        kind = jnp.where(odd, jnp.where(tile // 8 == b_half, 1, 3), 0)
        second = (near // 2 - 1 - here + 8) % 4

        def send(hop, kind):
            def to(n):
                def run():
                    pltpu.make_async_copy(src, to_x[n].at[kind, inner, :], sems.at[2 + n]).start()

                return run

            lax.cond(hop < 2, lambda: lax.cond(hop == 0, to(0), to(1)), lambda: lax.cond(hop == 2, to(2), to(3)))

        @pl.when(odd | (near < 8))
        def _():
            send(first, kind)

        @pl.when(even & (near > 0) & (near <= 8))
        def _():
            send(second, 2)

        @pl.when(even & (far <= 8))
        def _():
            pltpu.make_async_copy(src, b_z.at[far // 2, inner, :], sems.at[6]).start()

    for block in range(KB):
        if block % 4 == 0:
            load(at, held_a, block // 4, in_sems.at[block // 4]).wait()
        gain = wide_a[block:block + 1, :].astype(jnp.bfloat16)
        rows = pl.ds(block * BS, BS)
        held_a[rows, :] = held_a[rows, :] * gain
        pos = kdist[row_id * KB + block]
        slot = (pos % KB - 2 * row_id) * BS
        inner = pl.ds(pl.multiple_of(slot, BS), BS)
        for t in range(2):
            tile = (pos // KB - 2 * col_id - t + 2 * NP) % NP
            cols = pl.ds(t * W, W)
            src = held_a.at[rows, cols]
            near = (tile - 8 * a_half + NP) % NP
            far = (near + 8) % NP
            odd = tile % 2 == 1
            even = tile % 2 == 0
            first = jnp.where(odd, tile // 2 % 4 * 2 + t, near)
            first_row = jnp.where(odd, jnp.where(tile // 8 == a_half, 256, 384), t * 128) + slot

            @pl.when(odd | (near < 8))
            def _():
                dst = to_y.at[first, pl.ds(pl.multiple_of(first_row, BS), BS), :]
                pltpu.make_async_copy(src, dst, sems.at[0]).start()

            @pl.when(even & (near > 0) & (near <= 8))
            def _():
                dst = to_y.at[near - 1, pl.ds(pl.multiple_of(t * 128 + slot, BS), BS), :]
                pltpu.make_async_copy(src, dst, sems.at[0]).start()

            @pl.when(even & (far <= 8))
            def _():
                pltpu.make_async_copy(src, a_z.at[far // 2, inner, cols], sems.at[1]).start()

    for n, ref in enumerate((to_y, a_z, x0, x1, x2, x3, b_z)):
        pltpu.make_async_copy(ref, ref, sems.at[n]).wait()


CONTRACT = (((0,), (0,)), ((), ()))


def product(left, right):
    return lax.dot_general(left, right, CONTRACT, preferred_element_type=jnp.float32)


def multiply(ids, near_a, e_far, o_near, o_cross, o_swap, r0, r1, r2, r3, p0, p1, p2, p3,
             out, left_out, left_v, b_v, sems, out_sem):
    row_id, col_id = ids[0], ids[1]
    core = row_id % 2
    a_half = row_id // 8
    b_half, here = col_id // 4, col_id % 4
    copies = []

    def fetch(src, dst):
        copy = pltpu.make_async_copy(src, dst, sems.at[len(copies)])
        copy.start()
        copies.append(copy)

    def group(which):
        return pl.ds(pl.multiple_of(which * W, W), W)

    sources = pl.ds(0, 8)
    a_near = pl.ds(pl.multiple_of(a_half * 8, 8), 8)
    a_far = pl.ds(pl.multiple_of(8 - a_half * 8, 8), 8)
    fetch(near_a.at[sources, pl.ds(pl.multiple_of(core * 128, 128), 128)], left_v.at[0, core, a_near])
    fetch(near_a.at[sources, pl.ds(pl.multiple_of(128 - core * 128, 128), 128)], left_v.at[1, 1 - core, a_near])
    fetch(near_a.at[sources, pl.ds(256, 128)], left_v.at[1, core, a_near])
    fetch(o_near, left_v.at[0, 1 - core, a_near])
    for hop, near in enumerate((r0, r1, r2, r3)):
        place = (here - hop + 4) % 4
        fetch(near.at[pl.ds(0, 3)], b_v.at[:, pl.ds(pl.multiple_of((b_half * 4 + place) * 256, 256), 256)])
    for hop, far in enumerate((p0, p1, p2, p3)):
        place = (here - hop + 4) % 4
        rows = pl.ds(pl.multiple_of(((1 - b_half) * 4 + place) * 256, 256), 256)
        base = here if hop == 0 else 0
        fetch(far.at[base], b_v.at[0, rows])
        fetch(far.at[base + 1], b_v.at[2, rows])
    fetch(e_far.at[sources, :, group(core)], left_v.at[0, core, a_far])
    fetch(e_far.at[sources, :, group(1 - core)], left_v.at[1, 1 - core, a_far])
    fetch(o_cross, left_v.at[1, core, a_far])
    fetch(o_swap, left_v.at[0, 1 - core, a_far])
    for copy in copies:
        copy.wait()
    later = []
    for t in range(2):
        for hop in range(4):
            place = (here - hop + 4) % 4
            part = pltpu.make_async_copy(
                left_v.at[1, t, pl.ds((1 - b_half) * 8 + place * 2, 2)],
                left_out.at[t, pl.ds(hop * 2, 2)], out_sem.at[t * 4 + hop])
            part.start()
            later.append(part)
    near_rows = pl.ds(pl.multiple_of(b_half * W, W), W)
    near_pieces = pl.ds(pl.multiple_of(b_half * 8, 8), 8)
    for t in range(2):
        for m in range(4):
            cols = slice(m * 256, (m + 1) * 256)
            total = product(left_v[0, t, :, :, cols].reshape(2 * W, 256), b_v[2 * t])
            total += product(left_v[1, t, near_pieces, :, cols].reshape(W, 256), b_v[1, near_rows])
            out[t * W + m * 256:t * W + (m + 1) * 256, :] = total
    for part in later:
        part.wait()


def finish(filt, part, left, right, out, wide, done, sems):
    wide[...] = spread(filt[...], W)
    copies = []
    for t in range(2):
        for m in range(4):
            first = t * W + m * 256
            if len(copies) >= 2:
                copies[-2].wait()
            spot = done.at[len(copies) % 2]
            total = product(left[t, :, :, m * 256:(m + 1) * 256].reshape(W, 256), right[...].reshape(W, W))
            total += part[first:first + 256, :]
            for i in range(4):
                rows = slice(i * BS, (i + 1) * BS)
                block = first // BS + i
                spot[rows, :] = total[rows, :] * wide[block:block + 1, :]
            copies.append(pltpu.make_async_copy(spot, out.at[pl.ds(first, 256)], sems.at[len(copies) % 2]))
            copies[-1].start()
    for copy in copies[-2:]:
        copy.wait()


SMEM = pl.BlockSpec(memory_space=pltpu.SMEM)
ANY = pl.BlockSpec(memory_space=pl.ANY)
HBM = pl.BlockSpec(memory_space=pltpu.HBM)
VMEM = pl.BlockSpec(memory_space=pltpu.VMEM)


def bf16(*shape):
    return pltpu.HBM(shape, jnp.bfloat16)


def in_hbm(*values):
    return [pltpu.with_memory_space_constraint(value, pltpu.HBM) for value in values]


def in_vmem(*values):
    return [pltpu.with_memory_space_constraint(value, pltpu.VMEM) for value in values]


def on_device(at, bmat, mask_a, mask_b, filt, kdist):
    row_id = lax.axis_index("row")
    col_id = lax.axis_index("col")
    ids = jnp.stack([row_id, col_id]).astype(jnp.int32)
    here = col_id % 4

    def swap_z_hi(value):
        return lax.ppermute(value, "row", [(i, i ^ 8) for i in range(16)])

    def swap_z_lo(value):
        return lax.ppermute(value, "col", [(i, i ^ 4) for i in range(8)])

    def swap_core(value):
        return lax.ppermute(value, "row", [(i, i ^ 1) for i in range(16)])

    def along_x(value, hop):
        return lax.ppermute(value, "col", [(i, i // 4 * 4 + (i % 4 + hop) % 4) for i in range(8)])

    def along_y(value):
        return lax.all_to_all(value, "row", 0, 0, axis_index_groups=Y_GROUPS, tiled=True)

    a_y, a_z, x0, x1, x2, x3, b_z = pl.pallas_call(
        prep,
        out_shape=[bf16(8, 512, W), bf16(5, 128, 2 * W)] + [bf16(4, 256, W)] * 4 + [bf16(5, 256, W)],
        in_specs=[SMEM, SMEM, VMEM, HBM, VMEM, HBM],
        out_specs=[HBM] * 7,
        scratch_shapes=[pltpu.VMEM((32, 2 * W), jnp.float32), pltpu.VMEM((2048, 2 * W), jnp.bfloat16),
                        pltpu.VMEM((64, W), jnp.float32), pltpu.VMEM((4096, W), jnp.bfloat16),
                        pltpu.SemaphoreType.DMA((16,)), pltpu.SemaphoreType.DMA((7,))],
        compiler_params=pltpu.CompilerParams(vmem_limit_bytes=32 * MIB),
        name="prep",
    )(ids, kdist, mask_a, *in_hbm(at), mask_b.T, *in_hbm(bmat))

    b_cross = swap_z_lo(b_z)
    r1, r3 = along_x(x1, 1), along_x(x3, 3)
    x2, r1, r3 = lax.optimization_barrier((x2, r1, r3))
    r2 = along_x(x2, 2)
    a_cross = swap_z_hi(a_z)
    near_a = along_y(a_y)

    o_send = near_a[:, 384:]
    q_send = jnp.concatenate([v[3:4] for v in (x0, r1, r2, r3)], axis=0)
    a_cross, b_cross, near_a, o_send, q_send = lax.optimization_barrier((a_cross, b_cross, near_a, o_send, q_send))
    o_cross = swap_z_hi(o_send)
    o_near = swap_core(near_a[:, 256:384])

    far = [lax.dynamic_slice_in_dim(b_cross, (here + hop) % 4, 2, 0) for hop in range(1, 4)]
    a_cross, *far = lax.optimization_barrier((a_cross, *far))
    p1, p2, p3 = along_x(far[0], 1), along_x(far[1], 2), along_x(far[2], 3)
    e_far = along_y(jnp.stack([a_cross[:4], a_cross[1:]], axis=1).reshape(8, 128, 2 * W))

    q_send, o_cross, p1, p2, p3 = lax.optimization_barrier((q_send, o_cross, p1, p2, p3))
    q = swap_z_lo(q_send)
    o_swap = swap_core(o_cross)

    part, left = pl.pallas_call(
        multiply,
        out_shape=[pltpu.VMEM((2 * W, W), jnp.float32), pltpu.VMEM((2, 8, 128, W), jnp.bfloat16)],
        in_specs=[SMEM] + [ANY] * 13,
        out_specs=[VMEM, VMEM],
        scratch_shapes=[pltpu.VMEM((2, 2, 16, 128, W), jnp.bfloat16), pltpu.VMEM((3, 2048, W), jnp.bfloat16),
                        pltpu.SemaphoreType.DMA((20,)), pltpu.SemaphoreType.DMA((8,))],
        compiler_params=pltpu.CompilerParams(vmem_limit_bytes=38 * MIB),
        name="multiply",
    )(ids, *in_hbm(near_a, e_far, o_near, o_cross, o_swap, x0, r1, r2, r3, b_cross, p1, p2, p3))
    return pl.pallas_call(
        finish,
        out_shape=jax.ShapeDtypeStruct((2 * W, W), jnp.float32),
        in_specs=[VMEM] * 4,
        out_specs=HBM,
        scratch_shapes=[pltpu.VMEM((32, W), jnp.float32), pltpu.VMEM((2, 256, W), jnp.float32),
                        pltpu.SemaphoreType.DMA((2,))],
        compiler_params=pltpu.CompilerParams(vmem_limit_bytes=8 * MIB),
        name="finish",
    )(filt.T, *in_vmem(part, left, q))


def solution(mesh):
    in_specs = (
        P("row", "col"),
        P("col", "row"),
        P("row", "col"),
        P("col", "row"),
        P("col", "row"),
        P(),
    )
    out_specs = P("col", "row")
    return jax.shard_map(
        on_device, mesh=mesh, in_specs=in_specs, out_specs=out_specs, check_vma=False
    )
```

time: 258 us -> 263 us (1.019)
  waiting for transfers between devices: 152 us -> 168 us
  Pallas kernels: 53 us -> 45 us
    ppermute x2, waiting for transfers between devices: 17 us -> 36.7 us  [swap_z_lo(): return lax.ppermute(value, 'col', [(i, i ^ 4) for i in range(8)])]
    pallas_call x4 -> x3, Pallas kernels: 53 us -> 45 us  [the longest x1 23.2 us: on_device(): pl.pallas_call(multiply, out_shape=[pltpu.VMEM((2 * W, W), jnp.float32),...]
    ppermute x2, waiting for transfers between devices: 4.84 us -> 0.01 us  [swap_z_hi(): return lax.ppermute(value, 'row', [(i, i ^ 8) for i in range(16)])]
    ppermute x2, waiting for transfers between devices: 0.01 us -> 4.11 us  [swap_core(): return lax.ppermute(value, 'row', [(i, i ^ 1) for i in range(16)])]
    slice x4, local copies, waits for them, and re-layouts: 1.18 us -> 4.31 us  [on_device(): q_send = jnp.concatenate([v[3:4] for v in (x0, r1, r2, r3)], axis=0)]
  transfers between devices with their start and end apart: 14 -> 14, of which waited for: 6 -> 8; matrix products, arithmetic and copies ran while one was open for 7% -> 7% of each run, Pallas kernels for 10% -> 9%
where the time goes in v4:
time: 263 us
  waiting for transfers between devices  168 us (64%)
  Pallas kernels  45 us (17%)
  starting transfers between devices  29.2 us (11%)
  local copies, waits for them, and re-layouts  18.2 us (7%)
    ppermute x6, waiting for transfers between devices, along_x(): lax.ppermute(value, 'col', [(i, i // 4 * 4 + (i % 4 + hop) % 4) for i in...  127 us
    ppermute x2, waiting for transfers between devices, swap_z_lo(): return lax.ppermute(value, 'col', [(i, i ^ 4) for i in range(8)])  36.7 us
    pallas_call x1, Pallas kernels, on_device(): pl.pallas_call(multiply, out_shape=[pltpu.VMEM((2 * W, W), jnp.float32),...  23.2 us
    pallas_call x1, Pallas kernels, on_device(): pl.pallas_call(prep, out_shape=[bf16(8, 512, W), bf16(5, 128, 2 * W)] + [...  13.9 us
    all_to_all x2, starting transfers between devices, along_y(): lax.all_to_all(value, 'row', 0, 0, axis_index_groups=Y_GROUPS, tiled=True)  12.5 us
    ppermute x6, starting transfers between devices, along_x(): lax.ppermute(value, 'col', [(i, i // 4 * 4 + (i % 4 + hop) % 4) for i in...  8.31 us
    pallas_call x1, Pallas kernels, on_device(): pl.pallas_call(finish, out_shape=jax.ShapeDtypeStruct((2 * W, W), jnp.flo...  7.85 us
  transfers between devices with their start and end apart: 14, of which 8 were waited for; matrix products, arithmetic and copies ran while one was open for 7% of the time, Pallas kernels for 9%

profile of v4, /device:TPU:1, one launch (start us, length us, event | category | flops | bytes accessed | tf_op | source)
XLA Modules:
  0.0 262.7 jit_solution(903926299267645265)
XLA Ops:
  0.0 0.1 pad_add_fusion.ids
  0.1 0.7 copy-done
  0.8 0.7 copy-done.1
  1.5 0.7 copy-done.3
  2.2 13.9 %prep.1 = (bf16[8,512,1024]{2,1,0:T(8,128)(2,1)}, bf16[5,128,2048]{2,1,0:T(8,128)(2,1)}, bf16[4,256,1024]{2,1,0:T(8,128)(2,1)}, bf16[4,256,1024]{2,1,0:T(8,128)(...) custom-call(s32[2]{0:T(128)S(1)} %pad_add_fusion.ids, ...), custom_call_target="tpu_custom_call" | custom-call | tf_op jit(solution)/shard_map/prep/pallas_call | solution.py:245
  16.1 6.1 %all-to-all-start = ((bf16[8,512,1024]{2,1,0:T(8,128)(2,1)}), bf16[8,512,1024]{2,1,0:T(8,128)(2,1)}, u32[]{:S(2)}, u32[]{:S(2)}) async-start(bf16[8,512,1024]{2,1,0:T(8,128)(2,1)} %get-tuple-element.33), calls=%async_computation | async-start | bytes 16777216 | tf_op jit(solution)/shard_map/all_to_all | solution.py:243
  22.2 1.3 collective-permute-start.2
  23.5 1.7 collective-permute-start.3
  25.2 3.6 %collective-permute-start = (bf16[5,128,2048]{2,1,0:T(8,128)(2,1)}, bf16[5,128,2048]{2,1,0:T(8,128)(2,1)}, u32[]{:S(2)}, u32[]{:S(2)}) collective-permute-start(bf16[5,128,2048]{2,1,0:T(8,128)(2,1)} %get-tuple-element.31), channel_id=1, source_target_pairs={{0,64},{8,72},{16,80},{24,88},{32,96},{40,104},{48,112},{56,120},{... | collective-permute-start | bytes 7864328 | tf_op jit(solution)/shard_map/ppermute | solution.py:231
  28.7 1.0 collective-permute-start.1
  29.8 41.6 %collective-permute-done.2.r1 = bf16[4,256,1024]{2,1,0:T(8,128)(2,1)} collective-permute-done((bf16[4,256,1024]{2,1,0:T(8,128)(2,1)}, bf16[4,256,1024]{2,1,0:T(8,128)(2,1)}, u32[]{:S(2)}, u32[]{:S(2)}) %collective-permute-start.2) | collective-permute-done | bytes 2097184 | tf_op jit(solution)/shard_map/ppermute | solution.py:240
  71.4 0.0 collective-permute-done.3.r3
  71.4 2.0 collective-permute-start.4
  73.4 1.1 slice.25
  74.5 1.1 slice.26
  75.6 1.1 slice.28
  76.6 43.0 %collective-permute-done.4.r2 = bf16[4,256,1024]{2,1,0:T(8,128)(2,1)} collective-permute-done((bf16[4,256,1024]{2,1,0:T(8,128)(2,1)}, bf16[4,256,1024]{2,1,0:T(8,128)(2,1)}, u32[]{:S(2)}, u32[]{:S(2)}) %collective-permute-start.4) | collective-permute-done | bytes 2097184 | tf_op jit(solution)/shard_map/ppermute | solution.py:240
  119.7 1.1 slice.33
  120.7 1.6 pad_maximum_fusion.1
  122.3 0.0 all-to-all-done.near_a
  122.3 3.1 %slice.32 = bf16[8,128,1024]{2,1,0:T(8,128)(2,1)} slice(bf16[8,512,1024]{2,1,0:T(8,128)(2,1)} %all-to-all-done.near_a), slice={[0:8], [384:512], [0:1024]} | slice | bytes 4194304 | tf_op jit(solution)/shard_map/slice | solution.py:264
  125.4 0.0 collective-permute-done
  125.4 16.9 %collective-permute-done.1.p0 = bf16[5,256,1024]{2,1,0:T(8,128)(2,1)S(1)} collective-permute-done((bf16[5,256,1024]{2,1,0:T(8,128)(2,1)}, bf16[5,256,1024]{2,1,0:T(8,128)(2,1)S(1)}, u32[]{:S(2)}, u32[]{:S(2)}) %collective-permute-start.1) | collective-permute-done | bytes 2621472 | tf_op jit(solution)/shard_map/ppermute | solution.py:234
  142.3 0.8 collective-permute-start.6
  143.1 1.8 constant_dynamic-slice_fusion
  144.9 2.7 %slice_bitcast_fusion.1 = (bf16[4,1,128,2048]{3,2,0,1:T(8,128)(2,1)S(1)}, bf16[4,1,128,2048]{3,2,0,1:T(8,128)(2,1)S(1)}) fusion(bf16[5,128,2048]{2,1,0:T(8,128)(2,1)} %collective-permute-done), kind=kLoop, calls=%fused_computation.3 | loop fusion | bytes 8388608 | tf_op jit(solution)/shard_map/stack | solution.py:273
  147.7 0.4 pad_maximum_fusion
  148.1 2.3 copy.7
  150.4 6.4 %all-to-all-start.1 = ((bf16[8,128,2048]{2,1,0:T(8,128)(2,1)}), bf16[8,128,2048]{2,1,0:T(8,128)(2,1)}, u32[]{:S(2)}, u32[]{:S(2)}) async-start(bf16[8,128,2048]{2,1,0:T(8,128)(2,1)} %bitcast.11), calls=%async_computation.1 | async-start | bytes 8388608 | tf_op jit(solution)/shard_map/all_to_all | solution.py:243
  156.8 0.0 collective-permute-start.7
  156.8 2.0 collective-permute-start.8
  158.8 1.3 collective-permute-start.9
  160.1 1.8 slice.31
  161.9 0.0 copy-start.2
  161.9 1.1 collective-permute-start.5
  163.0 20.5 %collective-permute-done.7.p1 = bf16[2,256,1024]{2,1,0:T(8,128)(2,1)S(1)} collective-permute-done((bf16[2,256,1024]{2,1,0:T(8,128)(2,1)}, bf16[2,256,1024]{2,1,0:T(8,128)(2,1)S(1)}, u32[]{:S(2)}, u32[]{:S(2)}) %collective-permute-start.7) | collective-permute-done | bytes 1048608 | tf_op jit(solution)/shard_map/ppermute | solution.py:240
  183.5 21.2 %collective-permute-done.8.p2 = bf16[2,256,1024]{2,1,0:T(8,128)(2,1)S(1)} collective-permute-done((bf16[2,256,1024]{2,1,0:T(8,128)(2,1)}, bf16[2,256,1024]{2,1,0:T(8,128)(2,1)S(1)}, u32[]{:S(2)}, u32[]{:S(2)}) %collective-permute-start.8) | collective-permute-done | bytes 1048608 | tf_op jit(solution)/shard_map/ppermute | solution.py:240
  204.8 0.9 collective-permute-done.9.p3
  205.7 0.0 collective-permute-done.6.o_cross
  205.7 0.1 copy-done.6
  205.7 1.8 collective-permute-start.10
  207.6 0.0 collective-permute-start.11
  207.6 0.0 collective-permute-done.5.o_near
  207.6 0.0 all-to-all-done.1.e_far
  207.6 4.1 %collective-permute-done.10.o_swap = bf16[8,128,1024]{2,1,0:T(8,128)(2,1)} collective-permute-done((bf16[8,128,1024]{2,1,0:T(8,128)(2,1)}, bf16[8,128,1024]{2,1,0:T(8,128)(2,1)}, u32[]{:S(2)}, u32[]{:S(2)}) %collective-permute-start.10) | collective-permute-done | bytes 2097184 | tf_op jit(solution)/shard_map/ppermute | solution.py:237
  211.7 23.2 %multiply.1 = (f32[2048,1024]{1,0:T(8,128)S(1)}, bf16[2,8,128,1024]{3,2,1,0:T(8,128)(2,1)S(1)}) custom-call(s32[2]{0:T(128)S(1)} %pad_add_fusion.ids, bf16[8,512,1024]{2,1,0:T(8,128)(2,1)} %all-to-all-done.near_a, bf16[8,128,2048]{2,1,0:T(8,128)(2,1)} %all-to-all-done.1.e_far, bf16[8,128,1024]{2,1,0:T(8,128)(2,1)} %collective-permute-done.5.o_near, ...), custom_call_target="tpu_custom_call" | custom-call | tf_op jit(solution)/shard_map/multiply/pallas_call | solution.py:279
  234.9 19.8 %collective-permute-done.11.right = bf16[4,256,1024]{2,1,0:T(8,128)(2,1)S(1)} collective-permute-done((bf16[4,256,1024]{2,1,0:T(8,128)(2,1)}, bf16[4,256,1024]{2,1,0:T(8,128)(2,1)S(1)}, u32[]{:S(2)}, u32[]{:S(2)}) %collective-permute-start.11) | collective-permute-done | bytes 2097184 | tf_op jit(solution)/shard_map/ppermute | solution.py:234
  254.7 7.8 %finish.1 = f32[2048,1024]{1,0:T(8,128)} custom-call(s32[16,32]{1,0:T(8,128)S(1)} %bitcast.10, f32[2048,1024]{1,0:T(8,128)S(1)} %get-tuple-element.54.part, bf16[2,8,128,1024]{3,2,1,0:T(8,128)(2,1)S(1)} %get-tuple-element.55.left, bf16[4,256,1024]{2,1,0:T(8,128)(2,1)S(1)} %collective-permute-done.11.right), custom_call_target="tpu_custom_call" | custom-call | tf_op jit(solution)/shard_map/finish/pallas_call | solution.py:289
  (11 shorter events, 0.0 us)
Async XLA Ops:
  0.1 0.7 copy-start
  0.8 0.7 copy-start.1
  1.5 0.7 copy-start.3
  16.1 106.2 %all-to-all-start = ((bf16[8,512,1024]{2,1,0:T(8,128)(2,1)}), bf16[8,512,1024]{2,1,0:T(8,128)(2,1)}, u32[]{:S(2)}, u32[]{:S(2)}) async-start(bf16[8,512,1024]{2,1,0:T(8,128)(2,1)} %get-tuple-element.33), calls=%async_computation | async-start | bytes 16777216 | tf_op jit(solution)/shard_map/all_to_all | solution.py:243
  22.2 49.2 %collective-permute-start.2 = (bf16[4,256,1024]{2,1,0:T(8,128)(2,1)}, bf16[4,256,1024]{2,1,0:T(8,128)(2,1)}, u32[]{:S(2)}, u32[]{:S(2)}) collective-permute-start(bf16[4,256,1024]{2,1,0:T(8,128)(2,1)} %get-tuple-element.36), channel_id=1, source_target_pairs={{0,1},{1,2},{2,3},{3,0},{4,5},{5,6},{6,7},{7,4},{8,9},{9,10},{10,1... | collective-permute-start | bytes 6291464 | tf_op jit(solution)/shard_map/ppermute | solution.py:240
  23.5 47.9 %collective-permute-start.3 = (bf16[4,256,1024]{2,1,0:T(8,128)(2,1)}, bf16[4,256,1024]{2,1,0:T(8,128)(2,1)}, u32[]{:S(2)}, u32[]{:S(2)}) collective-permute-start(bf16[4,256,1024]{2,1,0:T(8,128)(2,1)} %get-tuple-element.37), channel_id=1, source_target_pairs={{0,3},{1,0},{2,1},{3,2},{4,7},{5,4},{6,5},{7,6},{8,11},{9,8},{10,9... | collective-permute-start | bytes 6291464 | tf_op jit(solution)/shard_map/ppermute | solution.py:240
  25.2 100.3 %collective-permute-start = (bf16[5,128,2048]{2,1,0:T(8,128)(2,1)}, bf16[5,128,2048]{2,1,0:T(8,128)(2,1)}, u32[]{:S(2)}, u32[]{:S(2)}) collective-permute-start(bf16[5,128,2048]{2,1,0:T(8,128)(2,1)} %get-tuple-element.31), channel_id=1, source_target_pairs={{0,64},{8,72},{16,80},{24,88},{32,96},{40,104},{48,112},{56,120},{... | collective-permute-start | bytes 7864328 | tf_op jit(solution)/shard_map/ppermute | solution.py:231
  28.7 113.6 %collective-permute-start.1 = (bf16[5,256,1024]{2,1,0:T(8,128)(2,1)}, bf16[5,256,1024]{2,1,0:T(8,128)(2,1)S(1)}, u32[]{:S(2)}, u32[]{:S(2)}) collective-permute-start(bf16[5,256,1024]{2,1,0:T(8,128)(2,1)} %get-tuple-element.32), channel_id=1, source_target_pairs={{0,4},{1,5},{2,6},{3,7},{4,0},{5,1},{6,2},{7,3},{8,12},{9,13},{10,... | collective-permute-start | bytes 7864328 | tf_op jit(solution)/shard_map/ppermute | solution.py:234
  71.4 48.3 %collective-permute-start.4 = (bf16[4,256,1024]{2,1,0:T(8,128)(2,1)}, bf16[4,256,1024]{2,1,0:T(8,128)(2,1)}, u32[]{:S(2)}, u32[]{:S(2)}) collective-permute-start(bf16[4,256,1024]{2,1,0:T(8,128)(2,1)} %get-tuple-element.39), channel_id=1, source_target_pairs={{0,2},{1,3},{2,0},{3,1},{4,6},{5,7},{6,4},{7,5},{8,10},{9,11},{10,... | collective-permute-start | bytes 6291464 | tf_op jit(solution)/shard_map/ppermute | solution.py:240
  142.3 2.6 copy-start.4
  142.3 63.4 %collective-permute-start.6 = (bf16[8,128,1024]{2,1,0:T(8,128)(2,1)}, bf16[8,128,1024]{2,1,0:T(8,128)(2,1)}, u32[]{:S(2)}, u32[]{:S(2)}) collective-permute-start(bf16[8,128,1024]{2,1,0:T(8,128)(2,1)} %slice.32), channel_id=1, source_target_pairs={{0,64},{8,72},{16,80},{24,88},{32,96},{40,104},{48,112},{56,120},{... | collective-permute-start | bytes 6291464 | tf_op jit(solution)/shard_map/ppermute | solution.py:231
  150.4 57.2 %all-to-all-start.1 = ((bf16[8,128,2048]{2,1,0:T(8,128)(2,1)}), bf16[8,128,2048]{2,1,0:T(8,128)(2,1)}, u32[]{:S(2)}, u32[]{:S(2)}) async-start(bf16[8,128,2048]{2,1,0:T(8,128)(2,1)} %bitcast.11), calls=%async_computation.1 | async-start | bytes 8388608 | tf_op jit(solution)/shard_map/all_to_all | solution.py:243
  156.8 26.7 %collective-permute-start.7 = (bf16[2,256,1024]{2,1,0:T(8,128)(2,1)}, bf16[2,256,1024]{2,1,0:T(8,128)(2,1)S(1)}, u32[]{:S(2)}, u32[]{:S(2)}) collective-permute-start(bf16[2,256,1024]{2,1,0:T(8,128)(2,1)} %get-tuple-element.47), channel_id=1, source_target_pairs={{0,1},{1,2},{2,3},{3,0},{4,5},{5,6},{6,7},{7,4},{8,9},{9,10},{10,1... | collective-permute-start | bytes 3145736 | tf_op jit(solution)/shard_map/ppermute | solution.py:240
  156.8 48.0 %collective-permute-start.8 = (bf16[2,256,1024]{2,1,0:T(8,128)(2,1)}, bf16[2,256,1024]{2,1,0:T(8,128)(2,1)S(1)}, u32[]{:S(2)}, u32[]{:S(2)}) collective-permute-start(bf16[2,256,1024]{2,1,0:T(8,128)(2,1)} %get-tuple-element.48), channel_id=1, source_target_pairs={{0,2},{1,3},{2,0},{3,1},{4,6},{5,7},{6,4},{7,5},{8,10},{9,11},{10,... | collective-permute-start | bytes 3145736 | tf_op jit(solution)/shard_map/ppermute | solution.py:240
  158.8 46.8 %collective-permute-start.9 = (bf16[2,256,1024]{2,1,0:T(8,128)(2,1)}, bf16[2,256,1024]{2,1,0:T(8,128)(2,1)S(1)}, u32[]{:S(2)}, u32[]{:S(2)}) collective-permute-start(bf16[2,256,1024]{2,1,0:T(8,128)(2,1)} %get-tuple-element.49), channel_id=1, source_target_pairs={{0,3},{1,0},{2,1},{3,2},{4,7},{5,4},{6,5},{7,6},{8,11},{9,8},{10,9... | collective-permute-start | bytes 3145736 | tf_op jit(solution)/shard_map/ppermute | solution.py:240
  161.9 92.8 %copy-start.2 = (s32[32,16]{0,1:T(8,128)S(1)}, s32[32,16]{0,1:T(8,128)}, u32[]{:S(2)}) copy-start(s32[32,16]{0,1:T(8,128)} %param.10) | copy-start | bytes 6148
  161.9 45.7 %collective-permute-start.5 = (bf16[8,128,1024]{2,1,0:T(8,128)(2,1)S(1)}, bf16[8,128,1024]{2,1,0:T(8,128)(2,1)}, u32[]{:S(2)}, u32[]{:S(2)}) collective-permute-start(bf16[8,128,1024]{2,1,0:T(8,128)(2,1)S(1)} %slice.31), channel_id=1, source_target_pairs={{0,8},{8,0},{16,24},{24,16},{32,40},{40,32},{48,56},{56,48},{64,72... | collective-permute-start | bytes 6291464 | tf_op jit(solution)/shard_map/ppermute | solution.py:237
  183.5 22.2 %copy-start.5 = (bf16[2,256,1024]{2,1,0:T(8,128)(2,1)}, bf16[2,256,1024]{2,1,0:T(8,128)(2,1)S(1)}, u32[]{:S(2)}) copy-start(bf16[2,256,1024]{2,1,0:T(8,128)(2,1)S(1)} %collective-permute-done.7.p1) | copy-start | bytes 3145732
  204.8 1.0 copy-start.6
  205.7 1.9 copy-start.7
  205.7 6.0 %collective-permute-start.10 = (bf16[8,128,1024]{2,1,0:T(8,128)(2,1)}, bf16[8,128,1024]{2,1,0:T(8,128)(2,1)}, u32[]{:S(2)}, u32[]{:S(2)}) collective-permute-start(bf16[8,128,1024]{2,1,0:T(8,128)(2,1)} %collective-permute-done.6.o_cross), channel_id=1, source_target_pairs={{0,8},{8,0},{16,24},{24,16},{32,40},{40,32},{48,56},{56,48},{64,72... | collective-permute-start | bytes 6291464 | tf_op jit(solution)/shard_map/ppermute | solution.py:237
  207.6 47.1 %collective-permute-start.11 = (bf16[4,256,1024]{2,1,0:T(8,128)(2,1)}, bf16[4,256,1024]{2,1,0:T(8,128)(2,1)S(1)}, u32[]{:S(2)}, u32[]{:S(2)}) collective-permute-start(bf16[4,256,1024]{2,1,0:T(8,128)(2,1)} %pad_maximum_fusion.1), channel_id=1, source_target_pairs={{0,4},{1,5},{2,6},{3,7},{4,0},{5,1},{6,2},{7,3},{8,12},{9,13},{10,... | collective-permute-start | bytes 6291464 | tf_op jit(solution)/shard_map/ppermute | solution.py:234

commit v5 on v4

--- a/solution.py
+++ b/solution.py
@@ -26,58 +26,12 @@
     return pltpu.make_async_copy(src.at[rows], dst.at[rows], sem)
 
 
-def prep(ids, kdist, mask_a, at, mask_b, bmat, to_y, a_z, x0, x1, x2, x3, b_z,
-         wide_a, held_a, wide_b, held_b, in_sems, sems):
+def prep_a(ids, kdist, mask_a, at, to_y, a_z, to_odd, wide_a, held_a, in_sems, sems):
     row_id, col_id = ids[0], ids[1]
     a_half = row_id // 8
-    b_half, here = col_id // 4, col_id % 4
-    to_x = (x0, x1, x2, x3)
-    for n in range(8):
-        load(bmat, held_b, n, in_sems.at[8 + n]).start()
     for n in range(8):
         load(at, held_a, n, in_sems.at[n]).start()
-    wide_b[...] = spread(mask_b[...], W)
     wide_a[...] = spread(mask_a[...].T, 2 * W)
-
-    for block in range(2 * KB):
-        if block % 8 == 0:
-            load(bmat, held_b, block // 8, in_sems.at[8 + block // 8]).wait()
-        gain = wide_b[block:block + 1, :].astype(jnp.bfloat16)
-        rows = pl.ds(block * BS, BS)
-        held_b[rows, :] = held_b[rows, :] * gain
-        pos = kdist[col_id * 2 * KB + block]
-        inner = pl.ds(pl.multiple_of((pos % KB - 4 * col_id) * BS, BS), BS)
-        tile = (pos // KB - row_id + NP) % NP
-        src = held_b.at[rows, :]
-        near = (tile - 8 * b_half + NP) % NP
-        far = (near + 8) % NP
-        odd = tile % 2 == 1
-        even = tile % 2 == 0
-        first = (jnp.where(odd, tile, near) // 2 - here + 8) % 4
-        kind = jnp.where(odd, jnp.where(tile // 8 == b_half, 1, 3), 0)
-        second = (near // 2 - 1 - here + 8) % 4
-
-        def send(hop, kind):
-            def to(n):
-                def run():
-                    pltpu.make_async_copy(src, to_x[n].at[kind, inner, :], sems.at[2 + n]).start()
-
-                return run
-
-            lax.cond(hop < 2, lambda: lax.cond(hop == 0, to(0), to(1)), lambda: lax.cond(hop == 2, to(2), to(3)))
-
-        @pl.when(odd | (near < 8))
-        def _():
-            send(first, kind)
-
-        @pl.when(even & (near > 0) & (near <= 8))
-        def _():
-            send(second, 2)
-
-        @pl.when(even & (far <= 8))
-        def _():
-            pltpu.make_async_copy(src, b_z.at[far // 2, inner, :], sems.at[6]).start()
-
     for block in range(KB):
         if block % 4 == 0:
             load(at, held_a, block // 4, in_sems.at[block // 4]).wait()
@@ -96,9 +50,13 @@
             odd = tile % 2 == 1
             even = tile % 2 == 0
             first = jnp.where(odd, tile // 2 % 4 * 2 + t, near)
-            first_row = jnp.where(odd, jnp.where(tile // 8 == a_half, 256, 384), t * 128) + slot
-
-            @pl.when(odd | (near < 8))
+            first_row = jnp.where(odd, 256, t * 128) + slot
+
+            @pl.when(odd & (near >= 8))
+            def _():
+                pltpu.make_async_copy(src, to_odd.at[first, inner, :], sems.at[2]).start()
+
+            @pl.when(near < 8)
             def _():
                 dst = to_y.at[first, pl.ds(pl.multiple_of(first_row, BS), BS), :]
                 pltpu.make_async_copy(src, dst, sems.at[0]).start()
@@ -112,7 +70,57 @@
             def _():
                 pltpu.make_async_copy(src, a_z.at[far // 2, inner, cols], sems.at[1]).start()
 
-    for n, ref in enumerate((to_y, a_z, x0, x1, x2, x3, b_z)):
+    for n, ref in enumerate((to_y, a_z, to_odd)):
+        pltpu.make_async_copy(ref, ref, sems.at[n]).wait()
+
+
+def prep_b(ids, kdist, mask_b, bmat, x0, x1, x2, x3, b_z, wide_b, held_b, in_sems, sems):
+    row_id, col_id = ids[0], ids[1]
+    b_half, here = col_id // 4, col_id % 4
+    to_x = (x0, x1, x2, x3)
+    for n in range(8):
+        load(bmat, held_b, n, in_sems.at[n]).start()
+    wide_b[...] = spread(mask_b[...], W)
+    for block in range(2 * KB):
+        if block % 8 == 0:
+            load(bmat, held_b, block // 8, in_sems.at[block // 8]).wait()
+        gain = wide_b[block:block + 1, :].astype(jnp.bfloat16)
+        rows = pl.ds(block * BS, BS)
+        held_b[rows, :] = held_b[rows, :] * gain
+        pos = kdist[col_id * 2 * KB + block]
+        inner = pl.ds(pl.multiple_of((pos % KB - 4 * col_id) * BS, BS), BS)
+        tile = (pos // KB - row_id + NP) % NP
+        src = held_b.at[rows, :]
+        near = (tile - 8 * b_half + NP) % NP
+        far = (near + 8) % NP
+        odd = tile % 2 == 1
+        even = tile % 2 == 0
+        first = (jnp.where(odd, tile, near) // 2 - here + 8) % 4
+        kind = jnp.where(odd, jnp.where(tile // 8 == b_half, 1, 3), 0)
+        second = (near // 2 - 1 - here + 8) % 4
+
+        def send(hop, kind):
+            def to(n):
+                def run():
+                    pltpu.make_async_copy(src, to_x[n].at[kind, inner, :], sems.at[n]).start()
+
+                return run
+
+            lax.cond(hop < 2, lambda: lax.cond(hop == 0, to(0), to(1)), lambda: lax.cond(hop == 2, to(2), to(3)))
+
+        @pl.when(odd | (near < 8))
+        def _():
+            send(first, kind)
+
+        @pl.when(even & (near > 0) & (near <= 8))
+        def _():
+            send(second, 2)
+
+        @pl.when(even & (far <= 8))
+        def _():
+            pltpu.make_async_copy(src, b_z.at[far // 2, inner, :], sems.at[4]).start()
+
+    for n, ref in enumerate((x0, x1, x2, x3, b_z)):
         pltpu.make_async_copy(ref, ref, sems.at[n]).wait()
 
 
@@ -242,37 +250,48 @@
     def along_y(value):
         return lax.all_to_all(value, "row", 0, 0, axis_index_groups=Y_GROUPS, tiled=True)
 
-    a_y, a_z, x0, x1, x2, x3, b_z = pl.pallas_call(
-        prep,
-        out_shape=[bf16(8, 512, W), bf16(5, 128, 2 * W)] + [bf16(4, 256, W)] * 4 + [bf16(5, 256, W)],
-        in_specs=[SMEM, SMEM, VMEM, HBM, VMEM, HBM],
-        out_specs=[HBM] * 7,
-        scratch_shapes=[pltpu.VMEM((32, 2 * W), jnp.float32), pltpu.VMEM((2048, 2 * W), jnp.bfloat16),
-                        pltpu.VMEM((64, W), jnp.float32), pltpu.VMEM((4096, W), jnp.bfloat16),
-                        pltpu.SemaphoreType.DMA((16,)), pltpu.SemaphoreType.DMA((7,))],
-        compiler_params=pltpu.CompilerParams(vmem_limit_bytes=32 * MIB),
-        name="prep",
-    )(ids, kdist, mask_a, *in_hbm(at), mask_b.T, *in_hbm(bmat))
+    x0, x1, x2, x3, b_z = pl.pallas_call(
+        prep_b,
+        out_shape=[bf16(4, 256, W)] * 4 + [bf16(5, 256, W)],
+        in_specs=[SMEM, SMEM, VMEM, HBM],
+        out_specs=[HBM] * 5,
+        scratch_shapes=[pltpu.VMEM((64, W), jnp.float32), pltpu.VMEM((4096, W), jnp.bfloat16),
+                        pltpu.SemaphoreType.DMA((8,)), pltpu.SemaphoreType.DMA((5,))],
+        compiler_params=pltpu.CompilerParams(vmem_limit_bytes=24 * MIB),
+        name="prep_b",
+    )(ids, kdist, mask_b.T, *in_hbm(bmat))
 
     b_cross = swap_z_lo(b_z)
     r1, r3 = along_x(x1, 1), along_x(x3, 3)
     x2, r1, r3 = lax.optimization_barrier((x2, r1, r3))
     r2 = along_x(x2, 2)
+    at, b_z = lax.optimization_barrier((at, b_z))
+    a_y, a_z, a_odd = pl.pallas_call(
+        prep_a,
+        out_shape=[bf16(8, 384, W), bf16(5, 128, 2 * W), bf16(8, 128, W)],
+        in_specs=[SMEM, SMEM, VMEM, HBM],
+        out_specs=[HBM] * 3,
+        scratch_shapes=[pltpu.VMEM((32, 2 * W), jnp.float32), pltpu.VMEM((2048, 2 * W), jnp.bfloat16),
+                        pltpu.SemaphoreType.DMA((8,)), pltpu.SemaphoreType.DMA((3,))],
+        compiler_params=pltpu.CompilerParams(vmem_limit_bytes=24 * MIB),
+        name="prep_a",
+    )(ids, kdist, mask_a, *in_hbm(at))
+    o_send = along_y(a_odd)
+    a_y, o_send = lax.optimization_barrier((a_y, o_send))
+    near_a = along_y(a_y)
+    a_z, b_cross, r1, r3 = lax.optimization_barrier((a_z, b_cross, r1, r3))
     a_cross = swap_z_hi(a_z)
-    near_a = along_y(a_y)
-
-    o_send = near_a[:, 384:]
+    far = [lax.dynamic_slice_in_dim(b_cross, (here + hop) % 4, 2, 0) for hop in range(1, 4)]
+    p1, p3 = along_x(far[0], 1), along_x(far[2], 3)
+
+    o_send, p2_send, a_cross, p1, p3 = lax.optimization_barrier((o_send, far[1], a_cross, p1, p3))
+    o_cross = swap_z_hi(o_send)
+    p2 = along_x(p2_send, 2)
+    e_far = along_y(jnp.stack([a_cross[:4], a_cross[1:]], axis=1).reshape(8, 128, 2 * W))
+    o_near = swap_core(near_a[:, 256:])
+
     q_send = jnp.concatenate([v[3:4] for v in (x0, r1, r2, r3)], axis=0)
-    a_cross, b_cross, near_a, o_send, q_send = lax.optimization_barrier((a_cross, b_cross, near_a, o_send, q_send))
-    o_cross = swap_z_hi(o_send)
-    o_near = swap_core(near_a[:, 256:384])
-
-    far = [lax.dynamic_slice_in_dim(b_cross, (here + hop) % 4, 2, 0) for hop in range(1, 4)]
-    a_cross, *far = lax.optimization_barrier((a_cross, *far))
-    p1, p2, p3 = along_x(far[0], 1), along_x(far[1], 2), along_x(far[2], 3)
-    e_far = along_y(jnp.stack([a_cross[:4], a_cross[1:]], axis=1).reshape(8, 128, 2 * W))
-
-    q_send, o_cross, p1, p2, p3 = lax.optimization_barrier((q_send, o_cross, p1, p2, p3))
+    q_send, o_cross, p2 = lax.optimization_barrier((q_send, o_cross, p2))
     q = swap_z_lo(q_send)
     o_swap = swap_core(o_cross)
 

time: 263 us -> 258 us (0.981); the launches traced: 263 us -> 255 us
  waiting for transfers between devices: 168 us -> 142 us
  starting transfers between devices: 29.2 us -> 49.9 us
  local copies, waits for them, and re-layouts: 18.2 us -> 14.1 us
    ppermute x6, waiting for transfers between devices: 127 us -> 60.1 us  [along_x(): lax.ppermute(value, 'col', [(i, i // 4 * 4 + (i % 4 + hop) % 4) for i in...]
    all_to_all x2 -> x3, waiting for transfers between devices: 0.01 us -> 43.4 us  [along_y(): lax.all_to_all(value, 'row', 0, 0, axis_index_groups=Y_GROUPS, tiled=True)]
    ppermute x2, waiting for transfers between devices: 0.01 us -> 27.3 us  [swap_z_hi(): return lax.ppermute(value, 'row', [(i, i ^ 8) for i in range(16)])]
    ppermute x2, waiting for transfers between devices: 36.7 us -> 11.5 us  [swap_z_lo(): return lax.ppermute(value, 'col', [(i, i ^ 4) for i in range(8)])]
    all_to_all x2 -> x3, starting transfers between devices: 12.5 us -> 33.6 us  [along_y(): lax.all_to_all(value, 'row', 0, 0, axis_index_groups=Y_GROUPS, tiled=True)]
    ppermute x2, waiting for transfers between devices: 4.11 us -> 0.01 us  [swap_core(): return lax.ppermute(value, 'row', [(i, i ^ 1) for i in range(16)])]
    pallas_call x1 -> x2, Pallas kernels: 13.9 us -> 14.8 us  [the longest x1 7.51 us: on_device(): pl.pallas_call(prep_a, out_shape=[bf16(8, 384, W), bf16(5, 128, 2 * W), b...]
  transfers between devices with their start and end apart: 14 -> 15, of which waited for: 8 -> 9; matrix products, arithmetic and copies ran while one was open for 7% -> 6% of each run, Pallas kernels for 9% -> 9%
where the time goes in v5:
time: 258 us; the launch traced here: 255 us
  waiting for transfers between devices  142 us (55%)
  starting transfers between devices  49.9 us (19%)
  Pallas kernels  45.9 us (18%)
  local copies, waits for them, and re-layouts  14.1 us (5%)
    ppermute x6, waiting for transfers between devices, along_x(): lax.ppermute(value, 'col', [(i, i // 4 * 4 + (i % 4 + hop) % 4) for i in...  60.1 us
    all_to_all x3, waiting for transfers between devices, along_y(): lax.all_to_all(value, 'row', 0, 0, axis_index_groups=Y_GROUPS, tiled=True)  43.4 us
    all_to_all x3, starting transfers between devices, along_y(): lax.all_to_all(value, 'row', 0, 0, axis_index_groups=Y_GROUPS, tiled=True)  33.6 us
    ppermute x2, waiting for transfers between devices, swap_z_hi(): return lax.ppermute(value, 'row', [(i, i ^ 8) for i in range(16)])  27.3 us
    pallas_call x1, Pallas kernels, on_device(): pl.pallas_call(multiply, out_shape=[pltpu.VMEM((2 * W, W), jnp.float32),...  23.2 us
    ppermute x2, waiting for transfers between devices, swap_z_lo(): return lax.ppermute(value, 'col', [(i, i ^ 4) for i in range(8)])  11.5 us
    pallas_call x1, Pallas kernels, on_device(): pl.pallas_call(finish, out_shape=jax.ShapeDtypeStruct((2 * W, W), jnp.flo...  7.85 us
    pallas_call x1, Pallas kernels, on_device(): pl.pallas_call(prep_a, out_shape=[bf16(8, 384, W), bf16(5, 128, 2 * W), b...  7.51 us
  transfers between devices with their start and end apart: 15, of which 9 were waited for; matrix products, arithmetic and copies ran while one was open for 6% of the time, Pallas kernels for 9%

profile of v5, /device:TPU:1, one launch (start us, length us, event | category | flops | bytes accessed | tf_op | source)
XLA Modules:
  0.0 254.6 jit_solution(17702529722439485720)
XLA Ops:
  0.0 0.1 pad_add_fusion.ids
  0.1 0.7 copy-done.2
  0.8 0.7 copy-done.3
  1.5 7.3 %prep_b.1 = (bf16[4,256,1024]{2,1,0:T(8,128)(2,1)}, bf16[4,256,1024]{2,1,0:T(8,128)(2,1)}, bf16[4,256,1024]{2,1,0:T(8,128)(2,1)}, bf16[4,256,1024]{2,1,0:T(8,128)(2,1)}, bf16[5,256,1024]{2,1,0:T(8,128)(2,1)}) custom-call(s32[2]{0:T(128)S(1)} %pad_add_fusion.ids, s32[512]{0:T(512)S(1)} %copy-done.3, s32[16,64]{1,0:T(8,128)S(1)} %bitcast.10, ...), custom_call_target="tpu_custom_call" | custom-call | tf_op jit(solution)/shard_map/prep_b/pallas_call | solution.py:253
  8.8 0.0 copy-done
  8.8 7.5 %prep_a.1 = (bf16[8,384,1024]{2,1,0:T(8,128)(2,1)}, bf16[5,128,2048]{2,1,0:T(8,128)(2,1)}, bf16[8,128,1024]{2,1,0:T(8,128)(2,1)}) custom-call(s32[2]{0:T(128)S(1)} %pad_add_fusion.ids, s32[512]{0:T(512)S(1)} %copy-done.3, s32[32,32]{1,0:T(8,128)S(1)} %copy-done, bf16[2048,2048]{1,0:T(8,128)(2,1)} %at), custom_call_target="tpu_custom_call" | custom-call | tf_op jit(solution)/shard_map/prep_a/pallas_call | solution.py:269
  16.3 6.0 %all-to-all-start = ((bf16[8,128,1024]{2,1,0:T(8,128)(2,1)}), bf16[8,128,1024]{2,1,0:T(8,128)(2,1)}, u32[]{:S(2)}, u32[]{:S(2)}) async-start(bf16[8,128,1024]{2,1,0:T(8,128)(2,1)} %get-tuple-element.36), calls=%async_computation | async-start | bytes 4194304 | tf_op jit(solution)/shard_map/all_to_all | solution.py:251
  22.3 1.5 collective-permute-start
  23.8 1.3 collective-permute-start.1
  25.0 1.4 collective-permute-start.2
  26.5 22.2 %all-to-all-done = bf16[8,128,1024]{2,1,0:T(8,128)(2,1)} async-done(((bf16[8,128,1024]{2,1,0:T(8,128)(2,1)}), bf16[8,128,1024]{2,1,0:T(8,128)(2,1)}, u32[]{:S(2)}, u32[]{:S(2)}) %all-to-all-start) | async-done | bytes 2097184 | tf_op jit(solution)/shard_map/all_to_all | solution.py:251
  48.7 5.5 %all-to-all-start.1 = ((bf16[8,384,1024]{2,1,0:T(8,128)(2,1)}), bf16[8,384,1024]{2,1,0:T(8,128)(2,1)}, u32[]{:S(2)}, u32[]{:S(2)}) async-start(bf16[8,384,1024]{2,1,0:T(8,128)(2,1)} %get-tuple-element.37), calls=%async_computation.1 | async-start | bytes 12582912 | tf_op jit(solution)/shard_map/all_to_all | solution.py:251
  54.2 18.0 %collective-permute-done.1.r1 = bf16[4,256,1024]{2,1,0:T(8,128)(2,1)} collective-permute-done((bf16[4,256,1024]{2,1,0:T(8,128)(2,1)}, bf16[4,256,1024]{2,1,0:T(8,128)(2,1)}, u32[]{:S(2)}, u32[]{:S(2)}) %collective-permute-start.1) | collective-permute-done | bytes 2097184 | tf_op jit(solution)/shard_map/ppermute | solution.py:248
  72.2 0.0 collective-permute-done.2.r3
  72.2 9.0 %collective-permute-done.p0 = bf16[5,256,1024]{2,1,0:T(8,128)(2,1)S(1)} collective-permute-done((bf16[5,256,1024]{2,1,0:T(8,128)(2,1)}, bf16[5,256,1024]{2,1,0:T(8,128)(2,1)S(1)}, u32[]{:S(2)}, u32[]{:S(2)}) %collective-permute-start) | collective-permute-done | bytes 2621472 | tf_op jit(solution)/shard_map/ppermute | solution.py:242
  81.2 3.6 %collective-permute-start.3 = (bf16[5,128,2048]{2,1,0:T(8,128)(2,1)}, bf16[5,128,2048]{2,1,0:T(8,128)(2,1)}, u32[]{:S(2)}, u32[]{:S(2)}) collective-permute-start(bf16[5,128,2048]{2,1,0:T(8,128)(2,1)} %get-tuple-element.46), channel_id=1, source_target_pairs={{0,64},{8,72},{16,80},{24,88},{32,96},{40,104},{48,112},{56,120},{... | collective-permute-start | bytes 7864328 | tf_op jit(solution)/shard_map/ppermute | solution.py:239
  84.8 1.3 constant_dynamic-slice_fusion
  86.1 2.5 collective-permute-start.5
  88.6 0.0 collective-permute-start.4
  88.6 1.5 collective-permute-start.7
  90.1 20.7 %collective-permute-done.5.p3 = bf16[2,256,1024]{2,1,0:T(8,128)(2,1)S(1)} collective-permute-done((bf16[2,256,1024]{2,1,0:T(8,128)(2,1)S(1)}, bf16[2,256,1024]{2,1,0:T(8,128)(2,1)S(1)}, u32[]{:S(2)}, u32[]{:S(2)}) %collective-permute-start.5) | collective-permute-done | bytes 1048608 | tf_op jit(solution)/shard_map/ppermute | solution.py:248
  110.8 3.6 %collective-permute-done.4.p1 = bf16[2,256,1024]{2,1,0:T(8,128)(2,1)S(1)} collective-permute-done((bf16[2,256,1024]{2,1,0:T(8,128)(2,1)S(1)}, bf16[2,256,1024]{2,1,0:T(8,128)(2,1)S(1)}, u32[]{:S(2)}, u32[]{:S(2)}) %collective-permute-start.4) | collective-permute-done | bytes 1048608 | tf_op jit(solution)/shard_map/ppermute | solution.py:248
  114.4 27.3 %collective-permute-done.3 = bf16[5,128,2048]{2,1,0:T(8,128)(2,1)} collective-permute-done((bf16[5,128,2048]{2,1,0:T(8,128)(2,1)}, bf16[5,128,2048]{2,1,0:T(8,128)(2,1)}, u32[]{:S(2)}, u32[]{:S(2)}) %collective-permute-start.3) | collective-permute-done | bytes 2621472 | tf_op jit(solution)/shard_map/ppermute | solution.py:239
  141.7 2.6 %collective-permute-start.8 = (bf16[8,128,1024]{2,1,0:T(8,128)(2,1)}, bf16[8,128,1024]{2,1,0:T(8,128)(2,1)}, u32[]{:S(2)}, u32[]{:S(2)}) collective-permute-start(bf16[8,128,1024]{2,1,0:T(8,128)(2,1)} %all-to-all-done), channel_id=1, source_target_pairs={{0,64},{8,72},{16,80},{24,88},{32,96},{40,104},{48,112},{56,120},{... | collective-permute-start | bytes 6291464 | tf_op jit(solution)/shard_map/ppermute | solution.py:239
  144.4 2.5 slice_bitcast_fusion.1
  146.9 0.4 pad_maximum_fusion
  147.3 2.4 copy.7
  149.7 0.0 all-to-all-done.1.near_a
  149.7 22.2 %all-to-all-start.2 = ((bf16[8,128,2048]{2,1,0:T(8,128)(2,1)}), bf16[8,128,2048]{2,1,0:T(8,128)(2,1)}, u32[]{:S(2)}, u32[]{:S(2)}) async-start(bf16[8,128,2048]{2,1,0:T(8,128)(2,1)} %bitcast.11), calls=%async_computation.2 | async-start | bytes 8388608 | tf_op jit(solution)/shard_map/all_to_all | solution.py:251
  171.8 0.0 collective-permute-start.9
  171.8 1.1 slice.24
  172.9 1.1 slice.25
  174.0 1.1 slice.27
  175.1 0.0 collective-permute-done.7.r2
  175.1 1.8 pad_maximum_fusion.1
  176.9 0.1 copy-done.5
  177.0 3.1 %slice.28 = bf16[8,128,1024]{2,1,0:T(8,128)(2,1)} slice(bf16[8,384,1024]{2,1,0:T(8,128)(2,1)} %all-to-all-done.1.near_a), slice={[0:8], [256:384], [0:1024]} | slice | bytes 4194304 | tf_op jit(solution)/shard_map/slice | solution.py:291
  180.1 0.2 collective-permute-start.6
  180.3 17.8 %collective-permute-done.9.p2 = bf16[2,256,1024]{2,1,0:T(8,128)(2,1)S(1)} collective-permute-done((bf16[2,256,1024]{2,1,0:T(8,128)(2,1)}, bf16[2,256,1024]{2,1,0:T(8,128)(2,1)S(1)}, u32[]{:S(2)}, u32[]{:S(2)}) %collective-permute-start.9) | collective-permute-done | bytes 1048608 | tf_op jit(solution)/shard_map/ppermute | solution.py:248
  198.1 0.0 collective-permute-done.8.o_cross
  198.1 1.0 collective-permute-start.10
  199.1 0.5 collective-permute-start.11
  199.6 21.1 %all-to-all-done.2.e_far = bf16[8,128,2048]{2,1,0:T(8,128)(2,1)} async-done(((bf16[8,128,2048]{2,1,0:T(8,128)(2,1)}), bf16[8,128,2048]{2,1,0:T(8,128)(2,1)}, u32[]{:S(2)}, u32[]{:S(2)}) %all-to-all-start.2) | async-done | bytes 4194336 | tf_op jit(solution)/shard_map/all_to_all | solution.py:251
  220.8 0.0 collective-permute-done.6.o_near
  220.8 0.0 collective-permute-done.10.o_swap
  220.8 23.2 %multiply.1 = (f32[2048,1024]{1,0:T(8,128)S(1)}, bf16[2,8,128,1024]{3,2,1,0:T(8,128)(2,1)S(1)}) custom-call(s32[2]{0:T(128)S(1)} %pad_add_fusion.ids, bf16[8,384,1024]{2,1,0:T(8,128)(2,1)} %all-to-all-done.1.near_a, bf16[8,128,2048]{2,1,0:T(8,128)(2,1)} %all-to-all-done.2.e_far, bf16[8,128,1024]{2,1,0:T(8,128)(2,1)} %collective-permute-done.6.o_near, ...), custom_call_target="tpu_custom_call" | custom-call | tf_op jit(solution)/shard_map/multiply/pallas_call | solution.py:298
  244.0 2.5 %collective-permute-done.11.right = bf16[4,256,1024]{2,1,0:T(8,128)(2,1)S(1)} collective-permute-done((bf16[4,256,1024]{2,1,0:T(8,128)(2,1)}, bf16[4,256,1024]{2,1,0:T(8,128)(2,1)S(1)}, u32[]{:S(2)}, u32[]{:S(2)}) %collective-permute-start.11) | collective-permute-done | bytes 2097184 | tf_op jit(solution)/shard_map/ppermute | solution.py:242
  246.5 7.9 %finish.1 = f32[2048,1024]{1,0:T(8,128)} custom-call(s32[16,32]{1,0:T(8,128)S(1)} %bitcast.9, f32[2048,1024]{1,0:T(8,128)S(1)} %get-tuple-element.58.part, bf16[2,8,128,1024]{3,2,1,0:T(8,128)(2,1)S(1)} %get-tuple-element.59.left, bf16[4,256,1024]{2,1,0:T(8,128)(2,1)S(1)} %collective-permute-done.11.right), custom_call_target="tpu_custom_call" | custom-call | tf_op jit(solution)/shard_map/finish/pallas_call | solution.py:308
  (15 shorter events, 0.1 us)
Async XLA Ops:
  0.1 0.7 copy-start.2
  0.8 0.7 copy-start.3
  1.5 7.3 %copy-start = (s32[32,32]{1,0:T(8,128)S(1)}, s32[32,32]{1,0:T(8,128)}, u32[]{:S(2)}) copy-start(s32[32,32]{1,0:T(8,128)} %mask_a.1) | copy-start | bytes 12292
  16.3 32.4 %all-to-all-start = ((bf16[8,128,1024]{2,1,0:T(8,128)(2,1)}), bf16[8,128,1024]{2,1,0:T(8,128)(2,1)}, u32[]{:S(2)}, u32[]{:S(2)}) async-start(bf16[8,128,1024]{2,1,0:T(8,128)(2,1)} %get-tuple-element.36), calls=%async_computation | async-start | bytes 4194304 | tf_op jit(solution)/shard_map/all_to_all | solution.py:251
  22.3 58.9 %collective-permute-start = (bf16[5,256,1024]{2,1,0:T(8,128)(2,1)}, bf16[5,256,1024]{2,1,0:T(8,128)(2,1)S(1)}, u32[]{:S(2)}, u32[]{:S(2)}) collective-permute-start(bf16[5,256,1024]{2,1,0:T(8,128)(2,1)} %get-tuple-element.33), channel_id=1, source_target_pairs={{0,4},{1,5},{2,6},{3,7},{4,0},{5,1},{6,2},{7,3},{8,12},{9,13},{10,... | collective-permute-start | bytes 7864328 | tf_op jit(solution)/shard_map/ppermute | solution.py:242
  23.8 48.4 %collective-permute-start.1 = (bf16[4,256,1024]{2,1,0:T(8,128)(2,1)}, bf16[4,256,1024]{2,1,0:T(8,128)(2,1)}, u32[]{:S(2)}, u32[]{:S(2)}) collective-permute-start(bf16[4,256,1024]{2,1,0:T(8,128)(2,1)} %get-tuple-element.41), channel_id=1, source_target_pairs={{0,1},{1,2},{2,3},{3,0},{4,5},{5,6},{6,7},{7,4},{8,9},{9,10},{10,1... | collective-permute-start | bytes 6291464 | tf_op jit(solution)/shard_map/ppermute | solution.py:248
  25.0 47.2 %collective-permute-start.2 = (bf16[4,256,1024]{2,1,0:T(8,128)(2,1)}, bf16[4,256,1024]{2,1,0:T(8,128)(2,1)}, u32[]{:S(2)}, u32[]{:S(2)}) collective-permute-start(bf16[4,256,1024]{2,1,0:T(8,128)(2,1)} %get-tuple-element.42), channel_id=1, source_target_pairs={{0,3},{1,0},{2,1},{3,2},{4,7},{5,4},{6,5},{7,6},{8,11},{9,8},{10,9... | collective-permute-start | bytes 6291464 | tf_op jit(solution)/shard_map/ppermute | solution.py:248
  48.7 101.0 %all-to-all-start.1 = ((bf16[8,384,1024]{2,1,0:T(8,128)(2,1)}), bf16[8,384,1024]{2,1,0:T(8,128)(2,1)}, u32[]{:S(2)}, u32[]{:S(2)}) async-start(bf16[8,384,1024]{2,1,0:T(8,128)(2,1)} %get-tuple-element.37), calls=%async_computation.1 | async-start | bytes 12582912 | tf_op jit(solution)/shard_map/all_to_all | solution.py:251
  81.2 4.9 %copy-start.4 = (bf16[5,256,1024]{2,1,0:T(8,128)(2,1)}, bf16[5,256,1024]{2,1,0:T(8,128)(2,1)S(1)}, u32[]{:S(2)}) copy-start(bf16[5,256,1024]{2,1,0:T(8,128)(2,1)S(1)} %collective-permute-done.p0) | copy-start | bytes 7864324
  81.2 60.6 %collective-permute-start.3 = (bf16[5,128,2048]{2,1,0:T(8,128)(2,1)}, bf16[5,128,2048]{2,1,0:T(8,128)(2,1)}, u32[]{:S(2)}, u32[]{:S(2)}) collective-permute-start(bf16[5,128,2048]{2,1,0:T(8,128)(2,1)} %get-tuple-element.46), channel_id=1, source_target_pairs={{0,64},{8,72},{16,80},{24,88},{32,96},{40,104},{48,112},{56,120},{... | collective-permute-start | bytes 7864328 | tf_op jit(solution)/shard_map/ppermute | solution.py:239
  86.1 24.7 %collective-permute-start.5 = (bf16[2,256,1024]{2,1,0:T(8,128)(2,1)S(1)}, bf16[2,256,1024]{2,1,0:T(8,128)(2,1)S(1)}, u32[]{:S(2)}, u32[]{:S(2)}) collective-permute-start(bf16[2,256,1024]{2,1,0:T(8,128)(2,1)S(1)} %get-tuple-element.63), channel_id=1, source_target_pairs={{0,3},{1,0},{2,1},{3,2},{4,7},{5,4},{6,5},{7,6},{8,11},{9,8},{10,9... | collective-permute-start | bytes 3145736 | tf_op jit(solution)/shard_map/ppermute | solution.py:248
  88.6 25.8 %collective-permute-start.4 = (bf16[2,256,1024]{2,1,0:T(8,128)(2,1)S(1)}, bf16[2,256,1024]{2,1,0:T(8,128)(2,1)S(1)}, u32[]{:S(2)}, u32[]{:S(2)}) collective-permute-start(bf16[2,256,1024]{2,1,0:T(8,128)(2,1)S(1)} %get-tuple-element.64), channel_id=1, source_target_pairs={{0,1},{1,2},{2,3},{3,0},{4,5},{5,6},{6,7},{7,4},{8,9},{9,10},{10,1... | collective-permute-start | bytes 3145736 | tf_op jit(solution)/shard_map/ppermute | solution.py:248
  88.6 86.5 %collective-permute-start.7 = (bf16[4,256,1024]{2,1,0:T(8,128)(2,1)}, bf16[4,256,1024]{2,1,0:T(8,128)(2,1)S(1)}, u32[]{:S(2)}, u32[]{:S(2)}) collective-permute-start(bf16[4,256,1024]{2,1,0:T(8,128)(2,1)} %get-tuple-element.50), channel_id=1, source_target_pairs={{0,2},{1,3},{2,0},{3,1},{4,6},{5,7},{6,4},{7,5},{8,10},{9,11},{10,... | collective-permute-start | bytes 6291464 | tf_op jit(solution)/shard_map/ppermute | solution.py:248
  110.8 36.1 %copy-start.6 = (bf16[2,256,1024]{2,1,0:T(8,128)(2,1)}, bf16[2,256,1024]{2,1,0:T(8,128)(2,1)S(1)}, u32[]{:S(2)}) copy-start(bf16[2,256,1024]{2,1,0:T(8,128)(2,1)S(1)} %collective-permute-done.5.p3) | copy-start | bytes 3145732
  114.4 27.3 %copy-start.7 = (bf16[2,256,1024]{2,1,0:T(8,128)(2,1)}, bf16[2,256,1024]{2,1,0:T(8,128)(2,1)S(1)}, u32[]{:S(2)}) copy-start(bf16[2,256,1024]{2,1,0:T(8,128)(2,1)S(1)} %collective-permute-done.4.p1) | copy-start | bytes 3145732
  141.7 56.4 %collective-permute-start.8 = (bf16[8,128,1024]{2,1,0:T(8,128)(2,1)}, bf16[8,128,1024]{2,1,0:T(8,128)(2,1)}, u32[]{:S(2)}, u32[]{:S(2)}) collective-permute-start(bf16[8,128,1024]{2,1,0:T(8,128)(2,1)} %all-to-all-done), channel_id=1, source_target_pairs={{0,64},{8,72},{16,80},{24,88},{32,96},{40,104},{48,112},{56,120},{... | collective-permute-start | bytes 6291464 | tf_op jit(solution)/shard_map/ppermute | solution.py:239
  149.7 71.1 %all-to-all-start.2 = ((bf16[8,128,2048]{2,1,0:T(8,128)(2,1)}), bf16[8,128,2048]{2,1,0:T(8,128)(2,1)}, u32[]{:S(2)}, u32[]{:S(2)}) async-start(bf16[8,128,2048]{2,1,0:T(8,128)(2,1)} %bitcast.11), calls=%async_computation.2 | async-start | bytes 8388608 | tf_op jit(solution)/shard_map/all_to_all | solution.py:251
  171.8 26.3 %collective-permute-start.9 = (bf16[2,256,1024]{2,1,0:T(8,128)(2,1)}, bf16[2,256,1024]{2,1,0:T(8,128)(2,1)S(1)}, u32[]{:S(2)}, u32[]{:S(2)}) collective-permute-start(bf16[2,256,1024]{2,1,0:T(8,128)(2,1)} %get-tuple-element.53), channel_id=1, source_target_pairs={{0,2},{1,3},{2,0},{3,1},{4,6},{5,7},{6,4},{7,5},{8,10},{9,11},{10,... | collective-permute-start | bytes 3145736 | tf_op jit(solution)/shard_map/ppermute | solution.py:248
  175.1 1.9 copy-start.5
  180.1 66.4 %copy-start.1 = (s32[32,16]{0,1:T(8,128)S(1)}, s32[32,16]{0,1:T(8,128)}, u32[]{:S(2)}) copy-start(s32[32,16]{0,1:T(8,128)} %param.10) | copy-start | bytes 6148
  180.1 40.7 %collective-permute-start.6 = (bf16[8,128,1024]{2,1,0:T(8,128)(2,1)}, bf16[8,128,1024]{2,1,0:T(8,128)(2,1)}, u32[]{:S(2)}, u32[]{:S(2)}) collective-permute-start(bf16[8,128,1024]{2,1,0:T(8,128)(2,1)} %slice.28), channel_id=1, source_target_pairs={{0,8},{8,0},{16,24},{24,16},{32,40},{40,32},{48,56},{56,48},{64,72... | collective-permute-start | bytes 6291464 | tf_op jit(solution)/shard_map/ppermute | solution.py:245
  198.1 22.7 %copy-start.8 = (bf16[2,256,1024]{2,1,0:T(8,128)(2,1)}, bf16[2,256,1024]{2,1,0:T(8,128)(2,1)S(1)}, u32[]{:S(2)}) copy-start(bf16[2,256,1024]{2,1,0:T(8,128)(2,1)S(1)} %collective-permute-done.9.p2) | copy-start | bytes 3145732
  198.1 22.7 %collective-permute-start.10 = (bf16[8,128,1024]{2,1,0:T(8,128)(2,1)}, bf16[8,128,1024]{2,1,0:T(8,128)(2,1)}, u32[]{:S(2)}, u32[]{:S(2)}) collective-permute-start(bf16[8,128,1024]{2,1,0:T(8,128)(2,1)} %collective-permute-done.8.o_cross), channel_id=1, source_target_pairs={{0,8},{8,0},{16,24},{24,16},{32,40},{40,32},{48,56},{56,48},{64,72... | collective-permute-start | bytes 6291464 | tf_op jit(solution)/shard_map/ppermute | solution.py:245
  199.1 47.4 %collective-permute-start.11 = (bf16[4,256,1024]{2,1,0:T(8,128)(2,1)}, bf16[4,256,1024]{2,1,0:T(8,128)(2,1)S(1)}, u32[]{:S(2)}, u32[]{:S(2)}) collective-permute-start(bf16[4,256,1024]{2,1,0:T(8,128)(2,1)} %pad_maximum_fusion.1), channel_id=1, source_target_pairs={{0,4},{1,5},{2,6},{3,7},{4,0},{5,1},{6,2},{7,3},{8,12},{9,13},{10,... | collective-permute-start | bytes 6291464 | tf_op jit(solution)/shard_map/ppermute | solution.py:242

commit v6 on v4

--- a/solution.py
+++ b/solution.py
@@ -142,10 +142,6 @@
     sources = pl.ds(0, 8)
     a_near = pl.ds(pl.multiple_of(a_half * 8, 8), 8)
     a_far = pl.ds(pl.multiple_of(8 - a_half * 8, 8), 8)
-    fetch(near_a.at[sources, pl.ds(pl.multiple_of(core * 128, 128), 128)], left_v.at[0, core, a_near])
-    fetch(near_a.at[sources, pl.ds(pl.multiple_of(128 - core * 128, 128), 128)], left_v.at[1, 1 - core, a_near])
-    fetch(near_a.at[sources, pl.ds(256, 128)], left_v.at[1, core, a_near])
-    fetch(o_near, left_v.at[0, 1 - core, a_near])
     for hop, near in enumerate((r0, r1, r2, r3)):
         place = (here - hop + 4) % 4
         fetch(near.at[pl.ds(0, 3)], b_v.at[:, pl.ds(pl.multiple_of((b_half * 4 + place) * 256, 256), 256)])
@@ -155,29 +151,33 @@
         base = here if hop == 0 else 0
         fetch(far.at[base], b_v.at[0, rows])
         fetch(far.at[base + 1], b_v.at[2, rows])
+    fetch(near_a.at[sources, pl.ds(pl.multiple_of(core * 128, 128), 128)], left_v.at[0, core, a_near])
     fetch(e_far.at[sources, :, group(core)], left_v.at[0, core, a_far])
+    fetch(near_a.at[sources, pl.ds(256, 128)], left_v.at[1, core, a_near])
+    fetch(o_cross, left_v.at[1, core, a_far])
+    ready = len(copies)
+    fetch(o_near, left_v.at[0, 1 - core, a_near])
+    fetch(o_swap, left_v.at[0, 1 - core, a_far])
+    fetch(near_a.at[sources, pl.ds(pl.multiple_of(128 - core * 128, 128), 128)], left_v.at[1, 1 - core, a_near])
     fetch(e_far.at[sources, :, group(1 - core)], left_v.at[1, 1 - core, a_far])
-    fetch(o_cross, left_v.at[1, core, a_far])
-    fetch(o_swap, left_v.at[0, 1 - core, a_far])
-    for copy in copies:
-        copy.wait()
     later = []
-    for t in range(2):
+    near_rows = pl.ds(pl.multiple_of(b_half * W, W), W)
+    near_pieces = pl.ds(pl.multiple_of(b_half * 8, 8), 8)
+    for turn, t in enumerate((core, 1 - core)):
+        for copy in copies[turn * ready:ready + turn * 4]:
+            copy.wait()
         for hop in range(4):
             place = (here - hop + 4) % 4
             part = pltpu.make_async_copy(
                 left_v.at[1, t, pl.ds((1 - b_half) * 8 + place * 2, 2)],
-                left_out.at[t, pl.ds(hop * 2, 2)], out_sem.at[t * 4 + hop])
+                left_out.at[t, pl.ds(hop * 2, 2)], out_sem.at[turn * 4 + hop])
             part.start()
             later.append(part)
-    near_rows = pl.ds(pl.multiple_of(b_half * W, W), W)
-    near_pieces = pl.ds(pl.multiple_of(b_half * 8, 8), 8)
-    for t in range(2):
         for m in range(4):
             cols = slice(m * 256, (m + 1) * 256)
             total = product(left_v[0, t, :, :, cols].reshape(2 * W, 256), b_v[2 * t])
             total += product(left_v[1, t, near_pieces, :, cols].reshape(W, 256), b_v[1, near_rows])
-            out[t * W + m * 256:t * W + (m + 1) * 256, :] = total
+            out[pl.ds(pl.multiple_of(t * W + m * 256, 256), 256), :] = total
     for part in later:
         part.wait()
 
@@ -267,12 +267,13 @@
     o_cross = swap_z_hi(o_send)
     o_near = swap_core(near_a[:, 256:384])
 
+    e_far = along_y(jnp.stack([a_cross[:4], a_cross[1:]], axis=1).reshape(8, 128, 2 * W))
     far = [lax.dynamic_slice_in_dim(b_cross, (here + hop) % 4, 2, 0) for hop in range(1, 4)]
-    a_cross, *far = lax.optimization_barrier((a_cross, *far))
-    p1, p2, p3 = along_x(far[0], 1), along_x(far[1], 2), along_x(far[2], 3)
-    e_far = along_y(jnp.stack([a_cross[:4], a_cross[1:]], axis=1).reshape(8, 128, 2 * W))
-
-    q_send, o_cross, p1, p2, p3 = lax.optimization_barrier((q_send, o_cross, p1, p2, p3))
+    p1, p3 = along_x(far[0], 1), along_x(far[2], 3)
+    p2_send, p1, p3 = lax.optimization_barrier((far[1], p1, p3))
+    p2 = along_x(p2_send, 2)
+
+    q_send, o_cross, p1, p3 = lax.optimization_barrier((q_send, o_cross, p1, p3))
     q = swap_z_lo(q_send)
     o_swap = swap_core(o_cross)
 

time: 263 us -> 249 us (0.947)
  waiting for transfers between devices: 168 us -> 157 us
  local copies, waits for them, and re-layouts: 18.2 us -> 14.7 us
    ppermute x2, waiting for transfers between devices: 36.7 us -> 16.2 us  [swap_z_lo(): return lax.ppermute(value, 'col', [(i, i ^ 4) for i in range(8)])]
    ppermute x2, waiting for transfers between devices: 0.01 us -> 7.2 us  [swap_z_hi(): return lax.ppermute(value, 'row', [(i, i ^ 8) for i in range(16)])]
    ppermute x6, waiting for transfers between devices: 127 us -> 134 us  [along_x(): lax.ppermute(value, 'col', [(i, i // 4 * 4 + (i % 4 + hop) % 4) for i in...]
    ppermute x2, waiting for transfers between devices: 4.11 us -> 0.01 us  [swap_core(): return lax.ppermute(value, 'row', [(i, i ^ 1) for i in range(16)])]
    slice x4, local copies, waits for them, and re-layouts: 4.31 us -> 1.18 us  [on_device(): q_send = jnp.concatenate([v[3:4] for v in (x0, r1, r2, r3)], axis=0)]
  transfers between devices with their start and end apart: 14 -> 14, of which waited for: 8 -> 7; matrix products, arithmetic and copies ran while one was open for 7% -> 5% of each run, Pallas kernels for 9% -> 9%
where the time goes in v6:
time: 249 us; the launch traced here: 248 us
  waiting for transfers between devices  157 us (63%)
  Pallas kernels  43 us (17%)
  starting transfers between devices  30.7 us (12%)
  local copies, waits for them, and re-layouts  14.7 us (6%)
    ppermute x6, waiting for transfers between devices, along_x(): lax.ppermute(value, 'col', [(i, i // 4 * 4 + (i % 4 + hop) % 4) for i in...  134 us
    pallas_call x1, Pallas kernels, on_device(): pl.pallas_call(multiply, out_shape=[pltpu.VMEM((2 * W, W), jnp.float32),...  21.3 us
    ppermute x2, waiting for transfers between devices, swap_z_lo(): return lax.ppermute(value, 'col', [(i, i ^ 4) for i in range(8)])  16.2 us
    pallas_call x1, Pallas kernels, on_device(): pl.pallas_call(prep, out_shape=[bf16(8, 512, W), bf16(5, 128, 2 * W)] + [...  13.8 us
    all_to_all x2, starting transfers between devices, along_y(): lax.all_to_all(value, 'row', 0, 0, axis_index_groups=Y_GROUPS, tiled=True)  12.9 us
    ppermute x6, starting transfers between devices, along_x(): lax.ppermute(value, 'col', [(i, i // 4 * 4 + (i % 4 + hop) % 4) for i in...  8.28 us
    pallas_call x1, Pallas kernels, on_device(): pl.pallas_call(finish, out_shape=jax.ShapeDtypeStruct((2 * W, W), jnp.flo...  7.85 us
    ppermute x2, waiting for transfers between devices, swap_z_hi(): return lax.ppermute(value, 'row', [(i, i ^ 8) for i in range(16)])  7.2 us
  transfers between devices with their start and end apart: 14, of which 7 were waited for; matrix products, arithmetic and copies ran while one was open for 5% of the time, Pallas kernels for 9%

profile of v6, /device:TPU:1, one launch (start us, length us, event | category | flops | bytes accessed | tf_op | source)
XLA Modules:
  0.0 248.0 jit_solution(12188349480686749088)
XLA Ops:
  0.0 0.1 pad_add_fusion.ids
  0.1 0.7 copy-done
  0.8 0.7 copy-done.1
  1.5 0.7 copy-done.3
  2.2 13.8 %prep.1 = (bf16[8,512,1024]{2,1,0:T(8,128)(2,1)}, bf16[5,128,2048]{2,1,0:T(8,128)(2,1)}, bf16[4,256,1024]{2,1,0:T(8,128)(2,1)}, bf16[4,256,1024]{2,1,0:T(8,128)(...) custom-call(s32[2]{0:T(128)S(1)} %pad_add_fusion.ids, ...), custom_call_target="tpu_custom_call" | custom-call | tf_op jit(solution)/shard_map/prep/pallas_call | solution.py:245
  16.0 6.4 %all-to-all-start = ((bf16[8,512,1024]{2,1,0:T(8,128)(2,1)}), bf16[8,512,1024]{2,1,0:T(8,128)(2,1)}, u32[]{:S(2)}, u32[]{:S(2)}) async-start(bf16[8,512,1024]{2,1,0:T(8,128)(2,1)} %get-tuple-element.31), calls=%async_computation | async-start | bytes 16777216 | tf_op jit(solution)/shard_map/all_to_all | solution.py:243
  22.3 1.3 collective-permute-start.2
  23.7 1.5 collective-permute-start.3
  25.1 3.4 %collective-permute-start = (bf16[5,128,2048]{2,1,0:T(8,128)(2,1)}, bf16[5,128,2048]{2,1,0:T(8,128)(2,1)}, u32[]{:S(2)}, u32[]{:S(2)}) collective-permute-start(bf16[5,128,2048]{2,1,0:T(8,128)(2,1)} %get-tuple-element.29), channel_id=1, source_target_pairs={{0,64},{8,72},{16,80},{24,88},{32,96},{40,104},{48,112},{56,120},{... | collective-permute-start | bytes 7864328 | tf_op jit(solution)/shard_map/ppermute | solution.py:231
  28.6 0.6 collective-permute-start.1
  29.2 42.0 %collective-permute-done.2.r1 = bf16[4,256,1024]{2,1,0:T(8,128)(2,1)S(1)} collective-permute-done((bf16[4,256,1024]{2,1,0:T(8,128)(2,1)}, bf16[4,256,1024]{2,1,0:T(8,128)(2,1)S(1)}, u32[]{:S(2)}, u32[]{:S(2)}) %collective-permute-start.2) | collective-permute-done | bytes 2097184 | tf_op jit(solution)/shard_map/ppermute | solution.py:240
  71.2 0.0 collective-permute-done.3.r3
  71.2 2.1 collective-permute-start.4
  73.4 1.1 slice.25
  74.4 0.0 copy-done.5
  74.5 0.0 copy-done.6
  74.5 44.9 %collective-permute-done.4.r2 = bf16[4,256,1024]{2,1,0:T(8,128)(2,1)S(1)} collective-permute-done((bf16[4,256,1024]{2,1,0:T(8,128)(2,1)}, bf16[4,256,1024]{2,1,0:T(8,128)(2,1)S(1)}, u32[]{:S(2)}, u32[]{:S(2)}) %collective-permute-start.4) | collective-permute-done | bytes 2097184 | tf_op jit(solution)/shard_map/ppermute | solution.py:240
  119.5 1.3 copy-done.7
  120.9 1.6 pad_maximum_fusion.1
  122.5 0.0 all-to-all-done.near_a
  122.5 3.1 %slice.32 = bf16[8,128,1024]{2,1,0:T(8,128)(2,1)} slice(bf16[8,512,1024]{2,1,0:T(8,128)(2,1)} %all-to-all-done.near_a), slice={[0:8], [384:512], [0:1024]} | slice | bytes 4194304 | tf_op jit(solution)/shard_map/slice | solution.py:264
  125.5 0.0 collective-permute-done
  125.5 16.2 %collective-permute-done.1.p0 = bf16[5,256,1024]{2,1,0:T(8,128)(2,1)S(1)} collective-permute-done((bf16[5,256,1024]{2,1,0:T(8,128)(2,1)}, bf16[5,256,1024]{2,1,0:T(8,128)(2,1)S(1)}, u32[]{:S(2)}, u32[]{:S(2)}) %collective-permute-start.1) | collective-permute-done | bytes 2621472 | tf_op jit(solution)/shard_map/ppermute | solution.py:234
  141.8 1.2 collective-permute-start.6
  143.0 2.6 %slice_bitcast_fusion.1 = (bf16[4,1,128,2048]{3,2,0,1:T(8,128)(2,1)S(1)}, bf16[4,1,128,2048]{3,2,0,1:T(8,128)(2,1)S(1)}) fusion(bf16[5,128,2048]{2,1,0:T(8,128)(2,1)} %collective-permute-done), kind=kLoop, calls=%fused_computation.3 | loop fusion | bytes 8388608 | tf_op jit(solution)/shard_map/stack | solution.py:270
  145.6 0.4 pad_maximum_fusion
  146.0 2.3 copy.7
  148.3 6.5 %all-to-all-start.1 = ((bf16[8,128,2048]{2,1,0:T(8,128)(2,1)}), bf16[8,128,2048]{2,1,0:T(8,128)(2,1)}, u32[]{:S(2)}, u32[]{:S(2)}) async-start(bf16[8,128,2048]{2,1,0:T(8,128)(2,1)} %bitcast.11), calls=%async_computation.1 | async-start | bytes 8388608 | tf_op jit(solution)/shard_map/all_to_all | solution.py:243
  154.8 0.0 copy-done.4
  154.8 0.4 constant_dynamic-slice_fusion
  155.2 1.1 collective-permute-start.8
  156.3 0.4 collective-permute-start.7
  156.7 1.8 slice.31
  158.5 0.9 collective-permute-start.5
  159.3 20.6 %collective-permute-done.8.p3 = bf16[2,256,1024]{2,1,0:T(8,128)(2,1)S(1)} collective-permute-done((bf16[2,256,1024]{2,1,0:T(8,128)(2,1)S(1)}, bf16[2,256,1024]{2,1,0:T(8,128)(2,1)S(1)}, u32[]{:S(2)}, u32[]{:S(2)}) %collective-permute-start.8) | collective-permute-done | bytes 1048608 | tf_op jit(solution)/shard_map/ppermute | solution.py:240
  179.9 1.9 collective-permute-done.7.p1
  181.9 7.2 %collective-permute-done.6.o_cross = bf16[8,128,1024]{2,1,0:T(8,128)(2,1)} collective-permute-done((bf16[8,128,1024]{2,1,0:T(8,128)(2,1)}, bf16[8,128,1024]{2,1,0:T(8,128)(2,1)}, u32[]{:S(2)}, u32[]{:S(2)}) %collective-permute-start.6) | collective-permute-done | bytes 2097184 | tf_op jit(solution)/shard_map/ppermute | solution.py:231
  189.1 0.0 copy-done.9
  189.1 2.6 %collective-permute-start.9 = (bf16[8,128,1024]{2,1,0:T(8,128)(2,1)}, bf16[8,128,1024]{2,1,0:T(8,128)(2,1)}, u32[]{:S(2)}, u32[]{:S(2)}) collective-permute-start(bf16[8,128,1024]{2,1,0:T(8,128)(2,1)} %collective-permute-done.6.o_cross), channel_id=1, source_target_pairs={{0,8},{8,0},{16,24},{24,16},{32,40},{40,32},{48,56},{56,48},{64,72... | collective-permute-start | bytes 6291464 | tf_op jit(solution)/shard_map/ppermute | solution.py:237
  191.6 0.8 collective-permute-start.11
  192.5 1.8 collective-permute-start.10
  194.3 24.3 %collective-permute-done.10.p2 = bf16[2,256,1024]{2,1,0:T(8,128)(2,1)} collective-permute-done((bf16[2,256,1024]{2,1,0:T(8,128)(2,1)S(1)}, bf16[2,256,1024]{2,1,0:T(8,128)(2,1)}, u32[]{:S(2)}, u32[]{:S(2)}) %collective-permute-start.10) | collective-permute-done | bytes 1048608 | tf_op jit(solution)/shard_map/ppermute | solution.py:240
  218.6 0.0 collective-permute-done.5.o_near
  218.6 0.0 all-to-all-done.1.e_far
  218.6 0.0 collective-permute-done.9.o_swap
  218.6 21.3 %multiply.1 = (f32[2048,1024]{1,0:T(8,128)S(1)}, bf16[2,8,128,1024]{3,2,1,0:T(8,128)(2,1)S(1)}) custom-call(s32[2]{0:T(128)S(1)} %pad_add_fusion.ids, bf16[8,512,1024]{2,1,0:T(8,128)(2,1)} %all-to-all-done.near_a, bf16[8,128,2048]{2,1,0:T(8,128)(2,1)} %all-to-all-done.1.e_far, bf16[8,128,1024]{2,1,0:T(8,128)(2,1)} %collective-permute-done.5.o_near, ...), custom_call_target="tpu_custom_call" | custom-call | tf_op jit(solution)/shard_map/multiply/pallas_call | solution.py:280
  239.9 0.0 collective-permute-done.11.right
  239.9 7.9 %finish.1 = f32[2048,1024]{1,0:T(8,128)} custom-call(s32[16,32]{1,0:T(8,128)S(1)} %bitcast.10, f32[2048,1024]{1,0:T(8,128)S(1)} %get-tuple-element.50.part, bf16[2,8,128,1024]{3,2,1,0:T(8,128)(2,1)S(1)} %get-tuple-element.51.left, bf16[4,256,1024]{2,1,0:T(8,128)(2,1)S(1)} %collective-permute-done.11.right), custom_call_target="tpu_custom_call" | custom-call | tf_op jit(solution)/shard_map/finish/pallas_call | solution.py:290
  (15 shorter events, 0.1 us)
Async XLA Ops:
  0.1 0.7 copy-start
  0.8 0.7 copy-start.1
  1.5 0.7 copy-start.3
  16.0 106.5 %all-to-all-start = ((bf16[8,512,1024]{2,1,0:T(8,128)(2,1)}), bf16[8,512,1024]{2,1,0:T(8,128)(2,1)}, u32[]{:S(2)}, u32[]{:S(2)}) async-start(bf16[8,512,1024]{2,1,0:T(8,128)(2,1)} %get-tuple-element.31), calls=%async_computation | async-start | bytes 16777216 | tf_op jit(solution)/shard_map/all_to_all | solution.py:243
  22.3 48.9 %collective-permute-start.2 = (bf16[4,256,1024]{2,1,0:T(8,128)(2,1)}, bf16[4,256,1024]{2,1,0:T(8,128)(2,1)S(1)}, u32[]{:S(2)}, u32[]{:S(2)}) collective-permute-start(bf16[4,256,1024]{2,1,0:T(8,128)(2,1)} %get-tuple-element.34), channel_id=1, source_target_pairs={{0,1},{1,2},{2,3},{3,0},{4,5},{5,6},{6,7},{7,4},{8,9},{9,10},{10,1... | collective-permute-start | bytes 6291464 | tf_op jit(solution)/shard_map/ppermute | solution.py:240
  23.7 47.5 %collective-permute-start.3 = (bf16[4,256,1024]{2,1,0:T(8,128)(2,1)}, bf16[4,256,1024]{2,1,0:T(8,128)(2,1)S(1)}, u32[]{:S(2)}, u32[]{:S(2)}) collective-permute-start(bf16[4,256,1024]{2,1,0:T(8,128)(2,1)} %get-tuple-element.35), channel_id=1, source_target_pairs={{0,3},{1,0},{2,1},{3,2},{4,7},{5,4},{6,5},{7,6},{8,11},{9,8},{10,9... | collective-permute-start | bytes 6291464 | tf_op jit(solution)/shard_map/ppermute | solution.py:240
  25.1 100.4 %collective-permute-start = (bf16[5,128,2048]{2,1,0:T(8,128)(2,1)}, bf16[5,128,2048]{2,1,0:T(8,128)(2,1)}, u32[]{:S(2)}, u32[]{:S(2)}) collective-permute-start(bf16[5,128,2048]{2,1,0:T(8,128)(2,1)} %get-tuple-element.29), channel_id=1, source_target_pairs={{0,64},{8,72},{16,80},{24,88},{32,96},{40,104},{48,112},{56,120},{... | collective-permute-start | bytes 7864328 | tf_op jit(solution)/shard_map/ppermute | solution.py:231
  28.6 113.2 %collective-permute-start.1 = (bf16[5,256,1024]{2,1,0:T(8,128)(2,1)}, bf16[5,256,1024]{2,1,0:T(8,128)(2,1)S(1)}, u32[]{:S(2)}, u32[]{:S(2)}) collective-permute-start(bf16[5,256,1024]{2,1,0:T(8,128)(2,1)} %get-tuple-element.30), channel_id=1, source_target_pairs={{0,4},{1,5},{2,6},{3,7},{4,0},{5,1},{6,2},{7,3},{8,12},{9,13},{10,... | collective-permute-start | bytes 7864328 | tf_op jit(solution)/shard_map/ppermute | solution.py:234
  71.2 3.2 %copy-start.5 = (bf16[4,256,1024]{2,1,0:T(8,128)(2,1)}, bf16[4,256,1024]{2,1,0:T(8,128)(2,1)S(1)}, u32[]{:S(2)}) copy-start(bf16[4,256,1024]{2,1,0:T(8,128)(2,1)S(1)} %collective-permute-done.2.r1) | copy-start | bytes 6291460
  71.2 3.3 %copy-start.6 = (bf16[4,256,1024]{2,1,0:T(8,128)(2,1)}, bf16[4,256,1024]{2,1,0:T(8,128)(2,1)S(1)}, u32[]{:S(2)}) copy-start(bf16[4,256,1024]{2,1,0:T(8,128)(2,1)S(1)} %collective-permute-done.3.r3) | copy-start | bytes 6291460
  71.2 48.2 %collective-permute-start.4 = (bf16[4,256,1024]{2,1,0:T(8,128)(2,1)}, bf16[4,256,1024]{2,1,0:T(8,128)(2,1)S(1)}, u32[]{:S(2)}, u32[]{:S(2)}) collective-permute-start(bf16[4,256,1024]{2,1,0:T(8,128)(2,1)} %get-tuple-element.37), channel_id=1, source_target_pairs={{0,2},{1,3},{2,0},{3,1},{4,6},{5,7},{6,4},{7,5},{8,10},{9,11},{10,... | collective-permute-start | bytes 6291464 | tf_op jit(solution)/shard_map/ppermute | solution.py:240
  119.5 1.4 copy-start.7
  141.8 13.0 %copy-start.4 = (bf16[5,256,1024]{2,1,0:T(8,128)(2,1)}, bf16[5,256,1024]{2,1,0:T(8,128)(2,1)S(1)}, u32[]{:S(2)}) copy-start(bf16[5,256,1024]{2,1,0:T(8,128)(2,1)S(1)} %collective-permute-done.1.p0) | copy-start | bytes 7864324
  141.8 47.3 %collective-permute-start.6 = (bf16[8,128,1024]{2,1,0:T(8,128)(2,1)}, bf16[8,128,1024]{2,1,0:T(8,128)(2,1)}, u32[]{:S(2)}, u32[]{:S(2)}) collective-permute-start(bf16[8,128,1024]{2,1,0:T(8,128)(2,1)} %slice.32), channel_id=1, source_target_pairs={{0,64},{8,72},{16,80},{24,88},{32,96},{40,104},{48,112},{56,120},{... | collective-permute-start | bytes 6291464 | tf_op jit(solution)/shard_map/ppermute | solution.py:231
  148.3 70.3 %all-to-all-start.1 = ((bf16[8,128,2048]{2,1,0:T(8,128)(2,1)}), bf16[8,128,2048]{2,1,0:T(8,128)(2,1)}, u32[]{:S(2)}, u32[]{:S(2)}) async-start(bf16[8,128,2048]{2,1,0:T(8,128)(2,1)} %bitcast.11), calls=%async_computation.1 | async-start | bytes 8388608 | tf_op jit(solution)/shard_map/all_to_all | solution.py:243
  155.2 24.7 %collective-permute-start.8 = (bf16[2,256,1024]{2,1,0:T(8,128)(2,1)S(1)}, bf16[2,256,1024]{2,1,0:T(8,128)(2,1)S(1)}, u32[]{:S(2)}, u32[]{:S(2)}) collective-permute-start(bf16[2,256,1024]{2,1,0:T(8,128)(2,1)S(1)} %get-tuple-element.53), channel_id=1, source_target_pairs={{0,3},{1,0},{2,1},{3,2},{4,7},{5,4},{6,5},{7,6},{8,11},{9,8},{10,9... | collective-permute-start | bytes 3145736 | tf_op jit(solution)/shard_map/ppermute | solution.py:240
  156.3 25.6 %collective-permute-start.7 = (bf16[2,256,1024]{2,1,0:T(8,128)(2,1)S(1)}, bf16[2,256,1024]{2,1,0:T(8,128)(2,1)S(1)}, u32[]{:S(2)}, u32[]{:S(2)}) collective-permute-start(bf16[2,256,1024]{2,1,0:T(8,128)(2,1)S(1)} %get-tuple-element.54), channel_id=1, source_target_pairs={{0,1},{1,2},{2,3},{3,0},{4,5},{5,6},{6,7},{7,4},{8,9},{9,10},{10,1... | collective-permute-start | bytes 3145736 | tf_op jit(solution)/shard_map/ppermute | solution.py:240
  158.5 60.1 %collective-permute-start.5 = (bf16[8,128,1024]{2,1,0:T(8,128)(2,1)S(1)}, bf16[8,128,1024]{2,1,0:T(8,128)(2,1)}, u32[]{:S(2)}, u32[]{:S(2)}) collective-permute-start(bf16[8,128,1024]{2,1,0:T(8,128)(2,1)S(1)} %slice.31), channel_id=1, source_target_pairs={{0,8},{8,0},{16,24},{24,16},{32,40},{40,32},{48,56},{56,48},{64,72... | collective-permute-start | bytes 6291464 | tf_op jit(solution)/shard_map/ppermute | solution.py:237
  179.9 2.0 copy-start.8
  181.9 7.2 %copy-start.9 = (bf16[2,256,1024]{2,1,0:T(8,128)(2,1)}, bf16[2,256,1024]{2,1,0:T(8,128)(2,1)S(1)}, u32[]{:S(2)}) copy-start(bf16[2,256,1024]{2,1,0:T(8,128)(2,1)S(1)} %collective-permute-done.7.p1) | copy-start | bytes 3145732
  181.9 58.1 %copy-start.2 = (s32[32,16]{0,1:T(8,128)S(1)}, s32[32,16]{0,1:T(8,128)}, u32[]{:S(2)}) copy-start(s32[32,16]{0,1:T(8,128)} %param.10) | copy-start | bytes 6148
  189.1 29.5 %collective-permute-start.9 = (bf16[8,128,1024]{2,1,0:T(8,128)(2,1)}, bf16[8,128,1024]{2,1,0:T(8,128)(2,1)}, u32[]{:S(2)}, u32[]{:S(2)}) collective-permute-start(bf16[8,128,1024]{2,1,0:T(8,128)(2,1)} %collective-permute-done.6.o_cross), channel_id=1, source_target_pairs={{0,8},{8,0},{16,24},{24,16},{32,40},{40,32},{48,56},{56,48},{64,72... | collective-permute-start | bytes 6291464 | tf_op jit(solution)/shard_map/ppermute | solution.py:237
  191.6 48.3 %collective-permute-start.11 = (bf16[4,256,1024]{2,1,0:T(8,128)(2,1)}, bf16[4,256,1024]{2,1,0:T(8,128)(2,1)S(1)}, u32[]{:S(2)}, u32[]{:S(2)}) collective-permute-start(bf16[4,256,1024]{2,1,0:T(8,128)(2,1)} %pad_maximum_fusion.1), channel_id=1, source_target_pairs={{0,4},{1,5},{2,6},{3,7},{4,0},{5,1},{6,2},{7,3},{8,12},{9,13},{10,... | collective-permute-start | bytes 6291464 | tf_op jit(solution)/shard_map/ppermute | solution.py:234
  192.5 26.1 %collective-permute-start.10 = (bf16[2,256,1024]{2,1,0:T(8,128)(2,1)S(1)}, bf16[2,256,1024]{2,1,0:T(8,128)(2,1)}, u32[]{:S(2)}, u32[]{:S(2)}) collective-permute-start(bf16[2,256,1024]{2,1,0:T(8,128)(2,1)S(1)} %get-tuple-element.48), channel_id=1, source_target_pairs={{0,2},{1,3},{2,0},{3,1},{4,6},{5,7},{6,4},{7,5},{8,10},{9,11},{10,... | collective-permute-start | bytes 3145736 | tf_op jit(solution)/shard_map/ppermute | solution.py:240

commit v7 on v5

--- a/solution.py
+++ b/solution.py
@@ -9,6 +9,7 @@
 KB = 32
 NP = 16
 W = 1024
+EARLY = 2
 MIB = 1 << 20
 Y_GROUPS = [list(range(8)), list(range(8, 16))]
 
@@ -26,7 +27,7 @@
     return pltpu.make_async_copy(src.at[rows], dst.at[rows], sem)
 
 
-def prep_a(ids, kdist, mask_a, at, to_y, a_z, to_odd, wide_a, held_a, in_sems, sems):
+def prep_a(ids, kdist, mask_a, at, to_y, a_z, wide_a, held_a, in_sems, sems):
     row_id, col_id = ids[0], ids[1]
     a_half = row_id // 8
     for n in range(8):
@@ -50,13 +51,9 @@
             odd = tile % 2 == 1
             even = tile % 2 == 0
             first = jnp.where(odd, tile // 2 % 4 * 2 + t, near)
-            first_row = jnp.where(odd, 256, t * 128) + slot
-
-            @pl.when(odd & (near >= 8))
-            def _():
-                pltpu.make_async_copy(src, to_odd.at[first, inner, :], sems.at[2]).start()
-
-            @pl.when(near < 8)
+            first_row = jnp.where(odd, jnp.where(tile // 8 == a_half, 256, 384), t * 128) + slot
+
+            @pl.when(odd | (near < 8))
             def _():
                 dst = to_y.at[first, pl.ds(pl.multiple_of(first_row, BS), BS), :]
                 pltpu.make_async_copy(src, dst, sems.at[0]).start()
@@ -70,16 +67,22 @@
             def _():
                 pltpu.make_async_copy(src, a_z.at[far // 2, inner, cols], sems.at[1]).start()
 
-    for n, ref in enumerate((to_y, a_z, to_odd)):
+    for n, ref in enumerate((to_y, a_z)):
         pltpu.make_async_copy(ref, ref, sems.at[n]).wait()
 
 
-def prep_b(ids, kdist, mask_b, bmat, x0, x1, x2, x3, b_z, wide_b, held_b, in_sems, sems):
+def prep_b(ids, kdist_in, mask_in, bmat, x0, x1, x2, x3, b_early, b_rest,
+           kdist, mask_b, wide_b, held_b, in_sems, sems):
+    small = [pltpu.make_async_copy(mask_in, mask_b, in_sems.at[8]), pltpu.make_async_copy(kdist_in, kdist, in_sems.at[9])]
+    for copy in small:
+        copy.start()
     row_id, col_id = ids[0], ids[1]
     b_half, here = col_id // 4, col_id % 4
     to_x = (x0, x1, x2, x3)
     for n in range(8):
         load(bmat, held_b, n, in_sems.at[n]).start()
+    for copy in small:
+        copy.wait()
     wide_b[...] = spread(mask_b[...], W)
     for block in range(2 * KB):
         if block % 8 == 0:
@@ -116,11 +119,15 @@
         def _():
             send(second, 2)
 
-        @pl.when(even & (far <= 8))
+        @pl.when(even & (far < 2 * EARLY))
         def _():
-            pltpu.make_async_copy(src, b_z.at[far // 2, inner, :], sems.at[4]).start()
-
-    for n, ref in enumerate((x0, x1, x2, x3, b_z)):
+            pltpu.make_async_copy(src, b_early.at[far // 2, inner, :], sems.at[4]).start()
+
+        @pl.when(even & (far >= 2 * EARLY) & (far <= 8))
+        def _():
+            pltpu.make_async_copy(src, b_rest.at[far // 2 - EARLY, inner, :], sems.at[5]).start()
+
+    for n, ref in enumerate((x0, x1, x2, x3, b_early, b_rest)):
         pltpu.make_async_copy(ref, ref, sems.at[n]).wait()
 
 
@@ -150,10 +157,6 @@
     sources = pl.ds(0, 8)
     a_near = pl.ds(pl.multiple_of(a_half * 8, 8), 8)
     a_far = pl.ds(pl.multiple_of(8 - a_half * 8, 8), 8)
-    fetch(near_a.at[sources, pl.ds(pl.multiple_of(core * 128, 128), 128)], left_v.at[0, core, a_near])
-    fetch(near_a.at[sources, pl.ds(pl.multiple_of(128 - core * 128, 128), 128)], left_v.at[1, 1 - core, a_near])
-    fetch(near_a.at[sources, pl.ds(256, 128)], left_v.at[1, core, a_near])
-    fetch(o_near, left_v.at[0, 1 - core, a_near])
     for hop, near in enumerate((r0, r1, r2, r3)):
         place = (here - hop + 4) % 4
         fetch(near.at[pl.ds(0, 3)], b_v.at[:, pl.ds(pl.multiple_of((b_half * 4 + place) * 256, 256), 256)])
@@ -163,29 +166,33 @@
         base = here if hop == 0 else 0
         fetch(far.at[base], b_v.at[0, rows])
         fetch(far.at[base + 1], b_v.at[2, rows])
+    fetch(near_a.at[sources, pl.ds(pl.multiple_of(core * 128, 128), 128)], left_v.at[0, core, a_near])
     fetch(e_far.at[sources, :, group(core)], left_v.at[0, core, a_far])
+    fetch(near_a.at[sources, pl.ds(256, 128)], left_v.at[1, core, a_near])
+    fetch(o_cross, left_v.at[1, core, a_far])
+    ready = len(copies)
+    fetch(o_near, left_v.at[0, 1 - core, a_near])
+    fetch(o_swap, left_v.at[0, 1 - core, a_far])
+    fetch(near_a.at[sources, pl.ds(pl.multiple_of(128 - core * 128, 128), 128)], left_v.at[1, 1 - core, a_near])
     fetch(e_far.at[sources, :, group(1 - core)], left_v.at[1, 1 - core, a_far])
-    fetch(o_cross, left_v.at[1, core, a_far])
-    fetch(o_swap, left_v.at[0, 1 - core, a_far])
-    for copy in copies:
-        copy.wait()
     later = []
-    for t in range(2):
+    near_rows = pl.ds(pl.multiple_of(b_half * W, W), W)
+    near_pieces = pl.ds(pl.multiple_of(b_half * 8, 8), 8)
+    for turn, t in enumerate((core, 1 - core)):
+        for copy in copies[turn * ready:ready + turn * 4]:
+            copy.wait()
         for hop in range(4):
             place = (here - hop + 4) % 4
             part = pltpu.make_async_copy(
                 left_v.at[1, t, pl.ds((1 - b_half) * 8 + place * 2, 2)],
-                left_out.at[t, pl.ds(hop * 2, 2)], out_sem.at[t * 4 + hop])
+                left_out.at[t, pl.ds(hop * 2, 2)], out_sem.at[turn * 4 + hop])
             part.start()
             later.append(part)
-    near_rows = pl.ds(pl.multiple_of(b_half * W, W), W)
-    near_pieces = pl.ds(pl.multiple_of(b_half * 8, 8), 8)
-    for t in range(2):
         for m in range(4):
             cols = slice(m * 256, (m + 1) * 256)
             total = product(left_v[0, t, :, :, cols].reshape(2 * W, 256), b_v[2 * t])
             total += product(left_v[1, t, near_pieces, :, cols].reshape(W, 256), b_v[1, near_rows])
-            out[t * W + m * 256:t * W + (m + 1) * 256, :] = total
+            out[pl.ds(pl.multiple_of(t * W + m * 256, 256), 256), :] = total
     for part in later:
         part.wait()
 
@@ -250,48 +257,52 @@
     def along_y(value):
         return lax.all_to_all(value, "row", 0, 0, axis_index_groups=Y_GROUPS, tiled=True)
 
-    x0, x1, x2, x3, b_z = pl.pallas_call(
+    x0, x1, x2, x3, b_early, b_rest = pl.pallas_call(
         prep_b,
-        out_shape=[bf16(4, 256, W)] * 4 + [bf16(5, 256, W)],
-        in_specs=[SMEM, SMEM, VMEM, HBM],
-        out_specs=[HBM] * 5,
-        scratch_shapes=[pltpu.VMEM((64, W), jnp.float32), pltpu.VMEM((4096, W), jnp.bfloat16),
-                        pltpu.SemaphoreType.DMA((8,)), pltpu.SemaphoreType.DMA((5,))],
+        out_shape=[bf16(4, 256, W)] * 4 + [bf16(EARLY, 256, W), bf16(5 - EARLY, 256, W)],
+        in_specs=[SMEM, HBM, HBM, HBM],
+        out_specs=[HBM] * 6,
+        scratch_shapes=[pltpu.SMEM((512,), jnp.int32), pltpu.VMEM((16, 64), jnp.int32),
+                        pltpu.VMEM((64, W), jnp.float32), pltpu.VMEM((4096, W), jnp.bfloat16),
+                        pltpu.SemaphoreType.DMA((10,)), pltpu.SemaphoreType.DMA((6,))],
         compiler_params=pltpu.CompilerParams(vmem_limit_bytes=24 * MIB),
         name="prep_b",
-    )(ids, kdist, mask_b.T, *in_hbm(bmat))
-
-    b_cross = swap_z_lo(b_z)
+    )(ids, *in_hbm(kdist, mask_b.T, bmat))
+
+    at, b_early = lax.optimization_barrier((at, b_early))
+    a_y, a_z = pl.pallas_call(
+        prep_a,
+        out_shape=[bf16(8, 512, W), bf16(5, 128, 2 * W)],
+        in_specs=[SMEM, SMEM, VMEM, HBM],
+        out_specs=[HBM] * 2,
+        scratch_shapes=[pltpu.VMEM((32, 2 * W), jnp.float32), pltpu.VMEM((2048, 2 * W), jnp.bfloat16),
+                        pltpu.SemaphoreType.DMA((8,)), pltpu.SemaphoreType.DMA((2,))],
+        compiler_params=pltpu.CompilerParams(vmem_limit_bytes=24 * MIB),
+        name="prep_a",
+    )(ids, kdist, mask_a, *in_hbm(at))
+
+    early = swap_z_lo(b_early)
+    a_y, a_z, early = lax.optimization_barrier((a_y, a_z, early))
+    near_a = along_y(a_y)
+    a_cross = swap_z_hi(a_z)
     r1, r3 = along_x(x1, 1), along_x(x3, 3)
     x2, r1, r3 = lax.optimization_barrier((x2, r1, r3))
     r2 = along_x(x2, 2)
-    at, b_z = lax.optimization_barrier((at, b_z))
-    a_y, a_z, a_odd = pl.pallas_call(
-        prep_a,
-        out_shape=[bf16(8, 384, W), bf16(5, 128, 2 * W), bf16(8, 128, W)],
-        in_specs=[SMEM, SMEM, VMEM, HBM],
-        out_specs=[HBM] * 3,
-        scratch_shapes=[pltpu.VMEM((32, 2 * W), jnp.float32), pltpu.VMEM((2048, 2 * W), jnp.bfloat16),
-                        pltpu.SemaphoreType.DMA((8,)), pltpu.SemaphoreType.DMA((3,))],
-        compiler_params=pltpu.CompilerParams(vmem_limit_bytes=24 * MIB),
-        name="prep_a",
-    )(ids, kdist, mask_a, *in_hbm(at))
-    o_send = along_y(a_odd)
-    a_y, o_send = lax.optimization_barrier((a_y, o_send))
-    near_a = along_y(a_y)
-    a_z, b_cross, r1, r3 = lax.optimization_barrier((a_z, b_cross, r1, r3))
-    a_cross = swap_z_hi(a_z)
+    b_cross = jnp.concatenate([early, swap_z_lo(b_rest)], axis=0)
+
+    o_send = near_a[:, 384:]
+    q_send = jnp.concatenate([v[3:4] for v in (x0, r1, r2, r3)], axis=0)
+    a_cross, b_cross, near_a, o_send, q_send = lax.optimization_barrier((a_cross, b_cross, near_a, o_send, q_send))
+    o_cross = swap_z_hi(o_send)
+    o_near = swap_core(near_a[:, 256:384])
+
+    e_far = along_y(jnp.stack([a_cross[:4], a_cross[1:]], axis=1).reshape(8, 128, 2 * W))
     far = [lax.dynamic_slice_in_dim(b_cross, (here + hop) % 4, 2, 0) for hop in range(1, 4)]
     p1, p3 = along_x(far[0], 1), along_x(far[2], 3)
-
-    o_send, p2_send, a_cross, p1, p3 = lax.optimization_barrier((o_send, far[1], a_cross, p1, p3))
-    o_cross = swap_z_hi(o_send)
+    p2_send, p1, p3 = lax.optimization_barrier((far[1], p1, p3))
     p2 = along_x(p2_send, 2)
-    e_far = along_y(jnp.stack([a_cross[:4], a_cross[1:]], axis=1).reshape(8, 128, 2 * W))
-    o_near = swap_core(near_a[:, 256:])
-
-    q_send = jnp.concatenate([v[3:4] for v in (x0, r1, r2, r3)], axis=0)
-    q_send, o_cross, p2 = lax.optimization_barrier((q_send, o_cross, p2))
+
+    q_send, o_cross, p1, p3 = lax.optimization_barrier((q_send, o_cross, p1, p3))
     q = swap_z_lo(q_send)
     o_swap = swap_core(o_cross)
 

time: 258 us -> 252 us (0.977)
  starting transfers between devices: 49.9 us -> 34.4 us
  waiting for transfers between devices: 142 us -> 155 us
    ppermute x2 -> x3, waiting for transfers between devices: 11.5 us -> 59.2 us  [swap_z_lo(): return lax.ppermute(value, 'col', [(i, i ^ 4) for i in range(8)])]
    all_to_all x3 -> x2, waiting for transfers between devices: 43.4 us -> 0.01 us  [along_y(): lax.all_to_all(value, 'row', 0, 0, axis_index_groups=Y_GROUPS, tiled=True)]
    ppermute x6, waiting for transfers between devices: 60.1 us -> 90.1 us  [along_x(): lax.ppermute(value, 'col', [(i, i // 4 * 4 + (i % 4 + hop) % 4) for i in...]
    ppermute x2, waiting for transfers between devices: 27.3 us -> 5.7 us  [swap_z_hi(): return lax.ppermute(value, 'row', [(i, i ^ 8) for i in range(16)])]
    all_to_all x3 -> x2, starting transfers between devices: 33.6 us -> 12.7 us  [along_y(): lax.all_to_all(value, 'row', 0, 0, axis_index_groups=Y_GROUPS, tiled=True)]
    ppermute x2 -> x3, starting transfers between devices: 2 us -> 4.68 us  [swap_z_lo(): return lax.ppermute(value, 'col', [(i, i ^ 4) for i in range(8)])]
  transfers between devices with their start and end apart: 15 -> 15, of which waited for: 9 -> 7; matrix products, arithmetic and copies ran while one was open for 6% -> 6% of each run, Pallas kernels for 9% -> 11%
where the time goes in v7:
time: 252 us; the launch traced here: 251 us
  waiting for transfers between devices  155 us (62%)
  Pallas kernels  44.2 us (18%)
  starting transfers between devices  34.4 us (14%)
  local copies, waits for them, and re-layouts  13.6 us (5%)
  other arithmetic  3.51 us (1%)
    ppermute x6, waiting for transfers between devices, along_x(): lax.ppermute(value, 'col', [(i, i // 4 * 4 + (i % 4 + hop) % 4) for i in...  90.1 us
    ppermute x3, waiting for transfers between devices, swap_z_lo(): return lax.ppermute(value, 'col', [(i, i ^ 4) for i in range(8)])  59.2 us
    pallas_call x1, Pallas kernels, on_device(): pl.pallas_call(multiply, out_shape=[pltpu.VMEM((2 * W, W), jnp.float32),...  21.4 us
    all_to_all x2, starting transfers between devices, along_y(): lax.all_to_all(value, 'row', 0, 0, axis_index_groups=Y_GROUPS, tiled=True)  12.7 us
    ppermute x6, starting transfers between devices, along_x(): lax.ppermute(value, 'col', [(i, i // 4 * 4 + (i % 4 + hop) % 4) for i in...  8.81 us
    pallas_call x1, Pallas kernels, on_device(): pl.pallas_call(finish, out_shape=jax.ShapeDtypeStruct((2 * W, W), jnp.flo...  7.85 us
    pallas_call x1, Pallas kernels, on_device(): pl.pallas_call(prep_b, out_shape=[bf16(4, 256, W)] * 4 + [bf16(EARLY, 256...  7.55 us
    pallas_call x1, Pallas kernels, on_device(): pl.pallas_call(prep_a, out_shape=[bf16(8, 512, W), bf16(5, 128, 2 * W)],...  7.38 us
  transfers between devices with their start and end apart: 15, of which 7 were waited for; matrix products, arithmetic and copies ran while one was open for 6% of the time, Pallas kernels for 11%

profile of v7, /device:TPU:1, one launch (start us, length us, event | category | flops | bytes accessed | tf_op | source)
XLA Modules:
  0.0 251.1 jit_solution(14992988670467827251)
XLA Ops:
  0.0 0.1 pad_add_fusion.ids
  0.1 7.5 %prep_b.1 = (bf16[4,256,1024]{2,1,0:T(8,128)(2,1)}, bf16[4,256,1024]{2,1,0:T(8,128)(2,1)}, bf16[4,256,1024]{2,1,0:T(8,128)(2,1)}, bf16[4,256,1024]{2,1,0:T(8,128...) custom-call(s32[2]{0:T(128)S(1)} %pad_add_fusion.ids, s32[512]{0:T(512)} %kdist.1, ...), custom_call_target="tpu_custom_call" | custom-call | tf_op jit(solution)/shard_map/prep_b/pallas_call | solution.py:260
  7.6 2.5 collective-permute-start
  10.1 0.0 copy-done
  10.1 7.4 %prep_a.1 = (bf16[8,512,1024]{2,1,0:T(8,128)(2,1)}, bf16[5,128,2048]{2,1,0:T(8,128)(2,1)}) custom-call(s32[2]{0:T(128)S(1)} %pad_add_fusion.ids, s32[512]{0:T(512)S(1)} %copy-done.2, s32[32,32]{1,0:T(8,128)S(1)} %copy-done, bf16[2048,2048]{1,0:T(8,128)(2,1)} %at), custom_call_target="tpu_custom_call" | custom-call | tf_op jit(solution)/shard_map/prep_a/pallas_call | solution.py:273
  17.5 15.6 %collective-permute-done = bf16[2,256,1024]{2,1,0:T(8,128)(2,1)S(1)} collective-permute-done((bf16[2,256,1024]{2,1,0:T(8,128)(2,1)}, bf16[2,256,1024]{2,1,0:T(8,128)(2,1)S(1)}, u32[]{:S(2)}, u32[]{:S(2)}) %collective-permute-start) | collective-permute-done | bytes 1048608 | tf_op jit(solution)/shard_map/ppermute | solution.py:249
  33.1 1.0 copy-done.9
  34.1 6.2 %all-to-all-start = ((bf16[8,512,1024]{2,1,0:T(8,128)(2,1)}), bf16[8,512,1024]{2,1,0:T(8,128)(2,1)}, u32[]{:S(2)}, u32[]{:S(2)}) async-start(bf16[8,512,1024]{2,1,0:T(8,128)(2,1)} %get-tuple-element.43), calls=%async_computation | async-start | bytes 16777216 | tf_op jit(solution)/shard_map/all_to_all | solution.py:258
  40.3 1.2 collective-permute-start.3
  41.6 1.4 collective-permute-start.4
  43.0 3.5 %collective-permute-start.1 = (bf16[5,128,2048]{2,1,0:T(8,128)(2,1)}, bf16[5,128,2048]{2,1,0:T(8,128)(2,1)}, u32[]{:S(2)}, u32[]{:S(2)}) collective-permute-start(bf16[5,128,2048]{2,1,0:T(8,128)(2,1)} %get-tuple-element.40), channel_id=1, source_target_pairs={{0,64},{8,72},{16,80},{24,88},{32,96},{40,104},{48,112},{56,120},{... | collective-permute-start | bytes 7864328 | tf_op jit(solution)/shard_map/ppermute | solution.py:246
  46.5 42.4 %collective-permute-done.3.r1 = bf16[4,256,1024]{2,1,0:T(8,128)(2,1)S(1)} collective-permute-done((bf16[4,256,1024]{2,1,0:T(8,128)(2,1)}, bf16[4,256,1024]{2,1,0:T(8,128)(2,1)S(1)}, u32[]{:S(2)}, u32[]{:S(2)}) %collective-permute-start.3) | collective-permute-done | bytes 2097184 | tf_op jit(solution)/shard_map/ppermute | solution.py:255
  88.9 0.0 collective-permute-done.4.r3
  88.9 2.2 collective-permute-start.5
  91.1 1.5 collective-permute-start.2
  92.6 1.1 slice.25
  93.6 43.6 %collective-permute-done.2 = bf16[3,256,1024]{2,1,0:T(8,128)(2,1)S(1)} collective-permute-done((bf16[3,256,1024]{2,1,0:T(8,128)(2,1)}, bf16[3,256,1024]{2,1,0:T(8,128)(2,1)S(1)}, u32[]{:S(2)}, u32[]{:S(2)}) %collective-permute-start.2) | collective-permute-done | bytes 1572896 | tf_op jit(solution)/shard_map/ppermute | solution.py:249
  137.3 1.5 pad_maximum_fusion.1.p0
  138.8 0.0 slice-start
  138.8 0.0 collective-permute-done.5.r2
  138.8 1.3 copy-done.6
  140.2 1.6 pad_maximum_fusion.2
  141.8 0.0 all-to-all-done.near_a
  141.8 3.1 %slice.32 = bf16[8,128,1024]{2,1,0:T(8,128)(2,1)} slice(bf16[8,512,1024]{2,1,0:T(8,128)(2,1)} %all-to-all-done.near_a), slice={[0:8], [384:512], [0:1024]} | slice | bytes 4194304 | tf_op jit(solution)/shard_map/slice | solution.py:293
  144.9 0.0 collective-permute-done.1
  144.9 1.6 collective-permute-start.7
  146.5 2.5 %slice_bitcast_fusion.1 = (bf16[4,1,128,2048]{3,2,0,1:T(8,128)(2,1)S(1)}, bf16[4,1,128,2048]{3,2,0,1:T(8,128)(2,1)S(1)}) fusion(bf16[5,128,2048]{2,1,0:T(8,128)(2,1)} %collective-permute-done.1), kind=kLoop, calls=%fused_computation.4 | loop fusion | bytes 8388608 | tf_op jit(solution)/shard_map/stack | solution.py:299
  149.0 0.4 pad_maximum_fusion
  149.4 2.3 copy.7
  151.7 6.5 %all-to-all-start.1 = ((bf16[8,128,2048]{2,1,0:T(8,128)(2,1)}), bf16[8,128,2048]{2,1,0:T(8,128)(2,1)}, u32[]{:S(2)}, u32[]{:S(2)}) async-start(bf16[8,128,2048]{2,1,0:T(8,128)(2,1)} %bitcast.10), calls=%async_computation.1 | async-start | bytes 8388608 | tf_op jit(solution)/shard_map/all_to_all | solution.py:258
  158.2 0.4 constant_dynamic-slice_fusion
  158.6 2.3 collective-permute-start.9
  160.9 0.0 collective-permute-start.8
  160.9 1.8 slice.31
  162.7 0.6 collective-permute-start.6
  163.3 20.0 %collective-permute-done.9.p3 = bf16[2,256,1024]{2,1,0:T(8,128)(2,1)S(1)} collective-permute-done((bf16[2,256,1024]{2,1,0:T(8,128)(2,1)S(1)}, bf16[2,256,1024]{2,1,0:T(8,128)(2,1)S(1)}, u32[]{:S(2)}, u32[]{:S(2)}) %collective-permute-start.9) | collective-permute-done | bytes 1048608 | tf_op jit(solution)/shard_map/ppermute | solution.py:255
  183.3 3.2 %collective-permute-done.8.p1 = bf16[2,256,1024]{2,1,0:T(8,128)(2,1)S(1)} collective-permute-done((bf16[2,256,1024]{2,1,0:T(8,128)(2,1)S(1)}, bf16[2,256,1024]{2,1,0:T(8,128)(2,1)S(1)}, u32[]{:S(2)}, u32[]{:S(2)}) %collective-permute-start.8) | collective-permute-done | bytes 1048608 | tf_op jit(solution)/shard_map/ppermute | solution.py:255
  186.5 5.7 %collective-permute-done.7.o_cross = bf16[8,128,1024]{2,1,0:T(8,128)(2,1)} collective-permute-done((bf16[8,128,1024]{2,1,0:T(8,128)(2,1)}, bf16[8,128,1024]{2,1,0:T(8,128)(2,1)}, u32[]{:S(2)}, u32[]{:S(2)}) %collective-permute-start.7) | collective-permute-done | bytes 2097184 | tf_op jit(solution)/shard_map/ppermute | solution.py:246
  192.2 2.6 %collective-permute-start.10 = (bf16[8,128,1024]{2,1,0:T(8,128)(2,1)}, bf16[8,128,1024]{2,1,0:T(8,128)(2,1)}, u32[]{:S(2)}, u32[]{:S(2)}) collective-permute-start(bf16[8,128,1024]{2,1,0:T(8,128)(2,1)} %collective-permute-done.7.o_cross), channel_id=1, source_target_pairs={{0,8},{8,0},{16,24},{24,16},{32,40},{40,32},{48,56},{56,48},{64,72... | collective-permute-start | bytes 6291464 | tf_op jit(solution)/shard_map/ppermute | solution.py:252
  194.8 0.7 collective-permute-start.12
  195.5 1.6 collective-permute-start.11
  197.1 24.5 %collective-permute-done.11.p2 = bf16[2,256,1024]{2,1,0:T(8,128)(2,1)} collective-permute-done((bf16[2,256,1024]{2,1,0:T(8,128)(2,1)S(1)}, bf16[2,256,1024]{2,1,0:T(8,128)(2,1)}, u32[]{:S(2)}, u32[]{:S(2)}) %collective-permute-start.11) | collective-permute-done | bytes 1048608 | tf_op jit(solution)/shard_map/ppermute | solution.py:255
  221.6 0.0 collective-permute-done.6.o_near
  221.6 0.0 all-to-all-done.1.e_far
  221.6 0.0 collective-permute-done.10.o_swap
  221.6 21.4 %multiply.1 = (f32[2048,1024]{1,0:T(8,128)S(1)}, bf16[2,8,128,1024]{3,2,1,0:T(8,128)(2,1)S(1)}) custom-call(s32[2]{0:T(128)S(1)} %pad_add_fusion.ids, bf16[8,512,1024]{2,1,0:T(8,128)(2,1)} %all-to-all-done.near_a, bf16[8,128,2048]{2,1,0:T(8,128)(2,1)} %all-to-all-done.1.e_far, bf16[8,128,1024]{2,1,0:T(8,128)(2,1)} %collective-permute-done.6.o_near, ...), custom_call_target="tpu_custom_call" | custom-call | tf_op jit(solution)/shard_map/multiply/pallas_call | solution.py:309
  243.1 0.0 collective-permute-done.12.right
  243.1 7.9 %finish.1 = f32[2048,1024]{1,0:T(8,128)} custom-call(s32[16,32]{1,0:T(8,128)S(1)} %bitcast.9, f32[2048,1024]{1,0:T(8,128)S(1)} %get-tuple-element.62.part, bf16[2,8,128,1024]{3,2,1,0:T(8,128)(2,1)S(1)} %get-tuple-element.63.left, bf16[4,256,1024]{2,1,0:T(8,128)(2,1)S(1)} %collective-permute-done.12.right), custom_call_target="tpu_custom_call" | custom-call | tf_op jit(solution)/shard_map/finish/pallas_call | solution.py:319
  (20 shorter events, 0.1 us)
Async XLA Ops:
  0.1 10.0 %copy-start = (s32[32,32]{1,0:T(8,128)S(1)}, s32[32,32]{1,0:T(8,128)}, u32[]{:S(2)}) copy-start(s32[32,32]{1,0:T(8,128)} %mask_a.1) | copy-start | bytes 12292
  0.1 10.0 %copy-start.2 = (s32[512]{0:T(512)S(1)}, s32[512]{0:T(512)}, u32[]{:S(2)}) copy-start(s32[512]{0:T(512)} %kdist.1) | copy-start | bytes 6148
  7.6 25.5 %collective-permute-start = (bf16[2,256,1024]{2,1,0:T(8,128)(2,1)}, bf16[2,256,1024]{2,1,0:T(8,128)(2,1)S(1)}, u32[]{:S(2)}, u32[]{:S(2)}) collective-permute-start(bf16[2,256,1024]{2,1,0:T(8,128)(2,1)} %get-tuple-element.39), channel_id=1, source_target_pairs={{0,4},{1,5},{2,6},{3,7},{4,0},{5,1},{6,2},{7,3},{8,12},{9,13},{10,... | collective-permute-start | bytes 3145736 | tf_op jit(solution)/shard_map/ppermute | solution.py:249
  33.1 1.0 copy-start.9
  34.1 107.7 %all-to-all-start = ((bf16[8,512,1024]{2,1,0:T(8,128)(2,1)}), bf16[8,512,1024]{2,1,0:T(8,128)(2,1)}, u32[]{:S(2)}, u32[]{:S(2)}) async-start(bf16[8,512,1024]{2,1,0:T(8,128)(2,1)} %get-tuple-element.43), calls=%async_computation | async-start | bytes 16777216 | tf_op jit(solution)/shard_map/all_to_all | solution.py:258
  40.3 48.6 %collective-permute-start.3 = (bf16[4,256,1024]{2,1,0:T(8,128)(2,1)}, bf16[4,256,1024]{2,1,0:T(8,128)(2,1)S(1)}, u32[]{:S(2)}, u32[]{:S(2)}) collective-permute-start(bf16[4,256,1024]{2,1,0:T(8,128)(2,1)} %get-tuple-element.46), channel_id=1, source_target_pairs={{0,1},{1,2},{2,3},{3,0},{4,5},{5,6},{6,7},{7,4},{8,9},{9,10},{10,1... | collective-permute-start | bytes 6291464 | tf_op jit(solution)/shard_map/ppermute | solution.py:255
  41.6 47.3 %collective-permute-start.4 = (bf16[4,256,1024]{2,1,0:T(8,128)(2,1)}, bf16[4,256,1024]{2,1,0:T(8,128)(2,1)S(1)}, u32[]{:S(2)}, u32[]{:S(2)}) collective-permute-start(bf16[4,256,1024]{2,1,0:T(8,128)(2,1)} %get-tuple-element.47), channel_id=1, source_target_pairs={{0,3},{1,0},{2,1},{3,2},{4,7},{5,4},{6,5},{7,6},{8,11},{9,8},{10,9... | collective-permute-start | bytes 6291464 | tf_op jit(solution)/shard_map/ppermute | solution.py:255
  43.0 101.9 %collective-permute-start.1 = (bf16[5,128,2048]{2,1,0:T(8,128)(2,1)}, bf16[5,128,2048]{2,1,0:T(8,128)(2,1)}, u32[]{:S(2)}, u32[]{:S(2)}) collective-permute-start(bf16[5,128,2048]{2,1,0:T(8,128)(2,1)} %get-tuple-element.40), channel_id=1, source_target_pairs={{0,64},{8,72},{16,80},{24,88},{32,96},{40,104},{48,112},{56,120},{... | collective-permute-start | bytes 7864328 | tf_op jit(solution)/shard_map/ppermute | solution.py:246
  88.9 49.8 %copy-start.4 = (bf16[4,256,1024]{2,1,0:T(8,128)(2,1)}, bf16[4,256,1024]{2,1,0:T(8,128)(2,1)S(1)}, u32[]{:S(2)}) copy-start(bf16[4,256,1024]{2,1,0:T(8,128)(2,1)S(1)} %collective-permute-done.3.r1) | copy-start | bytes 6291460
  88.9 49.8 %copy-start.5 = (bf16[4,256,1024]{2,1,0:T(8,128)(2,1)}, bf16[4,256,1024]{2,1,0:T(8,128)(2,1)S(1)}, u32[]{:S(2)}) copy-start(bf16[4,256,1024]{2,1,0:T(8,128)(2,1)S(1)} %collective-permute-done.4.r3) | copy-start | bytes 6291460
  88.9 49.9 %collective-permute-start.5 = (bf16[4,256,1024]{2,1,0:T(8,128)(2,1)}, bf16[4,256,1024]{2,1,0:T(8,128)(2,1)S(1)}, u32[]{:S(2)}, u32[]{:S(2)}) collective-permute-start(bf16[4,256,1024]{2,1,0:T(8,128)(2,1)} %get-tuple-element.49), channel_id=1, source_target_pairs={{0,2},{1,3},{2,0},{3,1},{4,6},{5,7},{6,4},{7,5},{8,10},{9,11},{10,... | collective-permute-start | bytes 6291464 | tf_op jit(solution)/shard_map/ppermute | solution.py:255
  91.1 46.2 %collective-permute-start.2 = (bf16[3,256,1024]{2,1,0:T(8,128)(2,1)}, bf16[3,256,1024]{2,1,0:T(8,128)(2,1)S(1)}, u32[]{:S(2)}, u32[]{:S(2)}) collective-permute-start(bf16[3,256,1024]{2,1,0:T(8,128)(2,1)} %get-tuple-element.42), channel_id=1, source_target_pairs={{0,4},{1,5},{2,6},{3,7},{4,0},{5,1},{6,2},{7,3},{8,12},{9,13},{10,... | collective-permute-start | bytes 4718600 | tf_op jit(solution)/shard_map/ppermute | solution.py:249
  138.7 19.5 %copy-start.3 = (bf16[5,256,1024]{2,1,0:T(8,128)(2,1)}, bf16[5,256,1024]{2,1,0:T(8,128)(2,1)S(1)}, u32[]{:S(2)}) copy-start(bf16[5,256,1024]{2,1,0:T(8,128)(2,1)S(1)} %pad_maximum_fusion.1.p0) | copy-start | bytes 7864324
  138.8 1.5 slice-start
  138.8 1.4 copy-start.6
  144.9 47.3 %collective-permute-start.7 = (bf16[8,128,1024]{2,1,0:T(8,128)(2,1)}, bf16[8,128,1024]{2,1,0:T(8,128)(2,1)}, u32[]{:S(2)}, u32[]{:S(2)}) collective-permute-start(bf16[8,128,1024]{2,1,0:T(8,128)(2,1)} %slice.32), channel_id=1, source_target_pairs={{0,64},{8,72},{16,80},{24,88},{32,96},{40,104},{48,112},{56,120},{... | collective-permute-start | bytes 6291464 | tf_op jit(solution)/shard_map/ppermute | solution.py:246
  151.7 69.9 %all-to-all-start.1 = ((bf16[8,128,2048]{2,1,0:T(8,128)(2,1)}), bf16[8,128,2048]{2,1,0:T(8,128)(2,1)}, u32[]{:S(2)}, u32[]{:S(2)}) async-start(bf16[8,128,2048]{2,1,0:T(8,128)(2,1)} %bitcast.10), calls=%async_computation.1 | async-start | bytes 8388608 | tf_op jit(solution)/shard_map/all_to_all | solution.py:258
  158.6 24.7 %collective-permute-start.9 = (bf16[2,256,1024]{2,1,0:T(8,128)(2,1)S(1)}, bf16[2,256,1024]{2,1,0:T(8,128)(2,1)S(1)}, u32[]{:S(2)}, u32[]{:S(2)}) collective-permute-start(bf16[2,256,1024]{2,1,0:T(8,128)(2,1)S(1)} %get-tuple-element.65), channel_id=1, source_target_pairs={{0,3},{1,0},{2,1},{3,2},{4,7},{5,4},{6,5},{7,6},{8,11},{9,8},{10,9... | collective-permute-start | bytes 3145736 | tf_op jit(solution)/shard_map/ppermute | solution.py:255
  160.9 25.6 %collective-permute-start.8 = (bf16[2,256,1024]{2,1,0:T(8,128)(2,1)S(1)}, bf16[2,256,1024]{2,1,0:T(8,128)(2,1)S(1)}, u32[]{:S(2)}, u32[]{:S(2)}) collective-permute-start(bf16[2,256,1024]{2,1,0:T(8,128)(2,1)S(1)} %get-tuple-element.66), channel_id=1, source_target_pairs={{0,1},{1,2},{2,3},{3,0},{4,5},{5,6},{6,7},{7,4},{8,9},{9,10},{10,1... | collective-permute-start | bytes 3145736 | tf_op jit(solution)/shard_map/ppermute | solution.py:255
  162.7 58.9 %collective-permute-start.6 = (bf16[8,128,1024]{2,1,0:T(8,128)(2,1)S(1)}, bf16[8,128,1024]{2,1,0:T(8,128)(2,1)}, u32[]{:S(2)}, u32[]{:S(2)}) collective-permute-start(bf16[8,128,1024]{2,1,0:T(8,128)(2,1)S(1)} %slice.31), channel_id=1, source_target_pairs={{0,8},{8,0},{16,24},{24,16},{32,40},{40,32},{48,56},{56,48},{64,72... | collective-permute-start | bytes 6291464 | tf_op jit(solution)/shard_map/ppermute | solution.py:252
  183.3 3.2 %copy-start.7 = (bf16[2,256,1024]{2,1,0:T(8,128)(2,1)}, bf16[2,256,1024]{2,1,0:T(8,128)(2,1)S(1)}, u32[]{:S(2)}) copy-start(bf16[2,256,1024]{2,1,0:T(8,128)(2,1)S(1)} %collective-permute-done.9.p3) | copy-start | bytes 3145732
  186.5 5.7 %copy-start.8 = (bf16[2,256,1024]{2,1,0:T(8,128)(2,1)}, bf16[2,256,1024]{2,1,0:T(8,128)(2,1)S(1)}, u32[]{:S(2)}) copy-start(bf16[2,256,1024]{2,1,0:T(8,128)(2,1)S(1)} %collective-permute-done.8.p1) | copy-start | bytes 3145732
  186.5 56.6 %copy-start.1 = (s32[32,16]{0,1:T(8,128)S(1)}, s32[32,16]{0,1:T(8,128)}, u32[]{:S(2)}) copy-start(s32[32,16]{0,1:T(8,128)} %param.10) | copy-start | bytes 6148
  192.2 29.4 %collective-permute-start.10 = (bf16[8,128,1024]{2,1,0:T(8,128)(2,1)}, bf16[8,128,1024]{2,1,0:T(8,128)(2,1)}, u32[]{:S(2)}, u32[]{:S(2)}) collective-permute-start(bf16[8,128,1024]{2,1,0:T(8,128)(2,1)} %collective-permute-done.7.o_cross), channel_id=1, source_target_pairs={{0,8},{8,0},{16,24},{24,16},{32,40},{40,32},{48,56},{56,48},{64,72... | collective-permute-start | bytes 6291464 | tf_op jit(solution)/shard_map/ppermute | solution.py:252
  194.8 48.3 %collective-permute-start.12 = (bf16[4,256,1024]{2,1,0:T(8,128)(2,1)}, bf16[4,256,1024]{2,1,0:T(8,128)(2,1)S(1)}, u32[]{:S(2)}, u32[]{:S(2)}) collective-permute-start(bf16[4,256,1024]{2,1,0:T(8,128)(2,1)} %pad_maximum_fusion.2), channel_id=1, source_target_pairs={{0,4},{1,5},{2,6},{3,7},{4,0},{5,1},{6,2},{7,3},{8,12},{9,13},{10,... | collective-permute-start | bytes 6291464 | tf_op jit(solution)/shard_map/ppermute | solution.py:249
  195.5 26.1 %collective-permute-start.11 = (bf16[2,256,1024]{2,1,0:T(8,128)(2,1)S(1)}, bf16[2,256,1024]{2,1,0:T(8,128)(2,1)}, u32[]{:S(2)}, u32[]{:S(2)}) collective-permute-start(bf16[2,256,1024]{2,1,0:T(8,128)(2,1)S(1)} %get-tuple-element.60), channel_id=1, source_target_pairs={{0,2},{1,3},{2,0},{3,1},{4,6},{5,7},{6,4},{7,5},{8,10},{9,11},{10,... | collective-permute-start | bytes 3145736 | tf_op jit(solution)/shard_map/ppermute | solution.py:255

commit v8 on v7

--- a/solution.py
+++ b/solution.py
@@ -9,7 +9,7 @@
 KB = 32
 NP = 16
 W = 1024
-EARLY = 2
+EARLY = 1
 MIB = 1 << 20
 Y_GROUPS = [list(range(8)), list(range(8, 16))]
 
@@ -292,7 +292,7 @@
 
     o_send = near_a[:, 384:]
     q_send = jnp.concatenate([v[3:4] for v in (x0, r1, r2, r3)], axis=0)
-    a_cross, b_cross, near_a, o_send, q_send = lax.optimization_barrier((a_cross, b_cross, near_a, o_send, q_send))
+    a_cross, near_a, o_send, q_send = lax.optimization_barrier((a_cross, near_a, o_send, q_send))
     o_cross = swap_z_hi(o_send)
     o_near = swap_core(near_a[:, 256:384])
 

time: 252 us -> 240 us (0.952)
  waiting for transfers between devices: 155 us -> 141 us
    ppermute x3, waiting for transfers between devices: 59.2 us -> 4.28 us  [swap_z_lo(): return lax.ppermute(value, 'col', [(i, i ^ 4) for i in range(8)])]
    ppermute x6, waiting for transfers between devices: 90.1 us -> 135 us  [along_x(): lax.ppermute(value, 'col', [(i, i // 4 * 4 + (i % 4 + hop) % 4) for i in...]
    ppermute x2, waiting for transfers between devices: 5.7 us -> 1.52 us  [swap_z_hi(): return lax.ppermute(value, 'row', [(i, i ^ 8) for i in range(16)])]
  transfers between devices with their start and end apart: 15 -> 15, of which waited for: 7 -> 7; matrix products, arithmetic and copies ran while one was open for 6% -> 5% of each run, Pallas kernels for 11% -> 12%
where the time goes in v8:
time: 240 us
  waiting for transfers between devices  141 us (59%)
  Pallas kernels  44.1 us (18%)
  starting transfers between devices  36.1 us (15%)
  local copies, waits for them, and re-layouts  15.6 us (6%)
    ppermute x6, waiting for transfers between devices, along_x(): lax.ppermute(value, 'col', [(i, i // 4 * 4 + (i % 4 + hop) % 4) for i in...  135 us
    pallas_call x1, Pallas kernels, on_device(): pl.pallas_call(multiply, out_shape=[pltpu.VMEM((2 * W, W), jnp.float32),...  21.3 us
    all_to_all x2, starting transfers between devices, along_y(): lax.all_to_all(value, 'row', 0, 0, axis_index_groups=Y_GROUPS, tiled=True)  12.8 us
    ppermute x6, starting transfers between devices, along_x(): lax.ppermute(value, 'col', [(i, i // 4 * 4 + (i % 4 + hop) % 4) for i in...  8.82 us
    pallas_call x1, Pallas kernels, on_device(): pl.pallas_call(finish, out_shape=jax.ShapeDtypeStruct((2 * W, W), jnp.flo...  7.86 us
    pallas_call x1, Pallas kernels, on_device(): pl.pallas_call(prep_b, out_shape=[bf16(4, 256, W)] * 4 + [bf16(EARLY, 256...  7.49 us
    pallas_call x1, Pallas kernels, on_device(): pl.pallas_call(prep_a, out_shape=[bf16(8, 512, W), bf16(5, 128, 2 * W)],...  7.43 us
    ppermute x2, starting transfers between devices, swap_z_hi(): return lax.ppermute(value, 'row', [(i, i ^ 8) for i in range(16)])  6.93 us
  transfers between devices with their start and end apart: 15, of which 7 were waited for; matrix products, arithmetic and copies ran while one was open for 5% of the time, Pallas kernels for 12%

profile of v8, /device:TPU:1, one launch (start us, length us, event | category | flops | bytes accessed | tf_op | source)
XLA Modules:
  0.0 239.5 jit_solution(13800219352028972398)
XLA Ops:
  0.0 0.1 pad_add_fusion.ids
  0.1 7.5 %prep_b.1 = (bf16[4,256,1024]{2,1,0:T(8,128)(2,1)}, bf16[4,256,1024]{2,1,0:T(8,128)(2,1)}, bf16[4,256,1024]{2,1,0:T(8,128)(2,1)}, bf16[4,256,1024]{2,1,0:T(8,128...) custom-call(s32[2]{0:T(128)S(1)} %pad_add_fusion.ids, s32[512]{0:T(512)} %kdist.1, ...), custom_call_target="tpu_custom_call" | custom-call | tf_op jit(solution)/shard_map/prep_b/pallas_call | solution.py:260
  7.6 2.5 %collective-permute-start = (bf16[1,256,1024]{2,1,0:T(8,128)(2,1)}, bf16[1,256,1024]{2,1,0:T(8,128)(2,1)S(1)}, u32[]{:S(2)}, u32[]{:S(2)}) collective-permute-start(bf16[1,256,1024]{2,1,0:T(8,128)(2,1)} %get-tuple-element.38), channel_id=1, source_target_pairs={{0,4},{1,5},{2,6},{3,7},{4,0},{5,1},{6,2},{7,3},{8,12},{9,13},{10,... | collective-permute-start | bytes 1572872 | tf_op jit(solution)/shard_map/ppermute | solution.py:249
  10.1 7.4 %prep_a.1 = (bf16[8,512,1024]{2,1,0:T(8,128)(2,1)}, bf16[5,128,2048]{2,1,0:T(8,128)(2,1)}) custom-call(s32[2]{0:T(128)S(1)} %pad_add_fusion.ids, s32[512]{0:T(512)S(1)} %copy-done.2, s32[32,32]{1,0:T(8,128)S(1)} %copy-done, bf16[2048,2048]{1,0:T(8,128)(2,1)} %at), custom_call_target="tpu_custom_call" | custom-call | tf_op jit(solution)/shard_map/prep_a/pallas_call | solution.py:273
  17.6 4.3 %collective-permute-done = bf16[1,256,1024]{2,1,0:T(8,128)(2,1)S(1)} collective-permute-done((bf16[1,256,1024]{2,1,0:T(8,128)(2,1)}, bf16[1,256,1024]{2,1,0:T(8,128)(2,1)S(1)}, u32[]{:S(2)}, u32[]{:S(2)}) %collective-permute-start) | collective-permute-done | bytes 524320 | tf_op jit(solution)/shard_map/ppermute | solution.py:249
  21.8 6.2 %all-to-all-start = ((bf16[8,512,1024]{2,1,0:T(8,128)(2,1)}), bf16[8,512,1024]{2,1,0:T(8,128)(2,1)}, u32[]{:S(2)}, u32[]{:S(2)}) async-start(bf16[8,512,1024]{2,1,0:T(8,128)(2,1)} %get-tuple-element.40), calls=%async_computation | async-start | bytes 16777216 | tf_op jit(solution)/shard_map/all_to_all | solution.py:258
  28.0 1.3 collective-permute-start.2
  29.3 1.4 collective-permute-start.3
  30.7 3.5 %collective-permute-start.1 = (bf16[5,128,2048]{2,1,0:T(8,128)(2,1)}, bf16[5,128,2048]{2,1,0:T(8,128)(2,1)S(1)}, u32[]{:S(2)}, u32[]{:S(2)}) collective-permute-start(bf16[5,128,2048]{2,1,0:T(8,128)(2,1)} %get-tuple-element.39), channel_id=1, source_target_pairs={{0,64},{8,72},{16,80},{24,88},{32,96},{40,104},{48,112},{56,120},{... | collective-permute-start | bytes 7864328 | tf_op jit(solution)/shard_map/ppermute | solution.py:246
  34.2 42.4 %collective-permute-done.2.r1 = bf16[4,256,1024]{2,1,0:T(8,128)(2,1)S(1)} collective-permute-done((bf16[4,256,1024]{2,1,0:T(8,128)(2,1)}, bf16[4,256,1024]{2,1,0:T(8,128)(2,1)S(1)}, u32[]{:S(2)}, u32[]{:S(2)}) %collective-permute-start.2) | collective-permute-done | bytes 2097184 | tf_op jit(solution)/shard_map/ppermute | solution.py:255
  76.6 0.0 collective-permute-done.3.r3
  76.6 2.3 collective-permute-start.4
  78.9 1.5 collective-permute-start.7
  80.3 1.1 slice.25
  81.5 43.1 %collective-permute-done.4.r2 = bf16[4,256,1024]{2,1,0:T(8,128)(2,1)S(1)} collective-permute-done((bf16[4,256,1024]{2,1,0:T(8,128)(2,1)}, bf16[4,256,1024]{2,1,0:T(8,128)(2,1)S(1)}, u32[]{:S(2)}, u32[]{:S(2)}) %collective-permute-start.4) | collective-permute-done | bytes 2097184 | tf_op jit(solution)/shard_map/ppermute | solution.py:255
  124.6 1.4 copy-done.6
  126.1 1.6 pad_maximum_fusion.1
  127.6 0.0 all-to-all-done.near_a
  127.6 3.1 %slice.32 = bf16[8,128,1024]{2,1,0:T(8,128)(2,1)} slice(bf16[8,512,1024]{2,1,0:T(8,128)(2,1)} %all-to-all-done.near_a), slice={[0:8], [384:512], [0:1024]} | slice | bytes 4194304 | tf_op jit(solution)/shard_map/slice | solution.py:293
  130.7 0.0 collective-permute-done.1
  130.7 3.5 %collective-permute-start.6 = (bf16[8,128,1024]{2,1,0:T(8,128)(2,1)}, bf16[8,128,1024]{2,1,0:T(8,128)(2,1)}, u32[]{:S(2)}, u32[]{:S(2)}) collective-permute-start(bf16[8,128,1024]{2,1,0:T(8,128)(2,1)} %slice.32), channel_id=1, source_target_pairs={{0,64},{8,72},{16,80},{24,88},{32,96},{40,104},{48,112},{56,120},{... | collective-permute-start | bytes 6291464 | tf_op jit(solution)/shard_map/ppermute | solution.py:246
  134.2 0.5 slice_bitcast_fusion.1
  134.7 0.4 pad_maximum_fusion
  135.1 2.3 copy.7
  137.4 6.6 %all-to-all-start.1 = ((bf16[8,128,2048]{2,1,0:T(8,128)(2,1)}), bf16[8,128,2048]{2,1,0:T(8,128)(2,1)}, u32[]{:S(2)}, u32[]{:S(2)}) async-start(bf16[8,128,2048]{2,1,0:T(8,128)(2,1)} %bitcast.10), calls=%async_computation.1 | async-start | bytes 8388608 | tf_op jit(solution)/shard_map/all_to_all | solution.py:258
  144.0 0.0 collective-permute-done.7
  144.0 1.8 constant_dynamic-update-slice_fusion.p0
  145.8 0.5 constant_dynamic-slice_fusion
  146.4 1.0 copy-done.3
  147.4 2.3 collective-permute-start.9
  149.7 0.0 collective-permute-start.8
  149.7 22.4 %collective-permute-done.9.p3 = bf16[2,256,1024]{2,1,0:T(8,128)(2,1)S(1)} collective-permute-done((bf16[2,256,1024]{2,1,0:T(8,128)(2,1)S(1)}, bf16[2,256,1024]{2,1,0:T(8,128)(2,1)S(1)}, u32[]{:S(2)}, u32[]{:S(2)}) %collective-permute-start.9) | collective-permute-done | bytes 1048608 | tf_op jit(solution)/shard_map/ppermute | solution.py:255
  172.1 3.2 %collective-permute-done.8.p1 = bf16[2,256,1024]{2,1,0:T(8,128)(2,1)S(1)} collective-permute-done((bf16[2,256,1024]{2,1,0:T(8,128)(2,1)S(1)}, bf16[2,256,1024]{2,1,0:T(8,128)(2,1)S(1)}, u32[]{:S(2)}, u32[]{:S(2)}) %collective-permute-start.8) | collective-permute-done | bytes 1048608 | tf_op jit(solution)/shard_map/ppermute | solution.py:255
  175.3 1.0 copy-done.8
  176.3 1.8 slice.31
  178.0 0.0 copy-start.1
  178.0 1.3 collective-permute-start.5
  179.3 1.5 collective-permute-done.6.o_cross
  180.9 1.3 collective-permute-start.10
  182.2 1.0 collective-permute-start.12
  183.2 1.6 collective-permute-start.11
  184.8 24.4 %collective-permute-done.11.p2 = bf16[2,256,1024]{2,1,0:T(8,128)(2,1)S(1)} collective-permute-done((bf16[2,256,1024]{2,1,0:T(8,128)(2,1)S(1)}, bf16[2,256,1024]{2,1,0:T(8,128)(2,1)S(1)}, u32[]{:S(2)}, u32[]{:S(2)}) %collective-permute-start.11) | collective-permute-done | bytes 1048608 | tf_op jit(solution)/shard_map/ppermute | solution.py:255
  209.1 0.0 collective-permute-done.5.o_near
  209.1 0.0 all-to-all-done.1.e_far
  209.1 0.0 collective-permute-done.10.o_swap
  209.2 1.0 copy-done.9
  210.1 21.3 %multiply.1 = (f32[2048,1024]{1,0:T(8,128)S(1)}, bf16[2,8,128,1024]{3,2,1,0:T(8,128)(2,1)S(1)}) custom-call(s32[2]{0:T(128)S(1)} %pad_add_fusion.ids, bf16[8,512,1024]{2,1,0:T(8,128)(2,1)} %all-to-all-done.near_a, bf16[8,128,2048]{2,1,0:T(8,128)(2,1)} %all-to-all-done.1.e_far, bf16[8,128,1024]{2,1,0:T(8,128)(2,1)} %collective-permute-done.5.o_near, ...), custom_call_target="tpu_custom_call" | custom-call | tf_op jit(solution)/shard_map/multiply/pallas_call | solution.py:309
  231.5 7.9 %finish.1 = f32[2048,1024]{1,0:T(8,128)} custom-call(s32[16,32]{1,0:T(8,128)S(1)} %bitcast.9, f32[2048,1024]{1,0:T(8,128)S(1)} %get-tuple-element.60.part, bf16[2,8,128,1024]{3,2,1,0:T(8,128)(2,1)S(1)} %get-tuple-element.61.left, bf16[4,256,1024]{2,1,0:T(8,128)(2,1)S(1)} %collective-permute-done.12.right), custom_call_target="tpu_custom_call" | custom-call | tf_op jit(solution)/shard_map/finish/pallas_call | solution.py:319
  (20 shorter events, 0.2 us)
Async XLA Ops:
  0.1 10.0 %copy-start = (s32[32,32]{1,0:T(8,128)S(1)}, s32[32,32]{1,0:T(8,128)}, u32[]{:S(2)}) copy-start(s32[32,32]{1,0:T(8,128)} %mask_a.1) | copy-start | bytes 12292
  0.1 10.0 %copy-start.2 = (s32[512]{0:T(512)S(1)}, s32[512]{0:T(512)}, u32[]{:S(2)}) copy-start(s32[512]{0:T(512)} %kdist.1) | copy-start | bytes 6148
  7.6 14.3 %collective-permute-start = (bf16[1,256,1024]{2,1,0:T(8,128)(2,1)}, bf16[1,256,1024]{2,1,0:T(8,128)(2,1)S(1)}, u32[]{:S(2)}, u32[]{:S(2)}) collective-permute-start(bf16[1,256,1024]{2,1,0:T(8,128)(2,1)} %get-tuple-element.38), channel_id=1, source_target_pairs={{0,4},{1,5},{2,6},{3,7},{4,0},{5,1},{6,2},{7,3},{8,12},{9,13},{10,... | collective-permute-start | bytes 1572872 | tf_op jit(solution)/shard_map/ppermute | solution.py:249
  21.8 105.8 %all-to-all-start = ((bf16[8,512,1024]{2,1,0:T(8,128)(2,1)}), bf16[8,512,1024]{2,1,0:T(8,128)(2,1)}, u32[]{:S(2)}, u32[]{:S(2)}) async-start(bf16[8,512,1024]{2,1,0:T(8,128)(2,1)} %get-tuple-element.40), calls=%async_computation | async-start | bytes 16777216 | tf_op jit(solution)/shard_map/all_to_all | solution.py:258
  28.0 48.6 %collective-permute-start.2 = (bf16[4,256,1024]{2,1,0:T(8,128)(2,1)}, bf16[4,256,1024]{2,1,0:T(8,128)(2,1)S(1)}, u32[]{:S(2)}, u32[]{:S(2)}) collective-permute-start(bf16[4,256,1024]{2,1,0:T(8,128)(2,1)} %get-tuple-element.43), channel_id=1, source_target_pairs={{0,1},{1,2},{2,3},{3,0},{4,5},{5,6},{6,7},{7,4},{8,9},{9,10},{10,1... | collective-permute-start | bytes 6291464 | tf_op jit(solution)/shard_map/ppermute | solution.py:255
  29.3 47.3 %collective-permute-start.3 = (bf16[4,256,1024]{2,1,0:T(8,128)(2,1)}, bf16[4,256,1024]{2,1,0:T(8,128)(2,1)S(1)}, u32[]{:S(2)}, u32[]{:S(2)}) collective-permute-start(bf16[4,256,1024]{2,1,0:T(8,128)(2,1)} %get-tuple-element.44), channel_id=1, source_target_pairs={{0,3},{1,0},{2,1},{3,2},{4,7},{5,4},{6,5},{7,6},{8,11},{9,8},{10,9... | collective-permute-start | bytes 6291464 | tf_op jit(solution)/shard_map/ppermute | solution.py:255
  30.7 100.0 %collective-permute-start.1 = (bf16[5,128,2048]{2,1,0:T(8,128)(2,1)}, bf16[5,128,2048]{2,1,0:T(8,128)(2,1)S(1)}, u32[]{:S(2)}, u32[]{:S(2)}) collective-permute-start(bf16[5,128,2048]{2,1,0:T(8,128)(2,1)} %get-tuple-element.39), channel_id=1, source_target_pairs={{0,64},{8,72},{16,80},{24,88},{32,96},{40,104},{48,112},{56,120},{... | collective-permute-start | bytes 7864328 | tf_op jit(solution)/shard_map/ppermute | solution.py:246
  76.6 4.8 %copy-start.4 = (bf16[4,256,1024]{2,1,0:T(8,128)(2,1)}, bf16[4,256,1024]{2,1,0:T(8,128)(2,1)S(1)}, u32[]{:S(2)}) copy-start(bf16[4,256,1024]{2,1,0:T(8,128)(2,1)S(1)} %collective-permute-done.2.r1) | copy-start | bytes 6291460
  76.6 4.9 %copy-start.5 = (bf16[4,256,1024]{2,1,0:T(8,128)(2,1)}, bf16[4,256,1024]{2,1,0:T(8,128)(2,1)S(1)}, u32[]{:S(2)}) copy-start(bf16[4,256,1024]{2,1,0:T(8,128)(2,1)S(1)} %collective-permute-done.3.r3) | copy-start | bytes 6291460
  76.6 48.0 %collective-permute-start.4 = (bf16[4,256,1024]{2,1,0:T(8,128)(2,1)}, bf16[4,256,1024]{2,1,0:T(8,128)(2,1)S(1)}, u32[]{:S(2)}, u32[]{:S(2)}) collective-permute-start(bf16[4,256,1024]{2,1,0:T(8,128)(2,1)} %get-tuple-element.46), channel_id=1, source_target_pairs={{0,2},{1,3},{2,0},{3,1},{4,6},{5,7},{6,4},{7,5},{8,10},{9,11},{10,... | collective-permute-start | bytes 6291464 | tf_op jit(solution)/shard_map/ppermute | solution.py:255
  78.9 65.2 %collective-permute-start.7 = (bf16[4,256,1024]{2,1,0:T(8,128)(2,1)}, bf16[4,256,1024]{2,1,0:T(8,128)(2,1)}, u32[]{:S(2)}, u32[]{:S(2)}) collective-permute-start(bf16[4,256,1024]{2,1,0:T(8,128)(2,1)} %get-tuple-element.53), channel_id=1, source_target_pairs={{0,4},{1,5},{2,6},{3,7},{4,0},{5,1},{6,2},{7,3},{8,12},{9,13},{10,... | collective-permute-start | bytes 6291464 | tf_op jit(solution)/shard_map/ppermute | solution.py:249
  124.6 1.4 copy-start.6
  130.7 50.2 %collective-permute-start.6 = (bf16[8,128,1024]{2,1,0:T(8,128)(2,1)}, bf16[8,128,1024]{2,1,0:T(8,128)(2,1)}, u32[]{:S(2)}, u32[]{:S(2)}) collective-permute-start(bf16[8,128,1024]{2,1,0:T(8,128)(2,1)} %slice.32), channel_id=1, source_target_pairs={{0,64},{8,72},{16,80},{24,88},{32,96},{40,104},{48,112},{56,120},{... | collective-permute-start | bytes 6291464 | tf_op jit(solution)/shard_map/ppermute | solution.py:246
  137.4 71.8 %all-to-all-start.1 = ((bf16[8,128,2048]{2,1,0:T(8,128)(2,1)}), bf16[8,128,2048]{2,1,0:T(8,128)(2,1)}, u32[]{:S(2)}, u32[]{:S(2)}) async-start(bf16[8,128,2048]{2,1,0:T(8,128)(2,1)} %bitcast.10), calls=%async_computation.1 | async-start | bytes 8388608 | tf_op jit(solution)/shard_map/all_to_all | solution.py:258
  145.8 1.6 copy-start.3
  147.4 24.7 %collective-permute-start.9 = (bf16[2,256,1024]{2,1,0:T(8,128)(2,1)S(1)}, bf16[2,256,1024]{2,1,0:T(8,128)(2,1)S(1)}, u32[]{:S(2)}, u32[]{:S(2)}) collective-permute-start(bf16[2,256,1024]{2,1,0:T(8,128)(2,1)S(1)} %get-tuple-element.63), channel_id=1, source_target_pairs={{0,3},{1,0},{2,1},{3,2},{4,7},{5,4},{6,5},{7,6},{8,11},{9,8},{10,9... | collective-permute-start | bytes 3145736 | tf_op jit(solution)/shard_map/ppermute | solution.py:255
  149.7 25.6 %collective-permute-start.8 = (bf16[2,256,1024]{2,1,0:T(8,128)(2,1)S(1)}, bf16[2,256,1024]{2,1,0:T(8,128)(2,1)S(1)}, u32[]{:S(2)}, u32[]{:S(2)}) collective-permute-start(bf16[2,256,1024]{2,1,0:T(8,128)(2,1)S(1)} %get-tuple-element.64), channel_id=1, source_target_pairs={{0,1},{1,2},{2,3},{3,0},{4,5},{5,6},{6,7},{7,4},{8,9},{9,10},{10,1... | collective-permute-start | bytes 3145736 | tf_op jit(solution)/shard_map/ppermute | solution.py:255
  172.1 5.9 %copy-start.7 = (bf16[2,256,1024]{2,1,0:T(8,128)(2,1)}, bf16[2,256,1024]{2,1,0:T(8,128)(2,1)S(1)}, u32[]{:S(2)}) copy-start(bf16[2,256,1024]{2,1,0:T(8,128)(2,1)S(1)} %collective-permute-done.9.p3) | copy-start | bytes 3145732
  175.3 1.0 copy-start.8
  178.0 53.5 %copy-start.1 = (s32[32,16]{0,1:T(8,128)S(1)}, s32[32,16]{0,1:T(8,128)}, u32[]{:S(2)}) copy-start(s32[32,16]{0,1:T(8,128)} %param.10) | copy-start | bytes 6148
  178.0 31.1 %collective-permute-start.5 = (bf16[8,128,1024]{2,1,0:T(8,128)(2,1)S(1)}, bf16[8,128,1024]{2,1,0:T(8,128)(2,1)}, u32[]{:S(2)}, u32[]{:S(2)}) collective-permute-start(bf16[8,128,1024]{2,1,0:T(8,128)(2,1)S(1)} %slice.31), channel_id=1, source_target_pairs={{0,8},{8,0},{16,24},{24,16},{32,40},{40,32},{48,56},{56,48},{64,72... | collective-permute-start | bytes 6291464 | tf_op jit(solution)/shard_map/ppermute | solution.py:252
  180.9 28.3 %collective-permute-start.10 = (bf16[8,128,1024]{2,1,0:T(8,128)(2,1)}, bf16[8,128,1024]{2,1,0:T(8,128)(2,1)}, u32[]{:S(2)}, u32[]{:S(2)}) collective-permute-start(bf16[8,128,1024]{2,1,0:T(8,128)(2,1)} %collective-permute-done.6.o_cross), channel_id=1, source_target_pairs={{0,8},{8,0},{16,24},{24,16},{32,40},{40,32},{48,56},{56,48},{64,72... | collective-permute-start | bytes 6291464 | tf_op jit(solution)/shard_map/ppermute | solution.py:252
  182.2 49.3 %collective-permute-start.12 = (bf16[4,256,1024]{2,1,0:T(8,128)(2,1)}, bf16[4,256,1024]{2,1,0:T(8,128)(2,1)S(1)}, u32[]{:S(2)}, u32[]{:S(2)}) collective-permute-start(bf16[4,256,1024]{2,1,0:T(8,128)(2,1)} %pad_maximum_fusion.1), channel_id=1, source_target_pairs={{0,4},{1,5},{2,6},{3,7},{4,0},{5,1},{6,2},{7,3},{8,12},{9,13},{10,... | collective-permute-start | bytes 6291464 | tf_op jit(solution)/shard_map/ppermute | solution.py:249
  183.2 26.0 %collective-permute-start.11 = (bf16[2,256,1024]{2,1,0:T(8,128)(2,1)S(1)}, bf16[2,256,1024]{2,1,0:T(8,128)(2,1)S(1)}, u32[]{:S(2)}, u32[]{:S(2)}) collective-permute-start(bf16[2,256,1024]{2,1,0:T(8,128)(2,1)S(1)} %get-tuple-element.58), channel_id=1, source_target_pairs={{0,2},{1,3},{2,0},{3,1},{4,6},{5,7},{6,4},{7,5},{8,10},{9,11},{10,... | collective-permute-start | bytes 3145736 | tf_op jit(solution)/shard_map/ppermute | solution.py:255
  209.1 1.0 copy-start.9

commit v9 on v8

--- a/solution.py
+++ b/solution.py
@@ -203,18 +203,16 @@
     for t in range(2):
         for m in range(4):
             first = t * W + m * 256
-            if len(copies) >= 2:
-                copies[-2].wait()
-            spot = done.at[len(copies) % 2]
+            spot = done.at[len(copies)]
             total = product(left[t, :, :, m * 256:(m + 1) * 256].reshape(W, 256), right[...].reshape(W, W))
             total += part[first:first + 256, :]
             for i in range(4):
                 rows = slice(i * BS, (i + 1) * BS)
                 block = first // BS + i
                 spot[rows, :] = total[rows, :] * wide[block:block + 1, :]
-            copies.append(pltpu.make_async_copy(spot, out.at[pl.ds(first, 256)], sems.at[len(copies) % 2]))
+            copies.append(pltpu.make_async_copy(spot, out.at[pl.ds(first, 256)], sems.at[len(copies)]))
             copies[-1].start()
-    for copy in copies[-2:]:
+    for copy in copies:
         copy.wait()
 
 
@@ -321,9 +319,9 @@
         out_shape=jax.ShapeDtypeStruct((2 * W, W), jnp.float32),
         in_specs=[VMEM] * 4,
         out_specs=HBM,
-        scratch_shapes=[pltpu.VMEM((32, W), jnp.float32), pltpu.VMEM((2, 256, W), jnp.float32),
-                        pltpu.SemaphoreType.DMA((2,))],
-        compiler_params=pltpu.CompilerParams(vmem_limit_bytes=8 * MIB),
+        scratch_shapes=[pltpu.VMEM((32, W), jnp.float32), pltpu.VMEM((8, 256, W), jnp.float32),
+                        pltpu.SemaphoreType.DMA((8,))],
+        compiler_params=pltpu.CompilerParams(vmem_limit_bytes=16 * MIB),
         name="finish",
     )(filt.T, *in_vmem(part, left, q))
 

time: 240 us -> 238 us (level)
  transfers between devices with their start and end apart: 15 -> 15, of which waited for: 7 -> 7; matrix products, arithmetic and copies ran while one was open for 5% -> 6% of each run, Pallas kernels for 12% -> 12%
where the time goes in v9:
time: 238 us
  waiting for transfers between devices  142 us (60%)
  Pallas kernels  42.4 us (18%)
  starting transfers between devices  35.8 us (15%)
  local copies, waits for them, and re-layouts  15.6 us (7%)
    ppermute x6, waiting for transfers between devices, along_x(): lax.ppermute(value, 'col', [(i, i // 4 * 4 + (i % 4 + hop) % 4) for i in...  136 us
    pallas_call x1, Pallas kernels, on_device(): pl.pallas_call(multiply, out_shape=[pltpu.VMEM((2 * W, W), jnp.float32),...  21.3 us
    all_to_all x2, starting transfers between devices, along_y(): lax.all_to_all(value, 'row', 0, 0, axis_index_groups=Y_GROUPS, tiled=True)  12.7 us
    ppermute x6, starting transfers between devices, along_x(): lax.ppermute(value, 'col', [(i, i // 4 * 4 + (i % 4 + hop) % 4) for i in...  8.62 us
    pallas_call x1, Pallas kernels, on_device(): pl.pallas_call(prep_a, out_shape=[bf16(8, 512, W), bf16(5, 128, 2 * W)],...  7.62 us
    pallas_call x1, Pallas kernels, on_device(): pl.pallas_call(prep_b, out_shape=[bf16(4, 256, W)] * 4 + [bf16(EARLY, 256...  7.5 us
    ppermute x2, starting transfers between devices, swap_z_hi(): return lax.ppermute(value, 'row', [(i, i ^ 8) for i in range(16)])  6.72 us
    pallas_call x1, Pallas kernels, on_device(): pl.pallas_call(finish, out_shape=jax.ShapeDtypeStruct((2 * W, W), jnp.flo...  5.91 us
  transfers between devices with their start and end apart: 15, of which 7 were waited for; matrix products, arithmetic and copies ran while one was open for 6% of the time, Pallas kernels for 12%

profile of v9, /device:TPU:1, one launch (start us, length us, event | category | flops | bytes accessed | tf_op | source)
XLA Modules:
  0.0 237.7 jit_solution(16392745265145554931)
XLA Ops:
  0.0 0.1 pad_add_fusion.ids
  0.1 7.5 %prep_b.1 = (bf16[4,256,1024]{2,1,0:T(8,128)(2,1)}, bf16[4,256,1024]{2,1,0:T(8,128)(2,1)}, bf16[4,256,1024]{2,1,0:T(8,128)(2,1)}, bf16[4,256,1024]{2,1,0:T(8,128...) custom-call(s32[2]{0:T(128)S(1)} %pad_add_fusion.ids, s32[512]{0:T(512)} %kdist.1, ...), custom_call_target="tpu_custom_call" | custom-call | tf_op jit(solution)/shard_map/prep_b/pallas_call | solution.py:258
  7.6 2.6 %collective-permute-start = (bf16[1,256,1024]{2,1,0:T(8,128)(2,1)}, bf16[1,256,1024]{2,1,0:T(8,128)(2,1)S(1)}, u32[]{:S(2)}, u32[]{:S(2)}) collective-permute-start(bf16[1,256,1024]{2,1,0:T(8,128)(2,1)} %get-tuple-element.38), channel_id=1, source_target_pairs={{0,4},{1,5},{2,6},{3,7},{4,0},{5,1},{6,2},{7,3},{8,12},{9,13},{10,... | collective-permute-start | bytes 1572872 | tf_op jit(solution)/shard_map/ppermute | solution.py:247
  10.2 7.6 %prep_a.1 = (bf16[8,512,1024]{2,1,0:T(8,128)(2,1)}, bf16[5,128,2048]{2,1,0:T(8,128)(2,1)}) custom-call(s32[2]{0:T(128)S(1)} %pad_add_fusion.ids, s32[512]{0:T(512)S(1)} %copy-done.2, s32[32,32]{1,0:T(8,128)S(1)} %copy-done, bf16[2048,2048]{1,0:T(8,128)(2,1)} %at), custom_call_target="tpu_custom_call" | custom-call | tf_op jit(solution)/shard_map/prep_a/pallas_call | solution.py:271
  17.8 4.2 %collective-permute-done = bf16[1,256,1024]{2,1,0:T(8,128)(2,1)S(1)} collective-permute-done((bf16[1,256,1024]{2,1,0:T(8,128)(2,1)}, bf16[1,256,1024]{2,1,0:T(8,128)(2,1)S(1)}, u32[]{:S(2)}, u32[]{:S(2)}) %collective-permute-start) | collective-permute-done | bytes 524320 | tf_op jit(solution)/shard_map/ppermute | solution.py:247
  22.0 6.1 %all-to-all-start = ((bf16[8,512,1024]{2,1,0:T(8,128)(2,1)}), bf16[8,512,1024]{2,1,0:T(8,128)(2,1)}, u32[]{:S(2)}, u32[]{:S(2)}) async-start(bf16[8,512,1024]{2,1,0:T(8,128)(2,1)} %get-tuple-element.40), calls=%async_computation | async-start | bytes 16777216 | tf_op jit(solution)/shard_map/all_to_all | solution.py:256
  28.1 1.2 collective-permute-start.2
  29.3 1.5 collective-permute-start.3
  30.8 3.4 %collective-permute-start.1 = (bf16[5,128,2048]{2,1,0:T(8,128)(2,1)}, bf16[5,128,2048]{2,1,0:T(8,128)(2,1)S(1)}, u32[]{:S(2)}, u32[]{:S(2)}) collective-permute-start(bf16[5,128,2048]{2,1,0:T(8,128)(2,1)} %get-tuple-element.39), channel_id=1, source_target_pairs={{0,64},{8,72},{16,80},{24,88},{32,96},{40,104},{48,112},{56,120},{... | collective-permute-start | bytes 7864328 | tf_op jit(solution)/shard_map/ppermute | solution.py:244
  34.1 42.5 %collective-permute-done.2.r1 = bf16[4,256,1024]{2,1,0:T(8,128)(2,1)S(1)} collective-permute-done((bf16[4,256,1024]{2,1,0:T(8,128)(2,1)}, bf16[4,256,1024]{2,1,0:T(8,128)(2,1)S(1)}, u32[]{:S(2)}, u32[]{:S(2)}) %collective-permute-start.2) | collective-permute-done | bytes 2097184 | tf_op jit(solution)/shard_map/ppermute | solution.py:253
  76.7 0.0 collective-permute-done.3.r3
  76.7 2.1 collective-permute-start.4
  78.8 1.5 collective-permute-start.7
  80.2 1.1 slice.25
  81.4 43.3 %collective-permute-done.4.r2 = bf16[4,256,1024]{2,1,0:T(8,128)(2,1)S(1)} collective-permute-done((bf16[4,256,1024]{2,1,0:T(8,128)(2,1)}, bf16[4,256,1024]{2,1,0:T(8,128)(2,1)S(1)}, u32[]{:S(2)}, u32[]{:S(2)}) %collective-permute-start.4) | collective-permute-done | bytes 2097184 | tf_op jit(solution)/shard_map/ppermute | solution.py:253
  124.7 1.4 copy-done.6
  126.1 1.6 pad_maximum_fusion.1
  127.7 0.0 all-to-all-done.near_a
  127.7 3.1 %slice.32 = bf16[8,128,1024]{2,1,0:T(8,128)(2,1)} slice(bf16[8,512,1024]{2,1,0:T(8,128)(2,1)} %all-to-all-done.near_a), slice={[0:8], [384:512], [0:1024]} | slice | bytes 4194304 | tf_op jit(solution)/shard_map/slice | solution.py:291
  130.7 0.0 collective-permute-done.1
  130.8 3.4 %collective-permute-start.6 = (bf16[8,128,1024]{2,1,0:T(8,128)(2,1)}, bf16[8,128,1024]{2,1,0:T(8,128)(2,1)}, u32[]{:S(2)}, u32[]{:S(2)}) collective-permute-start(bf16[8,128,1024]{2,1,0:T(8,128)(2,1)} %slice.32), channel_id=1, source_target_pairs={{0,64},{8,72},{16,80},{24,88},{32,96},{40,104},{48,112},{56,120},{... | collective-permute-start | bytes 6291464 | tf_op jit(solution)/shard_map/ppermute | solution.py:244
  134.1 0.5 slice_bitcast_fusion.1
  134.6 0.4 pad_maximum_fusion
  135.0 2.3 copy.7
  137.3 6.6 %all-to-all-start.1 = ((bf16[8,128,2048]{2,1,0:T(8,128)(2,1)}), bf16[8,128,2048]{2,1,0:T(8,128)(2,1)}, u32[]{:S(2)}, u32[]{:S(2)}) async-start(bf16[8,128,2048]{2,1,0:T(8,128)(2,1)} %bitcast.10), calls=%async_computation.1 | async-start | bytes 8388608 | tf_op jit(solution)/shard_map/all_to_all | solution.py:256
  144.0 0.0 collective-permute-done.7
  144.0 1.8 constant_dynamic-update-slice_fusion.p0
  145.8 0.5 constant_dynamic-slice_fusion
  146.3 1.0 copy-done.3
  147.4 2.3 collective-permute-start.9
  149.7 22.4 %collective-permute-done.9.p3 = bf16[2,256,1024]{2,1,0:T(8,128)(2,1)S(1)} collective-permute-done((bf16[2,256,1024]{2,1,0:T(8,128)(2,1)S(1)}, bf16[2,256,1024]{2,1,0:T(8,128)(2,1)S(1)}, u32[]{:S(2)}, u32[]{:S(2)}) %collective-permute-start.9) | collective-permute-done | bytes 1048608 | tf_op jit(solution)/shard_map/ppermute | solution.py:253
  172.0 3.2 %collective-permute-done.8.p1 = bf16[2,256,1024]{2,1,0:T(8,128)(2,1)S(1)} collective-permute-done((bf16[2,256,1024]{2,1,0:T(8,128)(2,1)S(1)}, bf16[2,256,1024]{2,1,0:T(8,128)(2,1)S(1)}, u32[]{:S(2)}, u32[]{:S(2)}) %collective-permute-start.8) | collective-permute-done | bytes 1048608 | tf_op jit(solution)/shard_map/ppermute | solution.py:253
  175.2 1.0 copy-done.8
  176.2 1.8 slice.31
  178.0 0.0 copy-start.1
  178.0 1.3 collective-permute-start.5
  179.3 1.5 collective-permute-done.6.o_cross
  180.8 1.3 collective-permute-start.10
  182.2 1.1 collective-permute-start.12
  183.2 1.6 collective-permute-start.11
  184.8 24.4 %collective-permute-done.11.p2 = bf16[2,256,1024]{2,1,0:T(8,128)(2,1)S(1)} collective-permute-done((bf16[2,256,1024]{2,1,0:T(8,128)(2,1)S(1)}, bf16[2,256,1024]{2,1,0:T(8,128)(2,1)S(1)}, u32[]{:S(2)}, u32[]{:S(2)}) %collective-permute-start.11) | collective-permute-done | bytes 1048608 | tf_op jit(solution)/shard_map/ppermute | solution.py:253
  209.2 0.0 collective-permute-done.5.o_near
  209.2 0.0 all-to-all-done.1.e_far
  209.2 0.0 collective-permute-done.10.o_swap
  209.2 1.0 copy-done.9
  210.2 21.3 %multiply.1 = (f32[2048,1024]{1,0:T(8,128)S(1)}, bf16[2,8,128,1024]{3,2,1,0:T(8,128)(2,1)S(1)}) custom-call(s32[2]{0:T(128)S(1)} %pad_add_fusion.ids, bf16[8,512,1024]{2,1,0:T(8,128)(2,1)} %all-to-all-done.near_a, bf16[8,128,2048]{2,1,0:T(8,128)(2,1)} %all-to-all-done.1.e_far, bf16[8,128,1024]{2,1,0:T(8,128)(2,1)} %collective-permute-done.5.o_near, ...), custom_call_target="tpu_custom_call" | custom-call | tf_op jit(solution)/shard_map/multiply/pallas_call | solution.py:307
  231.5 0.0 collective-permute-done.12.right
  231.6 5.9 %finish.1 = f32[2048,1024]{1,0:T(8,128)} custom-call(s32[16,32]{1,0:T(8,128)S(1)} %bitcast.9, f32[2048,1024]{1,0:T(8,128)S(1)} %get-tuple-element.60.part, bf16[2,8,128,1024]{3,2,1,0:T(8,128)(2,1)S(1)} %get-tuple-element.61.left, bf16[4,256,1024]{2,1,0:T(8,128)(2,1)S(1)} %collective-permute-done.12.right), custom_call_target="tpu_custom_call" | custom-call | tf_op jit(solution)/shard_map/finish/pallas_call | solution.py:317
  (20 shorter events, 0.2 us)
Async XLA Ops:
  0.1 10.1 %copy-start = (s32[32,32]{1,0:T(8,128)S(1)}, s32[32,32]{1,0:T(8,128)}, u32[]{:S(2)}) copy-start(s32[32,32]{1,0:T(8,128)} %mask_a.1) | copy-start | bytes 12292
  0.1 10.1 %copy-start.2 = (s32[512]{0:T(512)S(1)}, s32[512]{0:T(512)}, u32[]{:S(2)}) copy-start(s32[512]{0:T(512)} %kdist.1) | copy-start | bytes 6148
  7.6 14.4 %collective-permute-start = (bf16[1,256,1024]{2,1,0:T(8,128)(2,1)}, bf16[1,256,1024]{2,1,0:T(8,128)(2,1)S(1)}, u32[]{:S(2)}, u32[]{:S(2)}) collective-permute-start(bf16[1,256,1024]{2,1,0:T(8,128)(2,1)} %get-tuple-element.38), channel_id=1, source_target_pairs={{0,4},{1,5},{2,6},{3,7},{4,0},{5,1},{6,2},{7,3},{8,12},{9,13},{10,... | collective-permute-start | bytes 1572872 | tf_op jit(solution)/shard_map/ppermute | solution.py:247
  22.0 105.7 %all-to-all-start = ((bf16[8,512,1024]{2,1,0:T(8,128)(2,1)}), bf16[8,512,1024]{2,1,0:T(8,128)(2,1)}, u32[]{:S(2)}, u32[]{:S(2)}) async-start(bf16[8,512,1024]{2,1,0:T(8,128)(2,1)} %get-tuple-element.40), calls=%async_computation | async-start | bytes 16777216 | tf_op jit(solution)/shard_map/all_to_all | solution.py:256
  28.1 48.6 %collective-permute-start.2 = (bf16[4,256,1024]{2,1,0:T(8,128)(2,1)}, bf16[4,256,1024]{2,1,0:T(8,128)(2,1)S(1)}, u32[]{:S(2)}, u32[]{:S(2)}) collective-permute-start(bf16[4,256,1024]{2,1,0:T(8,128)(2,1)} %get-tuple-element.43), channel_id=1, source_target_pairs={{0,1},{1,2},{2,3},{3,0},{4,5},{5,6},{6,7},{7,4},{8,9},{9,10},{10,1... | collective-permute-start | bytes 6291464 | tf_op jit(solution)/shard_map/ppermute | solution.py:253
  29.3 47.3 %collective-permute-start.3 = (bf16[4,256,1024]{2,1,0:T(8,128)(2,1)}, bf16[4,256,1024]{2,1,0:T(8,128)(2,1)S(1)}, u32[]{:S(2)}, u32[]{:S(2)}) collective-permute-start(bf16[4,256,1024]{2,1,0:T(8,128)(2,1)} %get-tuple-element.44), channel_id=1, source_target_pairs={{0,3},{1,0},{2,1},{3,2},{4,7},{5,4},{6,5},{7,6},{8,11},{9,8},{10,9... | collective-permute-start | bytes 6291464 | tf_op jit(solution)/shard_map/ppermute | solution.py:253
  30.8 100.0 %collective-permute-start.1 = (bf16[5,128,2048]{2,1,0:T(8,128)(2,1)}, bf16[5,128,2048]{2,1,0:T(8,128)(2,1)S(1)}, u32[]{:S(2)}, u32[]{:S(2)}) collective-permute-start(bf16[5,128,2048]{2,1,0:T(8,128)(2,1)} %get-tuple-element.39), channel_id=1, source_target_pairs={{0,64},{8,72},{16,80},{24,88},{32,96},{40,104},{48,112},{56,120},{... | collective-permute-start | bytes 7864328 | tf_op jit(solution)/shard_map/ppermute | solution.py:244
  76.7 4.7 %copy-start.4 = (bf16[4,256,1024]{2,1,0:T(8,128)(2,1)}, bf16[4,256,1024]{2,1,0:T(8,128)(2,1)S(1)}, u32[]{:S(2)}) copy-start(bf16[4,256,1024]{2,1,0:T(8,128)(2,1)S(1)} %collective-permute-done.2.r1) | copy-start | bytes 6291460
  76.7 4.7 %copy-start.5 = (bf16[4,256,1024]{2,1,0:T(8,128)(2,1)}, bf16[4,256,1024]{2,1,0:T(8,128)(2,1)S(1)}, u32[]{:S(2)}) copy-start(bf16[4,256,1024]{2,1,0:T(8,128)(2,1)S(1)} %collective-permute-done.3.r3) | copy-start | bytes 6291460
  76.7 48.0 %collective-permute-start.4 = (bf16[4,256,1024]{2,1,0:T(8,128)(2,1)}, bf16[4,256,1024]{2,1,0:T(8,128)(2,1)S(1)}, u32[]{:S(2)}, u32[]{:S(2)}) collective-permute-start(bf16[4,256,1024]{2,1,0:T(8,128)(2,1)} %get-tuple-element.46), channel_id=1, source_target_pairs={{0,2},{1,3},{2,0},{3,1},{4,6},{5,7},{6,4},{7,5},{8,10},{9,11},{10,... | collective-permute-start | bytes 6291464 | tf_op jit(solution)/shard_map/ppermute | solution.py:253
  78.8 65.2 %collective-permute-start.7 = (bf16[4,256,1024]{2,1,0:T(8,128)(2,1)}, bf16[4,256,1024]{2,1,0:T(8,128)(2,1)}, u32[]{:S(2)}, u32[]{:S(2)}) collective-permute-start(bf16[4,256,1024]{2,1,0:T(8,128)(2,1)} %get-tuple-element.53), channel_id=1, source_target_pairs={{0,4},{1,5},{2,6},{3,7},{4,0},{5,1},{6,2},{7,3},{8,12},{9,13},{10,... | collective-permute-start | bytes 6291464 | tf_op jit(solution)/shard_map/ppermute | solution.py:247
  124.7 1.4 copy-start.6
  130.8 50.1 %collective-permute-start.6 = (bf16[8,128,1024]{2,1,0:T(8,128)(2,1)}, bf16[8,128,1024]{2,1,0:T(8,128)(2,1)}, u32[]{:S(2)}, u32[]{:S(2)}) collective-permute-start(bf16[8,128,1024]{2,1,0:T(8,128)(2,1)} %slice.32), channel_id=1, source_target_pairs={{0,64},{8,72},{16,80},{24,88},{32,96},{40,104},{48,112},{56,120},{... | collective-permute-start | bytes 6291464 | tf_op jit(solution)/shard_map/ppermute | solution.py:244
  137.3 71.9 %all-to-all-start.1 = ((bf16[8,128,2048]{2,1,0:T(8,128)(2,1)}), bf16[8,128,2048]{2,1,0:T(8,128)(2,1)}, u32[]{:S(2)}, u32[]{:S(2)}) async-start(bf16[8,128,2048]{2,1,0:T(8,128)(2,1)} %bitcast.10), calls=%async_computation.1 | async-start | bytes 8388608 | tf_op jit(solution)/shard_map/all_to_all | solution.py:256
  145.8 1.6 copy-start.3
  147.4 24.7 %collective-permute-start.9 = (bf16[2,256,1024]{2,1,0:T(8,128)(2,1)S(1)}, bf16[2,256,1024]{2,1,0:T(8,128)(2,1)S(1)}, u32[]{:S(2)}, u32[]{:S(2)}) collective-permute-start(bf16[2,256,1024]{2,1,0:T(8,128)(2,1)S(1)} %get-tuple-element.63), channel_id=1, source_target_pairs={{0,3},{1,0},{2,1},{3,2},{4,7},{5,4},{6,5},{7,6},{8,11},{9,8},{10,9... | collective-permute-start | bytes 3145736 | tf_op jit(solution)/shard_map/ppermute | solution.py:253
  149.7 25.6 %collective-permute-start.8 = (bf16[2,256,1024]{2,1,0:T(8,128)(2,1)S(1)}, bf16[2,256,1024]{2,1,0:T(8,128)(2,1)S(1)}, u32[]{:S(2)}, u32[]{:S(2)}) collective-permute-start(bf16[2,256,1024]{2,1,0:T(8,128)(2,1)S(1)} %get-tuple-element.64), channel_id=1, source_target_pairs={{0,1},{1,2},{2,3},{3,0},{4,5},{5,6},{6,7},{7,4},{8,9},{9,10},{10,1... | collective-permute-start | bytes 3145736 | tf_op jit(solution)/shard_map/ppermute | solution.py:253
  172.0 5.9 %copy-start.7 = (bf16[2,256,1024]{2,1,0:T(8,128)(2,1)}, bf16[2,256,1024]{2,1,0:T(8,128)(2,1)S(1)}, u32[]{:S(2)}) copy-start(bf16[2,256,1024]{2,1,0:T(8,128)(2,1)S(1)} %collective-permute-done.9.p3) | copy-start | bytes 3145732
  175.2 1.0 copy-start.8
  178.0 53.6 %copy-start.1 = (s32[32,16]{0,1:T(8,128)S(1)}, s32[32,16]{0,1:T(8,128)}, u32[]{:S(2)}) copy-start(s32[32,16]{0,1:T(8,128)} %param.10) | copy-start | bytes 6148
  178.0 31.2 %collective-permute-start.5 = (bf16[8,128,1024]{2,1,0:T(8,128)(2,1)S(1)}, bf16[8,128,1024]{2,1,0:T(8,128)(2,1)}, u32[]{:S(2)}, u32[]{:S(2)}) collective-permute-start(bf16[8,128,1024]{2,1,0:T(8,128)(2,1)S(1)} %slice.31), channel_id=1, source_target_pairs={{0,8},{8,0},{16,24},{24,16},{32,40},{40,32},{48,56},{56,48},{64,72... | collective-permute-start | bytes 6291464 | tf_op jit(solution)/shard_map/ppermute | solution.py:250
  180.8 28.4 %collective-permute-start.10 = (bf16[8,128,1024]{2,1,0:T(8,128)(2,1)}, bf16[8,128,1024]{2,1,0:T(8,128)(2,1)}, u32[]{:S(2)}, u32[]{:S(2)}) collective-permute-start(bf16[8,128,1024]{2,1,0:T(8,128)(2,1)} %collective-permute-done.6.o_cross), channel_id=1, source_target_pairs={{0,8},{8,0},{16,24},{24,16},{32,40},{40,32},{48,56},{56,48},{64,72... | collective-permute-start | bytes 6291464 | tf_op jit(solution)/shard_map/ppermute | solution.py:250
  182.2 49.4 %collective-permute-start.12 = (bf16[4,256,1024]{2,1,0:T(8,128)(2,1)}, bf16[4,256,1024]{2,1,0:T(8,128)(2,1)S(1)}, u32[]{:S(2)}, u32[]{:S(2)}) collective-permute-start(bf16[4,256,1024]{2,1,0:T(8,128)(2,1)} %pad_maximum_fusion.1), channel_id=1, source_target_pairs={{0,4},{1,5},{2,6},{3,7},{4,0},{5,1},{6,2},{7,3},{8,12},{9,13},{10,... | collective-permute-start | bytes 6291464 | tf_op jit(solution)/shard_map/ppermute | solution.py:247
  183.2 26.0 %collective-permute-start.11 = (bf16[2,256,1024]{2,1,0:T(8,128)(2,1)S(1)}, bf16[2,256,1024]{2,1,0:T(8,128)(2,1)S(1)}, u32[]{:S(2)}, u32[]{:S(2)}) collective-permute-start(bf16[2,256,1024]{2,1,0:T(8,128)(2,1)S(1)} %get-tuple-element.58), channel_id=1, source_target_pairs={{0,2},{1,3},{2,0},{3,1},{4,6},{5,7},{6,4},{7,5},{8,10},{9,11},{10,... | collective-permute-start | bytes 3145736 | tf_op jit(solution)/shard_map/ppermute | solution.py:253
  209.2 1.0 copy-start.9
